TPU v7x, 32 devices: a whole 2x2x4 slice. The times are simulated.
32 devices in a mesh: dp: 4 (over z), wide: 8 (over y, x, core).
Axes of the slice: x: 2, y: 2, z: 4, core: 2. Of those that a mesh axis runs over, the one named last changes fastest.
Arguments:
- tokens: bfloat16 [32768, 768], P(('dp', 'wide')), may hold values from -6 to 6
- segment_ids: int32 [64, 512], P(('dp', 'wide')), may hold values from 0 to 7, never falling along the last dimension, each value on 1 to 256 neighbouring positions
- cotangent: bfloat16 [32768, 768], P(('dp', 'wide')), may hold values from -6 to 6
- query_frozen_weight: bfloat16 [768, 768], replicated, may hold values from -0.21875 to 0.21875
- query_bias_vector: bfloat16 [768], replicated, may hold values from -3 to 3
- w_key: bfloat16 [768, 768], replicated, may hold values from -0.21875 to 0.21875
- value_frozen_weight: bfloat16 [768, 768], replicated, may hold values from -0.21875 to 0.21875
- value_bias_vector: bfloat16 [768], replicated, may hold values from -3 to 3
- w_out: bfloat16 [768, 768], replicated, may hold values from -0.625 to 0.625
- b_out: bfloat16 [768], replicated, may hold values from -2 to 2
- norm1_gain: bfloat16 [768], replicated, may hold values from 0.5 to 1.5
- norm1_bias: bfloat16 [768], replicated, may hold values from -2 to 2
- w_up: bfloat16 [768, 3072], replicated, may hold values from -0.21875 to 0.21875
- b_up: bfloat16 [3072], replicated, may hold values from -3 to 3
- w_down: bfloat16 [3072, 768], replicated, may hold values from -0.109375 to 0.109375
- b_down: bfloat16 [768], replicated, may hold values from -2 to 2
- norm2_gain: bfloat16 [768], replicated, may hold values from 0.5 to 1.5
- norm2_bias: bfloat16 [768], replicated, may hold values from -2 to 2
- factors: float32 [24576], replicated, may hold values from -0.4 to 0.4
- moment_first: float32 [24576], P('wide'), may hold values from -0.006 to 0.006
- moment_second: float32 [24576], P('wide'), may hold values from 1e-08 to 1e-07
- step_count: int32 [1], replicated, may hold values from 1 to 10
- learn_rate: float32 [1], replicated, may hold values from 0.003 to 0.03
Outputs:
- output: bfloat16 [32768, 768], P(('dp', 'wide'))
- grad_tokens: bfloat16 [32768, 768], P(('dp', 'wide'))
- grad_factors: float32 [24576], P('wide')
- new_factors: float32 [24576], replicated
- new_first: float32 [24576], P('wide')
- new_second: float32 [24576], P('wide')
Inputs may be any that keep to these rules, and one draw needn't show every extreme that they name: `segment_ids`: segment ids never fall along a pack; each segment holds 1 to 256 rows, one exactly 256.
All inputs are finite; a program needn't handle non-finite values.
Results may differ from a plain program's by a relative error of at most 0.014.
Values sent between devices are 32-bit elements; how exact they have to be, the bound alone decides.
No kernel may reach another device: no remote copies, remote signals or barrier semaphores. Data moves between devices by JAX's collectives and lax.ppermute only.
A program may use at most 192 MiB of HBM per device.

v0:
```python
import jax
import jax.numpy as jnp
from jax import lax
from jax.sharding import PartitionSpec as P

HEADS = 12
RANK = 8


norm_eps = 1e-05
adapter_scale = 2.0
beta_one = 0.9
beta_two = 0.999
adam_eps = 1e-08
decay_rate = 0.01
rate_ratio = 16.0


def matrix_product(left, right):
    return jnp.dot(left, right, preferred_element_type=jnp.float32)


def layer_norm(layer_input, gain_vec, shift_vec):
    row_mean = jnp.mean(layer_input, axis=-1, keepdims=True)
    centered = layer_input - row_mean
    spread = jnp.mean(centered * centered, axis=-1, keepdims=True)
    return centered * lax.rsqrt(spread + norm_eps) * gain_vec + shift_vec


def gelu_exact(layer_input):
    return jax.nn.gelu(layer_input, approximate=False)


def split_heads(block):
    return block.reshape(block.shape[0], HEADS, block.shape[1] // HEADS)


def masked_scores(query_heads, key_heads, seg_block):
    head_dim = query_heads.shape[2]
    scores = jnp.einsum("qhd,khd->hqk", query_heads, key_heads, preferred_element_type=jnp.float32)
    scores = scores * head_dim ** (-0.5)
    same_segment = seg_block[:, None] == seg_block[None, :]
    return jnp.where(same_segment[None], scores, -1000000000.0)


def attend_pack(items):
    query_block, key_block, value_block, seg_block = items
    query_heads = split_heads(query_block)
    key_heads = split_heads(key_block)
    value_heads = split_heads(value_block)
    scores = masked_scores(query_heads, key_heads, seg_block)
    row_top = jnp.max(scores, axis=-1, keepdims=True)
    expanded = jnp.exp(scores - row_top)
    row_total = jnp.sum(expanded, axis=-1, keepdims=True)
    soft_weights = (expanded / row_total).astype(jnp.bfloat16)
    attended = jnp.einsum(
        "hqk,khd->qhd", soft_weights, value_heads, preferred_element_type=jnp.float32
    )
    attended = attended.reshape(query_block.shape[0], -1).astype(jnp.bfloat16)
    return (attended, row_top + jnp.log(row_total))


def attend_back(items):
    query_block, key_block, value_block, seg_block, log_total, d_block = items
    query_heads = split_heads(query_block)
    key_heads = split_heads(key_block)
    value_heads = split_heads(value_block)
    d_heads = split_heads(d_block)
    head_dim = query_heads.shape[2]
    scores = masked_scores(query_heads, key_heads, seg_block)
    soft_weights = jnp.exp(scores - log_total)
    d_soft = jnp.einsum("qhd,khd->hqk", d_heads, value_heads, preferred_element_type=jnp.float32)
    value_rows_gradient = jnp.einsum(
        "hqk,qhd->khd",
        soft_weights.astype(jnp.bfloat16),
        d_heads,
        preferred_element_type=jnp.float32,
    )
    row_delta = jnp.sum(d_soft * soft_weights, axis=-1, keepdims=True)
    d_scores = (soft_weights * (d_soft - row_delta)).astype(jnp.bfloat16)
    query_rows_gradient = jnp.einsum(
        "hqk,khd->qhd", d_scores, key_heads, preferred_element_type=jnp.float32
    )
    d_keys = jnp.einsum("hqk,qhd->khd", d_scores, query_heads, preferred_element_type=jnp.float32)
    row_count = query_block.shape[0]
    query_rows_gradient = (
        (query_rows_gradient * head_dim ** (-0.5)).reshape(row_count, -1).astype(jnp.bfloat16)
    )
    d_keys = (d_keys * head_dim ** (-0.5)).reshape(row_count, -1).astype(jnp.bfloat16)
    value_rows_gradient = value_rows_gradient.reshape(row_count, -1).astype(jnp.bfloat16)
    return (query_rows_gradient, d_keys, value_rows_gradient)


def adam_update(params, gradient, first, second, norm_sq, steps_done, rate_now):
    clip = jnp.minimum(1.0, lax.rsqrt(norm_sq + 1e-06))
    clipped = gradient * clip
    first_new = beta_one * first + (1.0 - beta_one) * clipped
    second_new = beta_two * second + (1.0 - beta_two) * clipped * clipped
    fix_one = 1.0 - jnp.power(beta_one, steps_done)
    fix_two = 1.0 - jnp.power(beta_two, steps_done)
    update = first_new / fix_one / (jnp.sqrt(second_new / fix_two) + adam_eps) + decay_rate * params
    return (params - rate_now * update, first_new, second_new)


def shards(
    tokens,
    segment_ids,
    cotangent,
    query_frozen_weight,
    query_bias_vector,
    w_key,
    value_frozen_weight,
    value_bias_vector,
    w_out,
    b_out,
    norm1_gain,
    norm1_bias,
    w_up,
    b_up,
    w_down,
    b_down,
    norm2_gain,
    norm2_bias,
    factors,
    moment_first,
    moment_second,
    step_count,
    learn_rate,
):
    model_width = tokens.shape[1]
    pack_count = segment_ids.shape[0]
    seq_len = segment_ids.shape[1]
    block_len = model_width * RANK
    factor_low = factors.astype(jnp.bfloat16)
    query_down_weight = factor_low[:block_len].reshape(model_width, RANK)
    value_down_weight = factor_low[block_len : 2 * block_len].reshape(model_width, RANK)
    query_up_weight = factor_low[2 * block_len : 3 * block_len].reshape(RANK, model_width)
    value_up_weight = factor_low[3 * block_len :].reshape(RANK, model_width)
    query_adapter_output = matrix_product(tokens, query_down_weight).astype(jnp.bfloat16)
    value_adapter_output = matrix_product(tokens, value_down_weight).astype(jnp.bfloat16)
    query_rows = (
        matrix_product(tokens, query_frozen_weight)
        + query_bias_vector
        + adapter_scale * matrix_product(query_adapter_output, query_up_weight)
    ).astype(jnp.bfloat16)
    keys_all = matrix_product(tokens, w_key).astype(jnp.bfloat16)
    value_rows_full = (
        matrix_product(tokens, value_frozen_weight)
        + value_bias_vector
        + adapter_scale * matrix_product(value_adapter_output, value_up_weight)
    ).astype(jnp.bfloat16)
    pack_shape = (pack_count, seq_len, model_width)
    packed = (
        query_rows.reshape(pack_shape),
        keys_all.reshape(pack_shape),
        value_rows_full.reshape(pack_shape),
        segment_ids,
    )
    attended, log_total = lax.map(attend_pack, packed)
    attended = attended.reshape(-1, model_width)
    gain_one = norm1_gain.astype(jnp.float32)
    shift_one = norm1_bias.astype(jnp.float32)
    gain_two = norm2_gain.astype(jnp.float32)
    shift_two = norm2_bias.astype(jnp.float32)
    first_sum = tokens.astype(jnp.float32) + matrix_product(attended, w_out) + b_out
    hidden, pull_one = jax.vjp(lambda summed: layer_norm(summed, gain_one, shift_one), first_sum)
    pre_act = matrix_product(hidden.astype(jnp.bfloat16), w_up) + b_up
    activated, pull_gelu = jax.vjp(gelu_exact, pre_act)
    mixed = matrix_product(activated.astype(jnp.bfloat16), w_down) + b_down
    result_full, pull_two = jax.vjp(
        lambda summed: layer_norm(summed, gain_two, shift_two), hidden + mixed
    )
    output = result_full.astype(jnp.bfloat16)
    d_second = pull_two(cotangent.astype(jnp.float32))[0]
    d_mixed = d_second.astype(jnp.bfloat16)
    d_pre = pull_gelu(matrix_product(d_mixed, w_down.T))[0].astype(jnp.bfloat16)
    d_hidden = d_second + matrix_product(d_pre, w_up.T)
    d_first = pull_one(d_hidden)[0]
    d_attended = matrix_product(d_first.astype(jnp.bfloat16), w_out.T).astype(jnp.bfloat16)
    query_rows_gradient, d_keys, value_rows_gradient = lax.map(
        attend_back, packed + (log_total, d_attended.reshape(pack_shape))
    )
    query_rows_gradient = query_rows_gradient.reshape(-1, model_width)
    d_keys = d_keys.reshape(-1, model_width)
    value_rows_gradient = value_rows_gradient.reshape(-1, model_width)
    query_adapter_gradient = (
        adapter_scale * matrix_product(query_rows_gradient, query_up_weight.T)
    ).astype(jnp.bfloat16)
    value_adapter_gradient = (
        adapter_scale * matrix_product(value_rows_gradient, value_up_weight.T)
    ).astype(jnp.bfloat16)
    grad_full = (
        d_first
        + matrix_product(query_rows_gradient, query_frozen_weight.T)
        + matrix_product(d_keys, w_key.T)
        + matrix_product(value_rows_gradient, value_frozen_weight.T)
        + matrix_product(query_adapter_gradient, query_down_weight.T)
        + matrix_product(value_adapter_gradient, value_down_weight.T)
    )
    grad_tokens = grad_full.astype(jnp.bfloat16)
    query_down_gradient = matrix_product(tokens.T, query_adapter_gradient)
    value_down_gradient = matrix_product(tokens.T, value_adapter_gradient)
    query_up_gradient = adapter_scale * matrix_product(query_adapter_output.T, query_rows_gradient)
    value_up_gradient = adapter_scale * matrix_product(value_adapter_output.T, value_rows_gradient)
    local_grad = jnp.concatenate(
        [
            query_down_gradient.reshape(-1),
            value_down_gradient.reshape(-1),
            query_up_gradient.reshape(-1),
            value_up_gradient.reshape(-1),
        ]
    )
    wide_count = lax.axis_size("wide")
    wide_index = lax.axis_index("wide")
    own_len = factors.shape[0] // wide_count
    steps_done = step_count[0].astype(jnp.float32)
    rate_now = jnp.where(wide_index < wide_count // 2, learn_rate[0], rate_ratio * learn_rate[0])
    share_part = lax.psum_scatter(local_grad, "wide", scatter_dimension=0, tiled=True)
    owned_grad = lax.psum(share_part, "dp")
    norm_sq = lax.psum(jnp.sum(owned_grad * owned_grad), "wide")
    own_params = lax.dynamic_slice_in_dim(factors, wide_index * own_len, own_len)
    params_new, new_first, new_second = adam_update(
        own_params, owned_grad, moment_first, moment_second, norm_sq, steps_done, rate_now
    )
    new_factors = lax.all_gather(params_new, "wide", axis=0, tiled=True)
    return (output, grad_tokens, owned_grad, new_factors, new_first, new_second)


def solution(mesh):
    in_specs = (
        P(("dp", "wide"), None),
        P(("dp", "wide"), None),
        P(("dp", "wide"), None),
        P(),
        P(),
        P(),
        P(),
        P(),
        P(),
        P(),
        P(),
        P(),
        P(),
        P(),
        P(),
        P(),
        P(),
        P(),
        P(),
        P("wide"),
        P("wide"),
        P(),
        P(),
    )
    out_specs = (
        P(("dp", "wide"), None),
        P(("dp", "wide"), None),
        P("wide"),
        P(),
        P("wide"),
        P("wide"),
    )
    return jax.shard_map(shards, mesh=mesh, in_specs=in_specs, out_specs=out_specs, check_vma=False)
```

profile of v0, /device:TPU:0, one launch (start us, length us, event | category | flops | bytes accessed | tf_op | source)
XLA Modules:
  0.0 371.8 jit_solution(16153916224654669189)
XLA Ops:
  9.2 2.7 copy.79
  12.5 2.7 fusion.51
  21.0 3.1 fusion.52
  26.0 2.6 copy.81
  28.6 4.3 %convolution_convert_fusion.1 = bf16[1024,768]{1,0:T(8,128)(2,1)} fusion(bf16[1024,768]{1,0:T(8,128)(2,1)} %param.27, bf16[768,768]{1,0:T(8,128)(2,1)} %param.32), kind=kOutput, calls=%fused_computation.77 | convolution fusion | flops 1208745984 | bytes 4325376 | tf_op jit(solution)/shard_map/dot_general | solution.py:20
  32.9 2.6 copy.82
  36.8 27.9 %while.26 = (s32[]{:T(128)}, bf16[2,512,768]{2,1,0:T(8,128)(2,1)}, f32[2,12,512,1]{2,1,3,0:T(8,128)}, bf16[2,512,768]{1,2,0:T(8,128)(2,1)S(1)}, s32[2,512]{1,0:T...) while((s32[]{:T(128)}, bf16[2,512,768]{2,1,0:T(8,128)(2,1)}, ...), condition=%wide.region_3.4_spmd, body=%wide.region_0.3_spmd.sunk | while | flops 843704320 | bytes 50019424 | solution.py:159
  44.1 4.4 %fusion.135 = bf16[12,64,512]{2,1,0:T(8,128)(2,1)} fusion(bf16[512,12,64]{0,2,1:T(8,128)(2,1)S(1)} %bitcast.166, f32[12,512,512]{1,2,0:T(8,128)S(1)} %get-tuple-element.341, f32[12,512]{1,0:T(8,128)S(1)} %fusion.134, f32[12,512]{1,0:T(8,128)S(1)} %get-tuple-element.342, pred[512,512]{0,1:T(8,128)(4,1)S(1)} %broadcast_compare_fusion.4), kind=kOutput, calls=%fused_computation.6.clone.1 | convolution fusion | flops 418775040 | bytes 14467072 | tf_op jit(solution)/shard_map/while/body/eval_jaxpr/hqk,khd->qhd/dot_general | solution.py:56
  57.9 4.4 %fusion.135 = bf16[12,64,512]{2,1,0:T(8,128)(2,1)} fusion(bf16[512,12,64]{0,2,1:T(8,128)(2,1)S(1)} %bitcast.166, f32[12,512,512]{1,2,0:T(8,128)S(1)} %get-tuple-element.341, f32[12,512]{1,0:T(8,128)S(1)} %fusion.134, f32[12,512]{1,0:T(8,128)S(1)} %get-tuple-element.342, pred[512,512]{0,1:T(8,128)(4,1)S(1)} %broadcast_compare_fusion.4), kind=kOutput, calls=%fused_computation.6.clone.1 | convolution fusion | flops 418775040 | bytes 14467072 | tf_op jit(solution)/shard_map/while/body/eval_jaxpr/hqk,khd->qhd/dot_general | solution.py:56
  64.7 4.1 %fusion.48 = (f32[1024]{0:T(1024)S(1)}, f32[1024,768]{0,1:T(8,128)S(1)}) fusion(f32[768]{0:T(1024)S(1)} %convert_element_type.167, bf16[1024,768]{1,0:T(8,128)(2,1)} %bitcast.178, bf16[768,768]{1,0:T(8,128)(2,1)S(1)} %copy-done, bf16[1024,768]{0,1:T(8,128)(2,1)} %copy.79), kind=kOutput, calls=%fused_computation.119 | convolution fusion | flops 1211104256 | bytes 7478272 | tf_op jit(solution)/shard_map/dot_general | solution.py:20
  69.7 36.4 %fusion.15 = (f32[1024,3072]{1,0:T(8,128)}, f32[1024,3072]{1,0:T(8,128)}) fusion(f32[3072]{0:T(1024)S(1)} %convert_element_type.171, bf16[768,3072]{1,0:T(8,128)(2,1)S(1)} %bitcast.183, f32[1024,768]{0,1:T(8,128)S(1)} %get-tuple-element.230, f32[768]{0:T(1024)S(1)} %convert_element_type.169, f32[768]{0:T(1024)S(1)} %convert_element_type.168, ...), kind=kOutput, calls=%fused_computation.38 | convolution fusion | flops 5033951232 | bytes 33056768 | tf_op jit(solution)/shard_map/dot_general | solution.py:20
  106.1 17.7 %fusion.49 = (f32[1024]{0:T(1024)S(1)}, f32[1024,768]{0,1:T(8,128)}) fusion(f32[768]{0:T(1024)S(1)} %convert_element_type.173, bf16[3072,768]{1,0:T(8,128)(2,1)} %param.41, f32[1024,3072]{1,0:T(8,128)} %get-tuple-element.231, f32[1024,3072]{1,0:T(8,128)} %get-tuple-element.232, f32[3072]{0:T(1024)S(1)} %convert_element_type.171, ...), kind=kOutput, calls=%fused_computation.120 | convolution fusion | flops 4849925120 | bytes 36209664 | tf_op jit(solution)/shard_map/dot_general | solution.py:20
  125.6 2.8 multiply_reduce_fusion.2
  130.8 22.3 %multiply_reduce_fusion.1 = (f32[1024]{0:T(1024)S(1)}, f32[1024,768]{0,1:T(8,128)}) fusion(f32[1024,768]{0,1:T(8,128)} %copy-done.12, f32[1024]{0:T(1024)S(1)} %broadcast_multiply_fusion.1, f32[768]{0:T(1024)S(1)} %convert_element_type.168, bf16[768,3072]{1,0:T(8,128)(2,1)} %param.39, f32[1024,3072]{1,0:T(8,128)} %get-tuple-element.231, ...), kind=kOutput, calls=%fused_computation.61 | convolution fusion | flops 9728162816 | bytes 45656064 | tf_op jit(solution)/shard_map/dot_general | solution.py:20
  153.2 4.0 %fusion.46 = (f32[1024]{0:T(1024)S(1)}, f32[1024,768]{0,1:T(8,128)S(1)}) fusion(f32[1024]{0:T(1024)S(1)} %multiply_multiply_fusion.6, f32[1024,768]{0,1:T(8,128)} %copy-done.12, f32[1024]{0:T(1024)S(1)} %broadcast_multiply_fusion.1, f32[1024,768]{0,1:T(8,128)} %get-tuple-element.236, f32[1024]{0:T(1024)S(1)} %fusion.39), kind=kLoop, calls=%fused_computation.117 | loop fusion | flops 4717568 | bytes 9453568 | tf_op jit(solution)/shard_map/transpose(jvp())/reduce_sum | solution.py:25
  157.2 2.7 convolution_convert_fusion
  163.6 94.7 %while.27 = (s32[]{:T(128)}, bf16[2,512,768]{2,1,0:T(8,128)(2,1)}, bf16[2,512,768]{2,1,0:T(8,128)(2,1)}, bf16[2,512,768]{2,1,0:T(8,128)(2,1)}, bf16[2,512,768]{1...) while((s32[]{:T(128)}, bf16[2,512,768]{2,1,0:T(8,128)(2,1)}, ...), condition=%wide.region_14.15_spmd, body=%wide.region_12.14_spmd.sunk | while | flops 2062673920 | bytes 202554192 | solution.py:180
  166.1 6.3 %fusion.146 = f32[12,512,512]{1,2,0:T(8,128)} fusion(bf16[512,12,64]{0,2,1:T(8,128)(2,1)S(1)} %bitcast.156, bf16[512,12,64]{0,2,1:T(8,128)(2,1)S(1)} %bitcast.154), kind=kOutput, calls=%fused_computation.121.clone.1 | convolution fusion | flops 402653184 | bytes 14155776 | tf_op jit(solution)/shard_map/while/body/eval_jaxpr/qhd,khd->hqk/dot_general | solution.py:40
  175.0 11.0 %multiply_reduce_fusion.7 = (f32[12,512]{1,0:T(8,128)S(1)}, f32[12,512,512]{1,2,0:T(8,128)}) fusion(f32[12,512,512]{1,2,0:T(8,128)} %fusion.146, f32[12,512]{1,0:T(8,128)S(1)} %dynamic-slice_bitcast_fusion.2, pred[512,512]{0,1:T(8,128)(4,1)S(1)} %broadcast_compare_fusion.5, bf16[512,12,64]{0,2,1:T(8,128)(2,1)S(1)} %bitcast.159, ...), kind=kOutput, calls=%fused_computation.17.clone.1 | convolution fusion | flops 418375680 | bytes 27049984 | tf_op jit(solution)/shard_map/while/body/eval_jaxpr/qhd,khd->hqk/dot_general | solution.py:72
  187.6 7.0 %multiply_convert_fusion.10 = bf16[12,512,512]{1,2,0:T(8,128)(2,1)S(1)} fusion(f32[12,512,512]{1,2,0:T(8,128)} %get-tuple-element.353, f32[12,512,512]{1,2,0:T(8,128)S(1)} %bitcast.153, f32[12,512]{1,0:T(8,128)S(1)} %get-tuple-element.354, f32[12,512]{1,0:T(8,128)S(1)} %dynamic-slice_bitcast_fusion.2, pred[512,512]{0,1:T(8,128)(4,1)S(1)} %broadcast_compare_fusion.5), kind=kLoop, calls=%fused_computation.16.clone.1 | loop fusion | flops 18874368 | bytes 31768576 | tf_op jit(solution)/shard_map/while/body/eval_jaxpr/convert_element_type | solution.py:80
  197.4 6.3 %fusion.147 = bf16[12,64,512]{2,1,0:T(8,128)(2,1)S(1)} fusion(bf16[512,12,64]{0,2,1:T(8,128)(2,1)S(1)} %bitcast.160, f32[12,512,512]{1,2,0:T(8,128)} %fusion.146, f32[12,512]{1,0:T(8,128)S(1)} %dynamic-slice_bitcast_fusion.2, pred[512,512]{0,1:T(8,128)(4,1)S(1)} %broadcast_compare_fusion.5), kind=kOutput, calls=%fused_computation.24.clone.1 | convolution fusion | flops 415629312 | bytes 14442496 | tf_op jit(solution)/shard_map/while/body/eval_jaxpr/hqk,qhd->khd/dot_general | solution.py:73
  205.3 4.0 %multiply_convert_fusion.11 = bf16[12,64,512]{2,1,0:T(8,128)(2,1)S(1)} fusion(bf16[512,12,64]{0,2,1:T(8,128)(2,1)S(1)} %bitcast.155, bf16[12,512,512]{1,2,0:T(8,128)(2,1)} %copy-done.2), kind=kOutput, calls=%fused_computation.23.clone.1 | convolution fusion | flops 403439616 | bytes 7864320 | tf_op jit(solution)/shard_map/while/body/eval_jaxpr/hqk,khd->qhd/dot_general | solution.py:81
  213.2 6.3 %fusion.146 = f32[12,512,512]{1,2,0:T(8,128)} fusion(bf16[512,12,64]{0,2,1:T(8,128)(2,1)S(1)} %bitcast.156, bf16[512,12,64]{0,2,1:T(8,128)(2,1)S(1)} %bitcast.154), kind=kOutput, calls=%fused_computation.121.clone.1 | convolution fusion | flops 402653184 | bytes 14155776 | tf_op jit(solution)/shard_map/while/body/eval_jaxpr/qhd,khd->hqk/dot_general | solution.py:40
  222.1 11.0 %multiply_reduce_fusion.7 = (f32[12,512]{1,0:T(8,128)S(1)}, f32[12,512,512]{1,2,0:T(8,128)}) fusion(f32[12,512,512]{1,2,0:T(8,128)} %fusion.146, f32[12,512]{1,0:T(8,128)S(1)} %dynamic-slice_bitcast_fusion.2, pred[512,512]{0,1:T(8,128)(4,1)S(1)} %broadcast_compare_fusion.5, bf16[512,12,64]{0,2,1:T(8,128)(2,1)S(1)} %bitcast.159, ...), kind=kOutput, calls=%fused_computation.17.clone.1 | convolution fusion | flops 418375680 | bytes 27049984 | tf_op jit(solution)/shard_map/while/body/eval_jaxpr/qhd,khd->hqk/dot_general | solution.py:72
  234.7 7.0 %multiply_convert_fusion.10 = bf16[12,512,512]{1,2,0:T(8,128)(2,1)S(1)} fusion(f32[12,512,512]{1,2,0:T(8,128)} %get-tuple-element.353, f32[12,512,512]{1,2,0:T(8,128)S(1)} %bitcast.153, f32[12,512]{1,0:T(8,128)S(1)} %get-tuple-element.354, f32[12,512]{1,0:T(8,128)S(1)} %dynamic-slice_bitcast_fusion.2, pred[512,512]{0,1:T(8,128)(4,1)S(1)} %broadcast_compare_fusion.5), kind=kLoop, calls=%fused_computation.16.clone.1 | loop fusion | flops 18874368 | bytes 31768576 | tf_op jit(solution)/shard_map/while/body/eval_jaxpr/convert_element_type | solution.py:80
  244.6 6.3 %fusion.147 = bf16[12,64,512]{2,1,0:T(8,128)(2,1)S(1)} fusion(bf16[512,12,64]{0,2,1:T(8,128)(2,1)S(1)} %bitcast.160, f32[12,512,512]{1,2,0:T(8,128)} %fusion.146, f32[12,512]{1,0:T(8,128)S(1)} %dynamic-slice_bitcast_fusion.2, pred[512,512]{0,1:T(8,128)(4,1)S(1)} %broadcast_compare_fusion.5), kind=kOutput, calls=%fused_computation.24.clone.1 | convolution fusion | flops 415629312 | bytes 14442496 | tf_op jit(solution)/shard_map/while/body/eval_jaxpr/hqk,qhd->khd/dot_general | solution.py:73
  252.5 4.0 %multiply_convert_fusion.11 = bf16[12,64,512]{2,1,0:T(8,128)(2,1)S(1)} fusion(bf16[512,12,64]{0,2,1:T(8,128)(2,1)S(1)} %bitcast.155, bf16[12,512,512]{1,2,0:T(8,128)(2,1)} %copy-done.2), kind=kOutput, calls=%fused_computation.23.clone.1 | convolution fusion | flops 403439616 | bytes 7864320 | tf_op jit(solution)/shard_map/while/body/eval_jaxpr/hqk,khd->qhd/dot_general | solution.py:81
  265.7 2.8 fusion.53
  280.1 39.4 %all-reduce.3.cloned.1.call-done = f32[24576]{0:T(1024)} async-done(((f32[24576]{0:T(1024)}), f32[24576]{0:T(1024)}) %all-reduce.3.cloned.1.call-update) | async-done | bytes 98320
  320.2 18.7 %psum.14 = f32[3072]{0:T(1024)S(1)} all-reduce(f32[3072]{0:T(1024)S(1)} %dynamic-slice.1), channel_id=1, replica_groups=mesh['dp'=4,'wide'=8] {'dp'}, use_global_device_ids=true, to_apply=%region_16.17 | all-reduce | flops 3072 | bytes 24576 | tf_op jit(solution)/shard_map/psum | solution.py:219
  339.4 12.4 %psum.15 = f32[]{:T(128)} all-reduce(f32[]{:T(128)} %multiply_reduce_fusion.5), channel_id=1, replica_groups=mesh['dp'=4,'wide'=8] {'wide'}, use_global_device_ids=true, to_apply=%region_18.19 | all-reduce | flops 1 | bytes 8 | tf_op jit(solution)/shard_map/psum | solution.py:220
  353.9 10.0 %all_gather.3 = f32[24576]{0:T(1024)S(1)} all-gather(f32[3072]{0:T(1024)S(1)} %get-tuple-element.208), channel_id=1, replica_groups=mesh['dp'=4,'wide'=8] {'wide'}, dimensions={0}, use_global_device_ids=true | all-gather | bytes 110592 | tf_op jit(solution)/shard_map/all_gather | solution.py:225
  (232 shorter events, 83.8 us)
Async XLA Ops:
  7.2 57.5 %copy-start = (bf16[768,768]{1,0:T(8,128)(2,1)S(1)}, bf16[768,768]{1,0:T(8,128)(2,1)}, u32[]{:S(2)}) copy-start(bf16[768,768]{1,0:T(8,128)(2,1)} %param.35) | copy-start | bytes 3538948
  7.2 4.7 %copy-start.4 = (bf16[1024,768]{1,0:T(8,128)(2,1)S(1)}, bf16[1024,768]{1,0:T(8,128)(2,1)}, u32[]{:S(2)}) copy-start(bf16[1024,768]{1,0:T(8,128)(2,1)} %param.27) | copy-start | bytes 4718596
  7.2 312.3 %all-reduce.3.cloned.1.call-start = ((), (), s32[]{:S(2)}) async-start(), calls=%async_computation | async-start | bytes 196608
  9.2 6.0 %copy-start.16 = (bf16[768,8]{1,0:T(8,128)(2,1)}, bf16[768,8]{1,0:T(8,128)(2,1)S(1)}, u32[]{:S(2)}) copy-start(bf16[768,8]{1,0:T(8,128)(2,1)S(1)} %slice.53) | copy-start | bytes 36868
  17.0 4.0 %copy-start.32 = (bf16[6144]{0:T(1024)(128)(2,1)S(1)}, bf16[6144]{0:T(1024)(128)(2,1)}, u32[]{:S(2)}) copy-start(bf16[6144]{0:T(1024)(128)(2,1)} %get-tuple-element.223) | copy-start | bytes 36868
  19.0 5.2 %copy-start.18 = (bf16[768,8]{1,0:T(8,128)(2,1)}, bf16[768,8]{1,0:T(8,128)(2,1)S(1)}, u32[]{:S(2)}) copy-start(bf16[768,8]{1,0:T(8,128)(2,1)S(1)} %slice.57) | copy-start | bytes 36868
  32.9 3.9 %copy-start.30 = (s32[2,512]{1,0:T(2,128)S(1)}, s32[2,512]{1,0:T(2,128)}, u32[]{:S(2)}) copy-start(s32[2,512]{1,0:T(2,128)} %param.28) | copy-start | bytes 12292
  36.7 27.9 %copy-start.40 = (bf16[768]{0:T(1024)(128)(2,1)S(1)}, bf16[768]{0:T(1024)(128)(2,1)}, u32[]{:S(2)}) copy-start(bf16[768]{0:T(1024)(128)(2,1)} %param.36) | copy-start | bytes 4612
  64.6 4.2 %copy-start.3 = (bf16[2,512,768]{1,2,0:T(8,128)(2,1)}, bf16[2,512,768]{1,2,0:T(8,128)(2,1)S(1)}, u32[]{:S(2)}) copy-start(bf16[2,512,768]{1,2,0:T(8,128)(2,1)S(1)} %get-tuple-element.427) | copy-start | bytes 4718596
  64.6 5.1 %slice-start.3 = ((s8[4718592]{0:T(1024)(128)(4,1)}), s8[4194304]{0:T(1024)(128)(4,1)S(1)}, s32[]{:S(2)}) async-start(s8[4718592]{0:T(1024)(128)(4,1)} %bitcast.182), calls=%async_computation.4 | async-start | bytes 8388608
  64.7 5.0 %slice-start.4 = ((s8[4718592]{0:T(1024)(128)(4,1)}), s8[524288]{0:T(1024)(128)(4,1)S(1)}, s32[]{:S(2)}) async-start(s8[4718592]{0:T(1024)(128)(4,1)} %bitcast.182), calls=%async_computation.5 | async-start | bytes 1048576
  68.8 37.3 %copy-start.12 = (f32[1024,768]{0,1:T(8,128)}, f32[1024,768]{0,1:T(8,128)S(1)}, u32[]{:S(2)}) copy-start(f32[1024,768]{0,1:T(8,128)S(1)} %get-tuple-element.230) | copy-start | bytes 9437188
  163.6 94.7 %copy-start.28 = (bf16[8,768]{1,0:T(8,128)(2,1)S(1)}, bf16[8,768]{1,0:T(8,128)(2,1)}, u32[]{:S(2)}) copy-start(bf16[8,768]{1,0:T(8,128)(2,1)} %copy-done.27) | copy-start | bytes 36868
  163.6 96.8 %copy-start.24 = (bf16[1024,8]{0,1:T(8,128)(2,1)S(1)}, bf16[1024,8]{0,1:T(8,128)(2,1)}, u32[]{:S(2)}) copy-start(bf16[1024,8]{0,1:T(8,128)(2,1)} %copy-done.23) | copy-start | bytes 49156
  166.0 7.4 %copy-start.15 = (bf16[2,512,768]{2,1,0:T(8,128)(2,1)S(1)}, bf16[2,512,768]{2,1,0:T(8,128)(2,1)}, u32[]{:S(2)}) copy-start(bf16[2,512,768]{2,1,0:T(8,128)(2,1)} %get-tuple-element.411) | copy-start | bytes 4718596 | tf_op jit(solution)/shard_map/while
  174.9 11.0 %slice-start = ((s8[12582912]{0:T(1024)(128)(4,1)}), s8[4194304]{0:T(1024)(128)(4,1)S(1)}, s32[]{:S(2)}) async-start(s8[12582912]{0:T(1024)(128)(4,1)} %bitcast.152), calls=%async_computation.1 | async-start | bytes 8388608 | tf_op jit(solution)/shard_map/while
  174.9 11.0 %slice-start.1 = ((s8[12582912]{0:T(1024)(128)(4,1)}), s8[4194304]{0:T(1024)(128)(4,1)S(1)}, s32[]{:S(2)}) async-start(s8[12582912]{0:T(1024)(128)(4,1)} %bitcast.152), calls=%async_computation.2 | async-start | bytes 8388608 | tf_op jit(solution)/shard_map/while
  175.0 12.6 %slice-start.2 = ((s8[12582912]{0:T(1024)(128)(4,1)}), s8[4194304]{0:T(1024)(128)(4,1)S(1)}, s32[]{:S(2)}) async-start(s8[12582912]{0:T(1024)(128)(4,1)} %bitcast.152), calls=%async_computation.3 | async-start | bytes 8388608 | tf_op jit(solution)/shard_map/while
  205.3 4.3 %copy-start.6 = (bf16[2,512,768]{2,1,0:T(8,128)(2,1)S(1)}, bf16[2,512,768]{2,1,0:T(8,128)(2,1)}, u32[]{:S(2)}) copy-start(bf16[2,512,768]{2,1,0:T(8,128)(2,1)} %get-tuple-element.393) | copy-start | bytes 4718596 | tf_op jit(solution)/shard_map/while
  213.2 7.4 %copy-start.15 = (bf16[2,512,768]{2,1,0:T(8,128)(2,1)S(1)}, bf16[2,512,768]{2,1,0:T(8,128)(2,1)}, u32[]{:S(2)}) copy-start(bf16[2,512,768]{2,1,0:T(8,128)(2,1)} %get-tuple-element.411) | copy-start | bytes 4718596 | tf_op jit(solution)/shard_map/while
  222.1 11.0 %slice-start = ((s8[12582912]{0:T(1024)(128)(4,1)}), s8[4194304]{0:T(1024)(128)(4,1)S(1)}, s32[]{:S(2)}) async-start(s8[12582912]{0:T(1024)(128)(4,1)} %bitcast.152), calls=%async_computation.1 | async-start | bytes 8388608 | tf_op jit(solution)/shard_map/while
  222.1 11.0 %slice-start.1 = ((s8[12582912]{0:T(1024)(128)(4,1)}), s8[4194304]{0:T(1024)(128)(4,1)S(1)}, s32[]{:S(2)}) async-start(s8[12582912]{0:T(1024)(128)(4,1)} %bitcast.152), calls=%async_computation.2 | async-start | bytes 8388608 | tf_op jit(solution)/shard_map/while
  222.1 12.6 %slice-start.2 = ((s8[12582912]{0:T(1024)(128)(4,1)}), s8[4194304]{0:T(1024)(128)(4,1)S(1)}, s32[]{:S(2)}) async-start(s8[12582912]{0:T(1024)(128)(4,1)} %bitcast.152), calls=%async_computation.3 | async-start | bytes 8388608 | tf_op jit(solution)/shard_map/while
  252.5 4.3 %copy-start.6 = (bf16[2,512,768]{2,1,0:T(8,128)(2,1)S(1)}, bf16[2,512,768]{2,1,0:T(8,128)(2,1)}, u32[]{:S(2)}) copy-start(bf16[2,512,768]{2,1,0:T(8,128)(2,1)} %get-tuple-element.393) | copy-start | bytes 4718596 | tf_op jit(solution)/shard_map/while
  258.3 3.9 %copy-start.9 = (bf16[2,512,768]{2,1,0:T(8,128)(2,1)S(1)}, bf16[2,512,768]{2,1,0:T(8,128)(2,1)}, u32[]{:S(2)}) copy-start(bf16[2,512,768]{2,1,0:T(8,128)(2,1)} %get-tuple-element.102) | copy-start | bytes 4718596
  258.3 4.4 %copy-start.22 = (bf16[1024,8]{0,1:T(8,128)(2,1)S(1)}, bf16[1024,8]{0,1:T(8,128)(2,1)}, u32[]{:S(2)}) copy-start(bf16[1024,8]{0,1:T(8,128)(2,1)} %copy-done.21) | copy-start | bytes 49156
  258.3 4.7 %copy-start.5 = (bf16[1024,768]{1,0:T(8,128)(2,1)S(1)}, bf16[1024,768]{1,0:T(8,128)(2,1)}, u32[]{:S(2)}) copy-start(bf16[1024,768]{1,0:T(8,128)(2,1)} %param.27) | copy-start | bytes 4718596
  274.6 89.9 %copy-start.1 = (bf16[768,768]{1,0:T(8,128)(2,1)S(1)}, bf16[768,768]{1,0:T(8,128)(2,1)}, u32[]{:S(2)}) copy-start(bf16[768,768]{1,0:T(8,128)(2,1)} %param.35) | copy-start | bytes 3538948
  274.7 4.2 %copy-start.48 = (u32[32]{0:T(128)S(1)}, u32[32]{0:T(128)}, u32[]{:S(2)}) copy-start(u32[32]{0:T(128)} %constant.169) | copy-start | bytes 388
  274.7 77.9 %copy-start.35 = (f32[3072]{0:T(1024)S(1)}, f32[3072]{0:T(1024)}, u32[]{:S(2)}) copy-start(f32[3072]{0:T(1024)} %param.47) | copy-start | bytes 36868
  274.7 77.9 %copy-start.36 = (f32[3072]{0:T(1024)S(1)}, f32[3072]{0:T(1024)}, u32[]{:S(2)}) copy-start(f32[3072]{0:T(1024)} %param.46) | copy-start | bytes 36868
  338.8 25.7 %copy-start.29 = (f32[3072]{0:T(1024)}, f32[3072]{0:T(1024)S(1)}, u32[]{:S(2)}) copy-start(f32[3072]{0:T(1024)S(1)} %psum.14) | copy-start | bytes 36868
  (30 other events, 66.5 us)
Sparse Core Ops, SparseCore 0:
  265.2 54.1 all-reduce.2
where the time goes:
time: 378 us; the launch traced here: 372 us
  matrix products  184 us (49%)
  local copies, waits for them, and re-layouts  53.9 us (14%)
  blocking collectives  41.1 us (11%)
  waiting for transfers between devices  39.4 us (10%)
  other arithmetic  34.4 us (9%)
  between operations  17.9 us (5%)
    dot_general x23, matrix products, matrix_product(): return jnp.dot(left, right, preferred_element_type=jnp.float32)  112 us
    unnamed x2, waiting for transfers between devices  39.4 us
    dot_general x2, matrix products, attend_back(): jnp.einsum('qhd,khd->hqk', d_heads, value_heads, preferred_element_type=j...  22 us
    psum x1, blocking collectives, shards(): owned_grad = lax.psum(share_part, 'dp')  18.7 us
    dot_general x4, matrix products, masked_scores(): jnp.einsum('qhd,khd->hqk', query_heads, key_heads, preferred_element_type...  16.9 us
    convert_element_type x2, other arithmetic, attend_back(): d_scores = (soft_weights * (d_soft - row_delta)).astype(jnp.bfloat16)  14 us
    dot_general x2, matrix products, attend_back(): jnp.einsum('hqk,qhd->khd', soft_weights.astype(jnp.bfloat16), d_heads, pr...  12.7 us
    psum x1, blocking collectives, shards(): norm_sq = lax.psum(jnp.sum(owned_grad * owned_grad), 'wide')  12.4 us
  transfers between devices with their start and end apart: 1, of which 1 were waited for; matrix products, arithmetic and copies ran while one was open for 3% of the time, Pallas kernels for 0%

commit v1 on v0

v1 whole, which is shorter than its diff:
```python
import functools

import jax
import jax.numpy as jnp
from jax import lax
from jax.experimental import pallas as pl
from jax.experimental.pallas import tpu as pltpu
from jax.sharding import PartitionSpec as P

HEADS = 12
RANK = 8
BIG = 256
HEAD_DIM = 64
LANES = 128

norm_eps = 1e-05
adapter_scale = 2.0
beta_one = 0.9
beta_two = 0.999
adam_eps = 1e-08
decay_rate = 0.01
rate_ratio = 16.0

bf16 = jnp.bfloat16
f32 = jnp.float32


def dot(left, right, ca=1, cb=0):
    return lax.dot_general(left, right, (((ca,), (cb,)), ((), ())), preferred_element_type=f32)


def rotate_rows(src, shift, emit):
    groups, _, width = src.shape
    coarse, fine = shift // 8, shift % 8
    back = lax.rem(8 - fine, 8)
    keep = lax.broadcasted_iota(jnp.int32, (8, width), 0) < 8 - fine
    spun = [
        pltpu.roll(src[lax.rem(coarse + i, groups)], back, 0) for i in range(groups + 1)
    ]
    moved = [jnp.where(keep, spun[i], spun[i + 1]) for i in range(groups)]
    for i in range(0, groups, 2):
        emit(i * 8, jnp.concatenate([moved[i], moved[i + 1]], axis=0))


def norm_rows(z):
    mean = jnp.mean(z, axis=-1, keepdims=True)
    centered = z - mean
    spread = jnp.mean(centered * centered, axis=-1, keepdims=True)
    root = lax.rsqrt(spread + norm_eps)
    return centered * root, root


def norm_rows_back(c, n, root):
    return root * (
        c - jnp.mean(c, axis=-1, keepdims=True) - n * jnp.mean(c * n, axis=-1, keepdims=True)
    )


def main_kernel(
    start_ref,
    tok_ref,
    cot_ref,
    seg_lo,
    seg_hi,
    wq_hbm,
    wk_hbm,
    wv_hbm,
    wo_hbm,
    wu_hbm,
    wd_hbm,
    dcat,
    uq,
    uv,
    bq,
    bv,
    bo,
    g1,
    b1,
    bu,
    bd,
    g2,
    b2,
    out_ref,
    dfirst_ref,
    dq_ref,
    dk_ref,
    dv_ref,
    dl_ref,
    grad_ref,
    wq,
    wk,
    wv,
    wo,
    wu,
    wd,
    sems,
    spin,
    xr,
    cr,
    qs,
    ks,
    vs,
    lora,
    probs,
    att,
    zs,
    n1,
    r1,
    hb,
    act,
    gp,
):
    pid = pl.program_id(0)
    rows, width = tok_ref.shape
    pairs = width // LANES
    copies = [
        pltpu.make_async_copy(src, dst, sems.at[i])
        for i, (src, dst) in enumerate(
            ((wq_hbm, wq), (wk_hbm, wk), (wv_hbm, wv), (wo_hbm, wo), (wu_hbm, wu), (wd_hbm, wd))
        )
    ]

    @pl.when(pid == 0)
    def _():
        for copy in copies:
            copy.start()

    def arrive(*which):
        @pl.when(pid == 0)
        def _():
            for i in which:
                copies[i].wait()

    start = start_ref[pid]

    def put(dst):
        def emit(at, block):
            dst[pl.ds(at, 16), :] = block.astype(dst.dtype)

        return emit

    spin[...] = tok_ref[...].astype(f32).reshape(spin.shape)
    rotate_rows(spin, start, put(xr))
    spin[...] = cot_ref[...].astype(f32).reshape(spin.shape)
    rotate_rows(spin, start, put(cr))

    lora[...] = dot(xr[...], dcat[...]).astype(bf16)
    arrive(0, 1, 2)
    query = dot(xr[...], wq[...]) + dot(lora[...], uq[...]) + bq[...].astype(f32)
    qs[...] = query.astype(bf16) * bf16(HEAD_DIM**-0.5)
    ks[...] = dot(xr[...], wk[...]).astype(bf16)
    value = dot(xr[...], wv[...]) + dot(lora[...], uv[...]) + bv[...].astype(f32)
    vs[...] = value.astype(bf16)

    row = lax.broadcasted_iota(jnp.int32, (BIG, LANES), 0) + (BIG + start)
    row = jnp.where(row >= rows, row - rows, row)
    lane = lax.broadcasted_iota(jnp.int32, (BIG, LANES), 1)
    inside = (row >= seg_lo[pl.ds(pid, 1), :]) & (row < seg_hi[pl.ds(pid, 1), :])
    own = jnp.where(inside, 1.0, 0.0)
    used = (lane % HEAD_DIM) < 8
    own_q = own.astype(bf16)
    other_k = jnp.where(used & jnp.logical_not(inside), -1e30, 0.0).astype(bf16)
    low = lane < HEAD_DIM
    none = jnp.zeros((BIG, LANES), bf16)

    def pair_forward(p, carry):
        at = pl.ds(pl.multiple_of(p * LANES, LANES), LANES)
        for block in range(2):
            span = pl.ds(block * BIG, BIG)
            qp, kp, vp = qs[span, at], ks[span, at], vs[span, at]
            fq, fk = (none, none) if block == 0 else (own_q, other_k)
            heads = []
            for half in range(2):
                mine = low if half == 0 else jnp.logical_not(low)
                scores = dot(jnp.where(mine, qp, fq), jnp.where(mine, kp, fk), 1, 1)
                top = jnp.max(scores, axis=-1, keepdims=True)
                e = jnp.exp(scores - top)
                total = jnp.sum(e, axis=-1, keepdims=True)
                soft = (e * (1.0 / total)).astype(bf16)
                probs[2 * p + half, block] = soft
                heads.append(dot(soft, vp))
            att[span, at] = jnp.where(low, heads[0], heads[1]).astype(bf16)
        return carry

    lax.fori_loop(0, pairs, pair_forward, 0)

    arrive(3)
    zs[...] = dot(att[...], wo[...])
    step = 64

    def first_norm(i, carry):
        at = pl.ds(pl.multiple_of(i * step, step), step)
        z = xr[at, :].astype(f32) + zs[at, :] + bo[...].astype(f32)
        n, root = norm_rows(z)
        n1[at, :] = n
        r1[at, :] = root
        hb[at, :] = (n * g1[...].astype(f32) + b1[...].astype(f32)).astype(bf16)
        return carry

    lax.fori_loop(0, rows // step, first_norm, 0)

    arrive(4)
    chunk = width
    count = act.shape[1] // chunk

    def up(c, carry):
        at = pl.ds(pl.multiple_of(c * chunk, chunk), chunk)
        u = dot(hb[...], wu[:, at]) + bu[:, at].astype(f32)
        half_cdf = 0.5 + 0.5 * lax.erf(u * (0.5**0.5))
        act[:, at] = (u * half_cdf).astype(bf16)
        bell = jnp.exp(u * u * -0.5) * 0.3989422804014327
        gp[:, at] = (half_cdf + u * bell).astype(bf16)
        return carry

    lax.fori_loop(0, count, up, 0)
    arrive(5)

    def down(c, carry):
        at = pl.ds(pl.multiple_of(c * BIG, BIG), BIG)
        zs[:, at] = dot(act[...], wd[:, at])
        return carry

    lax.fori_loop(0, width // BIG, down, 0)

    def second_norm(i, carry):
        at = pl.ds(pl.multiple_of(i * step, step), step)
        hidden = n1[at, :] * g1[...].astype(f32) + b1[...].astype(f32)
        z = hidden + zs[at, :] + bd[...].astype(f32)
        n, root = norm_rows(z)
        gain = g2[...].astype(f32)
        result = n * gain + b2[...].astype(f32)
        spin[pl.ds(i * (step // 8), step // 8)] = result.reshape(step // 8, 8, width)
        d = norm_rows_back(cr[at, :].astype(f32) * gain, n, root)
        zs[at, :] = d
        hb[at, :] = d.astype(bf16)
        return carry

    lax.fori_loop(0, rows // step, second_norm, 0)
    rotate_rows(spin, rows - start, put(out_ref))

    def up_back(c, carry):
        at = pl.ds(pl.multiple_of(c * chunk, chunk), chunk)
        t = dot(hb[...], wd[at, :], 1, 1)
        act[:, at] = (t * gp[:, at].astype(f32)).astype(bf16)
        return carry

    lax.fori_loop(0, count, up_back, 0)

    def down_back(c, carry):
        at = pl.ds(pl.multiple_of(c * BIG, BIG), BIG)
        zs[:, at] = zs[:, at] + dot(act[...], wu[at, :], 1, 1)
        return carry

    lax.fori_loop(0, width // BIG, down_back, 0)

    def first_norm_back(i, carry):
        at = pl.ds(pl.multiple_of(i * step, step), step)
        d = norm_rows_back(zs[at, :] * g1[...].astype(f32), n1[at, :], r1[at, :])
        dfirst_ref[at, :] = d
        hb[at, :] = d.astype(bf16)
        return carry

    lax.fori_loop(0, rows // step, first_norm_back, 0)
    cr[...] = dot(hb[...], wo[...], 1, 1).astype(bf16)

    def pair_back(p, carry):
        at = pl.ds(pl.multiple_of(p * LANES, LANES), LANES)
        for block in range(2):
            span = pl.ds(block * BIG, BIG)
            qp, kp, vp, dp = qs[span, at], ks[span, at], vs[span, at], cr[span, at]
            both = dp.astype(f32) * att[span, at].astype(f32)
            dqs, dks, dvs = [], [], []
            for half in range(2):
                mine = low if half == 0 else jnp.logical_not(low)
                delta = jnp.sum(jnp.where(mine, both, 0.0), axis=-1, keepdims=True)
                d_soft = dot(jnp.where(mine, dp, none), vp, 1, 1)
                soft = probs[2 * p + half, block]
                ds = (soft.astype(f32) * (d_soft - delta)).astype(bf16)
                dqs.append(dot(ds, kp))
                dks.append(dot(ds, qp, 0, 0))
                dvs.append(dot(soft, dp, 0, 0))
            dq_ref[span, at] = (jnp.where(low, *dqs) * HEAD_DIM**-0.5).astype(bf16)
            dk_ref[span, at] = jnp.where(low, *dks).astype(bf16)
            dv_ref[span, at] = jnp.where(low, *dvs).astype(bf16)
        return carry

    lax.fori_loop(0, pairs, pair_back, 0)

    dl = (dot(dq_ref[...], uq[...], 1, 1) + dot(dv_ref[...], uv[...], 1, 1)).astype(bf16)
    dl_ref[...] = dl
    gd = dot(dl, xr[...], 0, 0)
    gq = adapter_scale * dot(lora[...], dq_ref[...], 0, 0)
    gv = adapter_scale * dot(lora[...], dv_ref[...], 0, 0)
    grads = jnp.concatenate([gd[: 2 * RANK], gq[:RANK], gv[RANK : 2 * RANK]], axis=0)

    @pl.when(pid == 0)
    def _():
        grad_ref[...] = grads

    @pl.when(pid > 0)
    def _():
        grad_ref[...] += grads


def token_kernel(start_ref, dfirst, dq, dk, dv, dl, wq, wk, wv, dcat, out_ref, spin):
    pid = pl.program_id(0)
    rows, width = dfirst.shape
    total = dot(dq[...], wq[...], 1, 1) + dot(dk[...], wk[...], 1, 1)
    total = total + dot(dv[...], wv[...], 1, 1) + dot(dl[...], dcat[...], 1, 1)
    spin[...] = (dfirst[...] + total).reshape(spin.shape)

    def emit(at, block):
        out_ref[pl.ds(at, 16), :] = block.astype(bf16)

    rotate_rows(spin, rows - start_ref[pid], emit)


def swap(x, axis, bit):
    n = lax.axis_size(axis)
    return lax.ppermute(x, axis, [(i, i ^ bit) for i in range(n)])


def bits_of(axis):
    n = lax.axis_size(axis)
    return [1 << k for k in range(n.bit_length() - 1)]


def gather_shares(share, axis):
    index = lax.axis_index(axis)
    held = share[None]
    for bit in bits_of(axis):
        other = swap(held, axis, bit)
        first = (index & bit) == 0
        held = jnp.where(
            first, jnp.concatenate([held, other]), jnp.concatenate([other, held])
        )
    return held.reshape(-1)


def adam_update(params, gradient, first, second, norm_sq, steps_done, rate_now):
    clip = jnp.minimum(1.0, lax.rsqrt(norm_sq + 1e-06))
    clipped = gradient * clip
    first_new = beta_one * first + (1.0 - beta_one) * clipped
    second_new = beta_two * second + (1.0 - beta_two) * clipped * clipped
    fix_one = 1.0 - jnp.power(beta_one, steps_done)
    fix_two = 1.0 - jnp.power(beta_two, steps_done)
    update = first_new / fix_one / (jnp.sqrt(second_new / fix_two) + adam_eps) + decay_rate * params
    return (params - rate_now * update, first_new, second_new)


def shards(
    tokens,
    segment_ids,
    cotangent,
    query_frozen_weight,
    query_bias_vector,
    w_key,
    value_frozen_weight,
    value_bias_vector,
    w_out,
    b_out,
    norm1_gain,
    norm1_bias,
    w_up,
    b_up,
    w_down,
    b_down,
    norm2_gain,
    norm2_bias,
    factors,
    moment_first,
    moment_second,
    step_count,
    learn_rate,
):
    width = tokens.shape[1]
    packs, rows = segment_ids.shape
    ff = w_up.shape[1]
    block_len = width * RANK
    low = factors.astype(bf16)
    dcat = jnp.zeros((width, LANES), bf16)
    dcat = dcat.at[:, :RANK].set(low[:block_len].reshape(width, RANK))
    dcat = dcat.at[:, RANK : 2 * RANK].set(low[block_len : 2 * block_len].reshape(width, RANK))
    ups = low[2 * block_len :].reshape(2 * RANK, width) * bf16(adapter_scale)
    uq = jnp.zeros((LANES, width), bf16).at[:RANK].set(ups[:RANK])
    uv = jnp.zeros((LANES, width), bf16).at[RANK : 2 * RANK].set(ups[RANK:])

    same = segment_ids[:, : rows - BIG + 1] == segment_ids[:, BIG - 1 :]
    start = jnp.sum(jnp.where(same, jnp.arange(rows - BIG + 1), 0), axis=1).astype(jnp.int32)
    slot = jnp.arange(LANES) % HEAD_DIM
    seg_lo = jnp.sum(segment_ids[:, None, :] < slot[None, :, None], axis=2).astype(jnp.int32)
    seg_hi = jnp.sum(segment_ids[:, None, :] <= slot[None, :, None], axis=2).astype(jnp.int32)

    def vec(v):
        return v.reshape(1, -1)

    per_pack = pl.BlockSpec((rows, width), lambda i, s: (i, 0))
    whole = lambda shape: pl.BlockSpec(shape, lambda i, s: (0,) * len(shape))
    anywhere = pl.BlockSpec(memory_space=pl.ANY)
    total_rows = packs * rows
    result = lambda shape, dtype: jax.ShapeDtypeStruct(shape, dtype)
    weights = (query_frozen_weight, w_key, value_frozen_weight, w_out, w_up, w_down)
    vectors = (
        query_bias_vector,
        value_bias_vector,
        b_out,
        norm1_gain,
        norm1_bias,
        b_up,
        b_down,
        norm2_gain,
        norm2_bias,
    )
    output, dfirst, dq, dk, dv, dl, grads = pl.pallas_call(
        main_kernel,
        out_shape=(
            result((total_rows, width), bf16),
            result((total_rows, width), f32),
            result((total_rows, width), bf16),
            result((total_rows, width), bf16),
            result((total_rows, width), bf16),
            result((total_rows, LANES), bf16),
            result((4 * RANK, width), f32),
        ),
        grid_spec=pltpu.PrefetchScalarGridSpec(
            num_scalar_prefetch=1,
            grid=(packs,),
            in_specs=[per_pack, per_pack, whole((packs, LANES)), whole((packs, LANES))]
            + [anywhere] * 6
            + [whole((width, LANES)), whole((LANES, width)), whole((LANES, width))]
            + [whole((1, v.shape[0])) for v in vectors],
            out_specs=[per_pack] * 5
            + [pl.BlockSpec((rows, LANES), lambda i, s: (i, 0)), whole((4 * RANK, width))],
            scratch_shapes=[pltpu.VMEM(w.shape, bf16) for w in weights]
            + [
                pltpu.SemaphoreType.DMA((6,)),
                pltpu.VMEM((rows // 8, 8, width), f32),
                pltpu.VMEM((rows, width), bf16),
                pltpu.VMEM((rows, width), bf16),
                pltpu.VMEM((rows, width), bf16),
                pltpu.VMEM((rows, width), bf16),
                pltpu.VMEM((rows, width), bf16),
                pltpu.VMEM((rows, LANES), bf16),
                pltpu.VMEM((HEADS, 2, BIG, BIG), bf16),
                pltpu.VMEM((rows, width), bf16),
                pltpu.VMEM((rows, width), f32),
                pltpu.VMEM((rows, width), f32),
                pltpu.VMEM((rows, 1), f32),
                pltpu.VMEM((rows, width), bf16),
                pltpu.VMEM((rows, ff), bf16),
                pltpu.VMEM((rows, ff), bf16),
            ],
        ),
        compiler_params=pltpu.CompilerParams(
            dimension_semantics=("arbitrary",), vmem_limit_bytes=60 * 2**20
        ),
    )(
        start,
        tokens,
        cotangent,
        seg_lo,
        seg_hi,
        *weights,
        dcat,
        uq,
        uv,
        *[vec(v) for v in vectors],
    )

    down_grads = grads[: 2 * RANK].reshape(2, RANK, width).transpose(0, 2, 1).reshape(-1)
    total = jnp.concatenate([down_grads, grads[2 * RANK :].reshape(-1)])
    for axis in ("wide", "dp"):
        for bit in bits_of(axis):
            total = total + swap(total, axis, bit)

    grad_tokens = pl.pallas_call(
        token_kernel,
        out_shape=result((total_rows, width), bf16),
        grid_spec=pltpu.PrefetchScalarGridSpec(
            num_scalar_prefetch=1,
            grid=(packs,),
            in_specs=[per_pack] * 4
            + [pl.BlockSpec((rows, LANES), lambda i, s: (i, 0))]
            + [whole((width, width))] * 3
            + [whole((width, LANES))],
            out_specs=per_pack,
            scratch_shapes=[pltpu.VMEM((rows // 8, 8, width), f32)],
        ),
        compiler_params=pltpu.CompilerParams(
            dimension_semantics=("arbitrary",), vmem_limit_bytes=40 * 2**20
        ),
    )(start, dfirst, dq, dk, dv, dl, *weights[:3], dcat)

    wide_count = lax.axis_size("wide")
    wide_index = lax.axis_index("wide")
    own_len = factors.shape[0] // wide_count
    steps_done = step_count[0].astype(f32)
    rate_now = jnp.where(wide_index < wide_count // 2, learn_rate[0], rate_ratio * learn_rate[0])
    norm_sq = jnp.sum(total * total)
    owned_grad = lax.dynamic_slice_in_dim(total, wide_index * own_len, own_len)
    own_params = lax.dynamic_slice_in_dim(factors, wide_index * own_len, own_len)
    params_new, new_first, new_second = adam_update(
        own_params, owned_grad, moment_first, moment_second, norm_sq, steps_done, rate_now
    )
    new_factors = gather_shares(params_new, "wide")
    return (output, grad_tokens, owned_grad, new_factors, new_first, new_second)


def solution(mesh):
    rows = P(("dp", "wide"), None)
    in_specs = (rows,) * 3 + (P(),) * 16 + (P("wide"), P("wide"), P(), P())
    out_specs = (rows, rows, P("wide"), P(), P("wide"), P("wide"))
    return jax.shard_map(shards, mesh=mesh, in_specs=in_specs, out_specs=out_specs, check_vma=False)
```

time: 378 us -> 172 us (0.46); the launches traced: 372 us -> 171 us
  matrix products: 184 us -> 0 us
  Pallas kernels: 0 us -> 95.6 us
  blocking collectives: 41.1 us -> 0 us
  local copies, waits for them, and re-layouts: 53.9 us -> 28.1 us
  waiting for transfers between devices: 39.4 us -> 15.2 us
  other arithmetic: 34.4 us -> 15.5 us
  between operations: 17.9 us -> 2.92 us
  starting transfers between devices: 0.04 us -> 13.5 us
    dot_general x37 -> x0, matrix products: 184 us -> none  [the longest x23 112 us: matrix_product(): return jnp.dot(left, right, preferred_element_type=jnp.float32)]
    pallas_call x0 -> x2, Pallas kernels: none -> 95.6 us  [the longest x1 89.3 us: shards(): pl.pallas_call(main_kernel, out_shape=(result((total_rows, width), bf16),...]
    unnamed x2 -> x0, waiting for transfers between devices: 39.4 us -> none
    psum x2 -> x0, blocking collectives: 31.1 us -> none  [the longest x1 18.7 us: shards(): owned_grad = lax.psum(share_part, 'dp')]
    ppermute x0 -> x8, waiting for transfers between devices: none -> 15.2 us  [swap(): return lax.ppermute(x, axis, [(i, i ^ bit) for i in range(n)])]
    convert_element_type x12 -> x1, other arithmetic: 15 us -> 0.9 us  [shards(): low = factors.astype(bf16)]
    while x31 -> x0, local copies, waits for them, and re-layouts: 13.6 us -> none  [the longest x3 6.92 us: shards(): attended, log_total = lax.map(attend_pack, packed)]
    ppermute x0 -> x8, starting transfers between devices: none -> 13.5 us  [swap(): return lax.ppermute(x, axis, [(i, i ^ bit) for i in range(n)])]
  transfers between devices with their start and end apart: 1 -> 8, of which waited for: 1 -> 7; matrix products, arithmetic and copies ran while one was open for 3% -> 0% of each run, Pallas kernels for 0% -> 4%
where the time goes in v1:
time: 172 us; the launch traced here: 171 us
  Pallas kernels  95.6 us (56%)
  local copies, waits for them, and re-layouts  28.1 us (16%)
  other arithmetic  15.5 us (9%)
  waiting for transfers between devices  15.2 us (9%)
  starting transfers between devices  13.5 us (8%)
  between operations  2.92 us (2%)
    pallas_call x1, Pallas kernels, shards(): pl.pallas_call(main_kernel, out_shape=(result((total_rows, width), bf16),...  89.3 us
    ppermute x8, waiting for transfers between devices, swap(): return lax.ppermute(x, axis, [(i, i ^ bit) for i in range(n)])  15.2 us
    ppermute x8, starting transfers between devices, swap(): return lax.ppermute(x, axis, [(i, i ^ bit) for i in range(n)])  13.5 us
    unnamed x42, local copies, waits for them, and re-layouts  10.8 us
    pallas_call x1, Pallas kernels, shards(): pl.pallas_call(token_kernel, out_shape=result((total_rows, width), bf16),...  6.34 us
    reshape x9, local copies, waits for them, and re-layouts, vec(): return v.reshape(1, -1)  5.33 us
  transfers between devices with their start and end apart: 8, of which 7 were waited for; matrix products, arithmetic and copies ran while one was open for 0% of the time, Pallas kernels for 4%

profile of v1, /device:TPU:0, one launch (start us, length us, event | category | flops | bytes accessed | tf_op | source)
XLA Modules:
  0.0 170.8 jit_solution(3350377145799953484)
XLA Ops:
  2.0 1.5 fusion.2.start_ref
  3.5 1.5 convert_reduce_fusion
  5.9 1.3 slice_select_fusion
  14.6 2.4 %scatter.15.dcat = bf16[768,128]{1,0:T(8,128)(2,1)S(1)} dynamic-update-slice(bf16[768,128]{1,0:T(8,128)(2,1)S(1)} %scatter.14, bf16[768,8]{1,0:T(8,128)(2,1)S(1)} %reshape.209, s32[]{:T(128)} %constant.143.clone.1, s32[]{:T(128)} %constant.149.clone.1) | dynamic-update-slice | bytes 24580 | tf_op jit(solution)/shard_map/scatter | solution.py:383
  17.7 89.3 %shard_map.262 = (bf16[1024,768]{1,0:T(8,128)(2,1)}, f32[1024,768]{1,0:T(8,128)}, bf16[1024,768]{1,0:T(8,128)(2,1)}, bf16[1024,768]{1,0:T(8,128)(2,1)}, bf16[102...) custom-call(s32[2]{0:T(128)} %fusion.2.start_ref, bf16[1024,768]{1,0:T(8,128)(2,1)} %tok_ref.1, ...), custom_call_target="tpu_custom_call" | custom-call | tf_op jit(solution)/shard_map/pallas_call | solution.py:414
  107.0 1.4 fusion.4
  108.4 1.2 copy.30
  109.6 2.2 %reshape.220 = f32[12288]{0:T(1024)} reshape(f32[2,768,8]{2,1,0:T(8,128)} %bitcast.12) | data formatting | bytes 98304 | tf_op jit(solution)/shard_map/reshape | solution.py:470
  111.8 1.4 constant_dynamic-update-slice_fusion.1
  113.2 1.4 reshape.221
  114.6 1.4 constant_dynamic-update-slice_fusion
  118.6 2.9 %collective-permute-start.1 = (f32[24576]{0:T(1024)S(1)}, f32[24576]{0:T(1024)S(1)}, u32[]{:S(2)}, u32[]{:S(2)}) collective-permute-start(f32[24576]{0:T(1024)S(1)} %add.64), channel_id=1, source_target_pairs={{0,2},{1,3},{2,0},{3,1},{4,6},{5,7},{6,4},{7,5},{8,10},{9,11},{10,... | collective-permute-start | bytes 294920 | tf_op jit(solution)/shard_map/ppermute | solution.py:320
  121.5 3.1 %collective-permute-done.1 = f32[24576]{0:T(1024)S(1)} collective-permute-done((f32[24576]{0:T(1024)S(1)}, f32[24576]{0:T(1024)S(1)}, u32[]{:S(2)}, u32[]{:S(2)}) %collective-permute-start.1) | collective-permute-done | bytes 98336 | tf_op jit(solution)/shard_map/ppermute | solution.py:320
  124.6 1.8 %collective-permute-start.2 = (f32[24576]{0:T(1024)S(1)}, f32[24576]{0:T(1024)S(1)}, u32[]{:S(2)}, u32[]{:S(2)}) collective-permute-start(f32[24576]{0:T(1024)S(1)} %add.65), channel_id=1, source_target_pairs={{0,4},{1,5},{2,6},{3,7},{4,0},{5,1},{6,2},{7,3},{8,12},{9,13},{10,... | collective-permute-start | bytes 294920 | tf_op jit(solution)/shard_map/ppermute | solution.py:320
  126.4 2.8 %collective-permute-done.2 = f32[24576]{0:T(1024)S(1)} collective-permute-done((f32[24576]{0:T(1024)S(1)}, f32[24576]{0:T(1024)S(1)}, u32[]{:S(2)}, u32[]{:S(2)}) %collective-permute-start.2) | collective-permute-done | bytes 98336 | tf_op jit(solution)/shard_map/ppermute | solution.py:320
  129.3 1.9 %collective-permute-start.3 = (f32[24576]{0:T(1024)S(1)}, f32[24576]{0:T(1024)S(1)}, u32[]{:S(2)}, u32[]{:S(2)}) collective-permute-start(f32[24576]{0:T(1024)S(1)} %add.66), channel_id=1, source_target_pairs={{0,8},{8,0},{16,24},{24,16},{1,9},{9,1},{17,25},{25,17},{2,10},{10... | collective-permute-start | bytes 294920 | tf_op jit(solution)/shard_map/ppermute | solution.py:320
  131.2 2.8 %collective-permute-done.3 = f32[24576]{0:T(1024)S(1)} collective-permute-done((f32[24576]{0:T(1024)S(1)}, f32[24576]{0:T(1024)S(1)}, u32[]{:S(2)}, u32[]{:S(2)}) %collective-permute-start.3) | collective-permute-done | bytes 98336 | tf_op jit(solution)/shard_map/ppermute | solution.py:320
  134.6 2.8 %collective-permute-start.4 = (f32[24576]{0:T(1024)}, f32[24576]{0:T(1024)}, u32[]{:S(2)}, u32[]{:S(2)}) collective-permute-start(f32[24576]{0:T(1024)} %add.67), channel_id=1, source_target_pairs={{0,16},{8,24},{16,0},{24,8},{1,17},{9,25},{17,1},{25,9},{2,18},{10... | collective-permute-start | bytes 294920 | tf_op jit(solution)/shard_map/ppermute | solution.py:320
  138.9 1.6 collective-permute-done.4
  140.5 2.2 %multiply_reduce_fusion = (f32[]{:T(128)}, f32[24576]{0:T(1024)}) fusion(f32[24576]{0:T(1024)} %add.67, f32[24576]{0:T(1024)} %collective-permute-done.4), kind=kLoop, calls=%fused_computation.4 | loop fusion | flops 73727 | bytes 294916 | tf_op jit(solution)/shard_map/reduce_sum | solution.py:499
  143.4 1.4 multiply_subtract_fusion
  144.7 1.3 collective-permute-done.5
  146.0 1.4 maximum_select_fusion.2
  147.5 1.8 %collective-permute-start.6 = (f32[2,3072]{1,0:T(2,128)}, f32[2,3072]{1,0:T(2,128)}, u32[]{:S(2)}, u32[]{:S(2)}) collective-permute-start(f32[2,3072]{1,0:T(2,128)} %maximum_select_fusion.2), channel_id=1, source_target_pairs={{0,2},{1,3},{2,0},{3,1},{4,6},{5,7},{6,4},{7,5},{8,10},{9,11},{10,... | collective-permute-start | bytes 73736 | tf_op jit(solution)/shard_map/ppermute | solution.py:320
  149.2 2.4 %collective-permute-done.6 = f32[2,3072]{1,0:T(2,128)} collective-permute-done((f32[2,3072]{1,0:T(2,128)}, f32[2,3072]{1,0:T(2,128)}, u32[]{:S(2)}, u32[]{:S(2)}) %collective-permute-start.6) | collective-permute-done | bytes 24608 | tf_op jit(solution)/shard_map/ppermute | solution.py:320
  151.6 1.5 maximum_select_fusion.1
  153.1 1.8 %collective-permute-start.7 = (f32[4,3072]{1,0:T(4,128)}, f32[4,3072]{1,0:T(4,128)}, u32[]{:S(2)}, u32[]{:S(2)}) collective-permute-start(f32[4,3072]{1,0:T(4,128)} %maximum_select_fusion.1), channel_id=1, source_target_pairs={{0,4},{1,5},{2,6},{3,7},{4,0},{5,1},{6,2},{7,3},{8,12},{9,13},{10,... | collective-permute-start | bytes 147464 | tf_op jit(solution)/shard_map/ppermute | solution.py:320
  154.9 1.9 %copy-done.3 = f32[1024,768]{1,0:T(8,128)S(1)} copy-done((f32[1024,768]{1,0:T(8,128)S(1)}, f32[1024,768]{1,0:T(8,128)}, u32[]{:S(2)}) %copy-start.3) | copy-done | bytes 3145752
  157.7 1.4 copy-done.6
  159.1 1.4 copy-done.7
  160.5 1.4 copy-done.8
  162.9 6.3 %shard_map.263 = bf16[1024,768]{1,0:T(8,128)(2,1)} custom-call(s32[2]{0:T(128)S(1)} %copy-done.10, f32[1024,768]{1,0:T(8,128)S(1)} %copy-done.3, bf16[1024,768]{1,0:T(8,128)(2,1)S(1)} %copy-done.6, bf16[1024,768]{1,0:T(8,128)(2,1)S(1)} %copy-done.7, bf16[1024,768]{1,0:T(8,128)(2,1)S(1)} %copy-done.8, bf16[1024,128]{1,0:T(8,128)(2,1)S(1)} %copy-done.9, ...), custom_call_target="tpu_custom_call" | custom-call | tf_op jit(solution)/shard_map/pallas_call | solution.py:476
  (68 shorter events, 16.9 us)
Async XLA Ops:
  0.6 8.7 %copy-start.12 = (bf16[768]{0:T(1024)(128)(2,1)S(1)}, bf16[768]{0:T(1024)(128)(2,1)}, u32[]{:S(2)}) copy-start(bf16[768]{0:T(1024)(128)(2,1)} %param.35) | copy-start | bytes 4612
  0.6 9.2 %copy-start.13 = (bf16[768]{0:T(1024)(128)(2,1)S(1)}, bf16[768]{0:T(1024)(128)(2,1)}, u32[]{:S(2)}) copy-start(bf16[768]{0:T(1024)(128)(2,1)} %param.38) | copy-start | bytes 4612
  0.7 9.8 %copy-start.14 = (bf16[768]{0:T(1024)(128)(2,1)S(1)}, bf16[768]{0:T(1024)(128)(2,1)}, u32[]{:S(2)}) copy-start(bf16[768]{0:T(1024)(128)(2,1)} %param.40) | copy-start | bytes 4612
  0.7 10.4 %copy-start.15 = (bf16[768]{0:T(1024)(128)(2,1)S(1)}, bf16[768]{0:T(1024)(128)(2,1)}, u32[]{:S(2)}) copy-start(bf16[768]{0:T(1024)(128)(2,1)} %param.41) | copy-start | bytes 4612
  0.7 11.0 %copy-start.16 = (bf16[768]{0:T(1024)(128)(2,1)S(1)}, bf16[768]{0:T(1024)(128)(2,1)}, u32[]{:S(2)}) copy-start(bf16[768]{0:T(1024)(128)(2,1)} %param.42) | copy-start | bytes 4612
  0.7 11.6 %copy-start.11 = (bf16[3072]{0:T(1024)(128)(2,1)S(1)}, bf16[3072]{0:T(1024)(128)(2,1)}, u32[]{:S(2)}) copy-start(bf16[3072]{0:T(1024)(128)(2,1)} %param.44) | copy-start | bytes 18436
  0.7 12.2 %copy-start.17 = (bf16[768]{0:T(1024)(128)(2,1)S(1)}, bf16[768]{0:T(1024)(128)(2,1)}, u32[]{:S(2)}) copy-start(bf16[768]{0:T(1024)(128)(2,1)} %param.46) | copy-start | bytes 4612
  0.7 12.7 %copy-start.18 = (bf16[768]{0:T(1024)(128)(2,1)S(1)}, bf16[768]{0:T(1024)(128)(2,1)}, u32[]{:S(2)}) copy-start(bf16[768]{0:T(1024)(128)(2,1)} %param.47) | copy-start | bytes 4612
  0.7 13.3 %copy-start.19 = (bf16[768]{0:T(1024)(128)(2,1)S(1)}, bf16[768]{0:T(1024)(128)(2,1)}, u32[]{:S(2)}) copy-start(bf16[768]{0:T(1024)(128)(2,1)} %param.48) | copy-start | bytes 4612
  17.0 0.7 copy-start.4
  108.4 46.5 %copy-start.2 = (bf16[768,768]{1,0:T(8,128)(2,1)S(1)}, bf16[768,768]{1,0:T(8,128)(2,1)}, u32[]{:S(2)}) copy-start(bf16[768,768]{1,0:T(8,128)(2,1)} %wv.1) | copy-start | bytes 3538948
  109.6 45.3 %copy-start = (bf16[768,768]{1,0:T(8,128)(2,1)S(1)}, bf16[768,768]{1,0:T(8,128)(2,1)}, u32[]{:S(2)}) copy-start(bf16[768,768]{1,0:T(8,128)(2,1)} %wq.1) | copy-start | bytes 3538948
  109.6 45.3 %copy-start.1 = (bf16[768,768]{1,0:T(8,128)(2,1)S(1)}, bf16[768,768]{1,0:T(8,128)(2,1)}, u32[]{:S(2)}) copy-start(bf16[768,768]{1,0:T(8,128)(2,1)} %wk.1) | copy-start | bytes 3538948
  109.6 45.3 %copy-start.10 = (s32[2]{0:T(128)S(1)}, s32[2]{0:T(128)}, u32[]{:S(2)}) copy-start(s32[2]{0:T(128)} %fusion.2.start_ref) | copy-start | bytes 28
  116.1 1.6 collective-permute-start
  118.6 6.0 %collective-permute-start.1 = (f32[24576]{0:T(1024)S(1)}, f32[24576]{0:T(1024)S(1)}, u32[]{:S(2)}, u32[]{:S(2)}) collective-permute-start(f32[24576]{0:T(1024)S(1)} %add.64), channel_id=1, source_target_pairs={{0,2},{1,3},{2,0},{3,1},{4,6},{5,7},{6,4},{7,5},{8,10},{9,11},{10,... | collective-permute-start | bytes 294920 | tf_op jit(solution)/shard_map/ppermute | solution.py:320
  124.6 4.7 %collective-permute-start.2 = (f32[24576]{0:T(1024)S(1)}, f32[24576]{0:T(1024)S(1)}, u32[]{:S(2)}, u32[]{:S(2)}) collective-permute-start(f32[24576]{0:T(1024)S(1)} %add.65), channel_id=1, source_target_pairs={{0,4},{1,5},{2,6},{3,7},{4,0},{5,1},{6,2},{7,3},{8,12},{9,13},{10,... | collective-permute-start | bytes 294920 | tf_op jit(solution)/shard_map/ppermute | solution.py:320
  129.3 4.7 %collective-permute-start.3 = (f32[24576]{0:T(1024)S(1)}, f32[24576]{0:T(1024)S(1)}, u32[]{:S(2)}, u32[]{:S(2)}) collective-permute-start(f32[24576]{0:T(1024)S(1)} %add.66), channel_id=1, source_target_pairs={{0,8},{8,0},{16,24},{24,16},{1,9},{9,1},{17,25},{25,17},{2,10},{10... | collective-permute-start | bytes 294920 | tf_op jit(solution)/shard_map/ppermute | solution.py:320
  134.6 5.8 %collective-permute-start.4 = (f32[24576]{0:T(1024)}, f32[24576]{0:T(1024)}, u32[]{:S(2)}, u32[]{:S(2)}) collective-permute-start(f32[24576]{0:T(1024)} %add.67), channel_id=1, source_target_pairs={{0,16},{8,24},{16,0},{24,8},{1,17},{9,25},{17,1},{25,9},{2,18},{10... | collective-permute-start | bytes 294920 | tf_op jit(solution)/shard_map/ppermute | solution.py:320
  144.7 1.3 collective-permute-start.5
  147.5 4.1 %collective-permute-start.6 = (f32[2,3072]{1,0:T(2,128)}, f32[2,3072]{1,0:T(2,128)}, u32[]{:S(2)}, u32[]{:S(2)}) collective-permute-start(f32[2,3072]{1,0:T(2,128)} %maximum_select_fusion.2), channel_id=1, source_target_pairs={{0,2},{1,3},{2,0},{3,1},{4,6},{5,7},{6,4},{7,5},{8,10},{9,11},{10,... | collective-permute-start | bytes 73736 | tf_op jit(solution)/shard_map/ppermute | solution.py:320
  153.1 16.1 %collective-permute-start.7 = (f32[4,3072]{1,0:T(4,128)}, f32[4,3072]{1,0:T(4,128)}, u32[]{:S(2)}, u32[]{:S(2)}) collective-permute-start(f32[4,3072]{1,0:T(4,128)} %maximum_select_fusion.1), channel_id=1, source_target_pairs={{0,4},{1,5},{2,6},{3,7},{4,0},{5,1},{6,2},{7,3},{8,12},{9,13},{10,... | collective-permute-start | bytes 147464 | tf_op jit(solution)/shard_map/ppermute | solution.py:320
  154.9 1.9 %copy-start.3 = (f32[1024,768]{1,0:T(8,128)S(1)}, f32[1024,768]{1,0:T(8,128)}, u32[]{:S(2)}) copy-start(f32[1024,768]{1,0:T(8,128)} %get-tuple-element.62.dfirst) | copy-start | bytes 9437188
  156.8 0.9 copy-start.5
  157.7 1.4 copy-start.6
  159.1 1.4 copy-start.7
  160.5 1.4 copy-start.8
  161.9 0.9 copy-start.9

commit v2 on v1

v2 whole, which is shorter than its diff:
```python
import functools

import jax
import jax.numpy as jnp
from jax import lax
from jax.experimental import pallas as pl
from jax.experimental.pallas import tpu as pltpu
from jax.sharding import PartitionSpec as P

HEADS = 12
RANK = 8
BIG = 256
HEAD_DIM = 64
LANES = 128
GROUP = 3
LOG2E = 1.4426950408889634

norm_eps = 1e-05
adapter_scale = 2.0
beta_one = 0.9
beta_two = 0.999
adam_eps = 1e-08
decay_rate = 0.01
rate_ratio = 16.0

bf16 = jnp.bfloat16
f32 = jnp.float32


def dot(left, right, ca=1, cb=0):
    return lax.dot_general(left, right, (((ca,), (cb,)), ((), ())), preferred_element_type=f32)


def line(vector):
    return vector.astype(f32).reshape(1, -1)


def unpack_factors(fac_ref, dcat, uq, uv):
    width = dcat.shape[0]
    per = width * RANK // LANES
    group = LANES // RANK
    lane = lax.broadcasted_iota(jnp.int32, (width, LANES), 1)
    sub = lax.broadcasted_iota(jnp.int32, (width, LANES), 0)
    keep = (lane // RANK) == (sub % group)
    spread = []
    for which in range(2):
        flat = fac_ref[which * per : (which + 1) * per, :].astype(bf16).astype(f32)
        wide = jnp.broadcast_to(flat[:, None, :], (per, group, LANES)).reshape(width, LANES)
        wide = jnp.where(keep, wide, 0.0)
        for hop in (8, 16, 32, 64):
            wide = wide + pltpu.roll(wide, hop, 1)
        spread.append(wide)
    dcat[...] = jnp.where(lane < HEAD_DIM, *spread).astype(bf16)
    tiles = width // LANES
    none = jnp.zeros((HEAD_DIM, width), bf16)
    for which, ref in enumerate((uq, uv)):
        base = 2 * per + which * per
        block = jnp.concatenate(
            [fac_ref[pl.ds(base + j, RANK, stride=tiles), :] for j in range(tiles)], axis=1
        )
        block = (block * adapter_scale).astype(bf16)
        half = jnp.concatenate([block] * (HEAD_DIM // RANK), axis=0)
        ref[...] = jnp.concatenate([half, none] if which == 0 else [none, half], axis=0)


def pack_grads(grad_ref, gd, gq, gv):
    width = gd.shape[1]
    per = width * RANK // LANES
    group = LANES // RANK
    tiles = width // LANES
    lane = lax.broadcasted_iota(jnp.int32, (width, LANES), 1)
    sub = lax.broadcasted_iota(jnp.int32, (width, LANES), 0)
    keep = (lane // RANK) == (sub % group)
    turned = jnp.concatenate(
        [gd[:, j * LANES : (j + 1) * LANES].T for j in range(tiles)], axis=0
    )
    other = pltpu.roll(turned, HEAD_DIM, 1)
    for which, (first, second) in enumerate(((turned, other), (other, turned))):
        full = jnp.where(lane < HEAD_DIM, first, second)
        picked = jnp.where(keep, full, 0.0).reshape(per, group, LANES)
        grad_ref[which * per : (which + 1) * per, :] = jnp.sum(picked, axis=1)
    for which, block in enumerate((gq, gv)):
        base = 2 * per + which * per
        for j in range(tiles):
            grad_ref[pl.ds(base + j, RANK, stride=tiles), :] = block[:, j * LANES : (j + 1) * LANES]


def rotate_rows(src, shift, emit):
    groups, _, width = src.shape
    coarse, fine = shift // 8, shift % 8
    back = lax.rem(8 - fine, 8)
    keep = lax.broadcasted_iota(jnp.int32, (8, width), 0) < 8 - fine
    spun = [
        pltpu.roll(src[lax.rem(coarse + i, groups)], back, 0) for i in range(groups + 1)
    ]
    moved = [jnp.where(keep, spun[i], spun[i + 1]) for i in range(groups)]
    for i in range(0, groups, 2):
        emit(i * 8, jnp.concatenate([moved[i], moved[i + 1]], axis=0))


def norm_rows(z):
    mean = jnp.mean(z, axis=-1, keepdims=True)
    centered = z - mean
    spread = jnp.mean(centered * centered, axis=-1, keepdims=True)
    root = lax.rsqrt(spread + norm_eps)
    return centered * root, root


def norm_rows_back(c, n, root):
    return root * (
        c - jnp.mean(c, axis=-1, keepdims=True) - n * jnp.mean(c * n, axis=-1, keepdims=True)
    )


def main_kernel(
    seg_ref,
    fac_ref,
    first_ref,
    second_ref,
    tok_ref,
    cot_ref,
    wq_hbm,
    wk_hbm,
    wv_hbm,
    wo_hbm,
    wu_hbm,
    wd_hbm,
    bq,
    bv,
    bo,
    g1,
    b1,
    bu,
    bd,
    g2,
    b2,
    start_ref,
    dcat,
    out_ref,
    dfirst_ref,
    dq_ref,
    dk_ref,
    dv_ref,
    dl_ref,
    grad_ref,
    wq,
    wk,
    wv,
    wo,
    wu,
    wd,
    sems,
    spin,
    xr,
    cr,
    qs,
    ks,
    vs,
    lora,
    probs,
    att,
    zs,
    n1,
    r1,
    hb,
    act,
    gp,
    uq,
    uv,
    gd_sum,
    gu_sum,
    inv,
):
    pid = pl.program_id(0)
    rows, width = tok_ref.shape
    pairs = width // LANES
    copies = [
        pltpu.make_async_copy(src, dst, sems.at[i])
        for i, (src, dst) in enumerate(
            ((wq_hbm, wq), (wk_hbm, wk), (wv_hbm, wv), (wo_hbm, wo), (wu_hbm, wu), (wd_hbm, wd))
        )
    ]

    @pl.when(pid == 0)
    def _():
        for copy in copies:
            copy.start()

    def arrive(*which):
        @pl.when(pid == 0)
        def _():
            for i in which:
                copies[i].wait()

    @pl.when(pid == 0)
    def _():
        unpack_factors(fac_ref, dcat, uq, uv)

    seg = jnp.broadcast_to(seg_ref[pl.ds(pid, 1), :], (LANES, rows))
    slot = lax.broadcasted_iota(jnp.int32, (LANES, rows), 0) % HEAD_DIM
    ones = jnp.ones((8, rows), bf16)
    seg_lo = dot(ones, jnp.where(seg < slot, 1.0, 0.0).astype(bf16), 1, 1)[:1]
    seg_hi = dot(ones, jnp.where(seg <= slot, 1.0, 0.0).astype(bf16), 1, 1)[:1]
    low_lane = lax.broadcasted_iota(jnp.int32, (1, LANES), 1) < HEAD_DIM
    start = jnp.sum(jnp.where(low_lane & (seg_hi - seg_lo == BIG), seg_lo, 0.0)).astype(jnp.int32)
    start_ref[pid] = start
    seg_lo = seg_lo.astype(jnp.int32)
    seg_hi = seg_hi.astype(jnp.int32)

    def put(dst):
        def emit(at, block):
            dst[pl.ds(at, 16), :] = block.astype(dst.dtype)

        return emit

    spin[...] = tok_ref[...].astype(f32).reshape(spin.shape)
    rotate_rows(spin, start, put(xr))
    spin[...] = cot_ref[...].astype(f32).reshape(spin.shape)
    rotate_rows(spin, start, put(cr))

    lora[...] = dot(xr[...], dcat[...]).astype(bf16)
    narrow = lax.broadcasted_iota(jnp.int32, (rows, LANES), 1) % HEAD_DIM < RANK
    lora_once = jnp.where(narrow, lora[...], jnp.zeros((rows, LANES), bf16))
    arrive(0, 1, 2)
    query = dot(xr[...], wq[...]) + dot(lora_once, uq[...]) + line(bq[...])
    qs[...] = (query * (HEAD_DIM**-0.5 * LOG2E)).astype(bf16)
    ks[...] = dot(xr[...], wk[...]).astype(bf16)
    value = dot(xr[...], wv[...]) + dot(lora_once, uv[...]) + line(bv[...])
    vs[...] = value.astype(bf16)

    row = lax.broadcasted_iota(jnp.int32, (BIG, LANES), 0) + (BIG + start)
    row = jnp.where(row >= rows, row - rows, row)
    lane = lax.broadcasted_iota(jnp.int32, (BIG, LANES), 1)
    inside = (row >= seg_lo) & (row < seg_hi)
    own = jnp.where(inside, 1.0, 0.0)
    used = (lane % HEAD_DIM) < 8
    own_q = own.astype(bf16)
    other_k = jnp.where(used & jnp.logical_not(inside), -1e30, 0.0).astype(bf16)
    low = lane < HEAD_DIM
    high = jnp.logical_not(low)
    none = jnp.zeros((BIG, LANES), bf16)
    ones_pair = jnp.ones((BIG, LANES), bf16)

    def heads_of(group):
        units = []
        for k in range(GROUP):
            pair = group * GROUP + k
            at = pl.ds(pl.multiple_of(pair * LANES, LANES), LANES)
            for block in range(2):
                for half in range(2):
                    units.append((pair, block, pl.ds(block * BIG, BIG), at, half))
        return units

    def pipeline(units, first, second, third, finish):
        count = len(units)
        begun, middle, ended = {}, {}, {}

        def close(k):
            ended[k] = third(units[k], middle.pop(k))
            if k % 2:
                finish(units[k], ended.pop(k - 1), ended.pop(k))

        for k in range(min(2, count)):
            begun[k] = first(units[k])
        for k in range(count):
            if k + 2 < count:
                begun[k + 2] = first(units[k + 2])
            middle[k] = second(units[k], begun.pop(k))
            if k:
                close(k - 1)
        close(count - 1)

    def group_forward(group, carry):
        def scores(unit):
            _, block, span, at, half = unit
            mine = low if half == 0 else high
            if block == 0:
                return dot(qs[span, at], jnp.where(mine, ks[span, at], none), 1, 1)
            query = jnp.where(mine, qs[span, at], own_q)
            return dot(query, jnp.where(mine, ks[span, at], other_k), 1, 1)

        def soften(unit, s):
            pair, block, _, _, half = unit
            e = jnp.exp2(s - jnp.max(s, axis=-1, keepdims=True))
            low_e = e.astype(bf16)
            probs[2 * pair + half, block] = low_e
            return low_e, jnp.sum(e, axis=-1, keepdims=True)

        def mix(unit, held):
            _, _, span, at, _ = unit
            return dot(held[0], vs[span, at]), held[1]

        def finish(unit, one, two):
            _, _, span, at, _ = unit
            scale = 1.0 / jnp.where(low, one[1], two[1])
            inv[span, at] = scale
            att[span, at] = (jnp.where(low, one[0], two[0]) * scale).astype(bf16)

        pipeline(heads_of(group), scores, soften, mix, finish)
        return carry

    lax.fori_loop(0, pairs // GROUP, group_forward, 0)

    arrive(3)
    zs[...] = dot(att[...], wo[...])
    step = 64

    def first_norm(i, carry):
        at = pl.ds(pl.multiple_of(i * step, step), step)
        z = xr[at, :].astype(f32) + zs[at, :] + line(bo[...])
        n, root = norm_rows(z)
        n1[at, :] = n
        r1[at, :] = root
        hb[at, :] = (n * line(g1[...]) + line(b1[...])).astype(bf16)
        return carry

    lax.fori_loop(0, rows // step, first_norm, 0)

    arrive(4)
    chunk = width
    count = act.shape[1] // chunk

    def up(c, carry):
        at = pl.ds(pl.multiple_of(c * chunk, chunk), chunk)
        u = dot(hb[...], wu[:, at]) + line(bu[at])
        half_cdf = 0.5 + 0.5 * lax.erf(u * (0.5**0.5))
        act[:, at] = (u * half_cdf).astype(bf16)
        bell = jnp.exp(u * u * -0.5) * 0.3989422804014327
        gp[:, at] = (half_cdf + u * bell).astype(bf16)
        return carry

    lax.fori_loop(0, count, up, 0)
    arrive(5)

    def down(c, carry):
        at = pl.ds(pl.multiple_of(c * BIG, BIG), BIG)
        zs[:, at] = dot(act[...], wd[:, at])
        return carry

    lax.fori_loop(0, width // BIG, down, 0)

    def second_norm(i, carry):
        at = pl.ds(pl.multiple_of(i * step, step), step)
        hidden = n1[at, :] * line(g1[...]) + line(b1[...])
        z = hidden + zs[at, :] + line(bd[...])
        n, root = norm_rows(z)
        gain = line(g2[...])
        result = n * gain + line(b2[...])
        spin[pl.ds(i * (step // 8), step // 8)] = result.reshape(step // 8, 8, width)
        d = norm_rows_back(cr[at, :].astype(f32) * gain, n, root)
        zs[at, :] = d
        hb[at, :] = d.astype(bf16)
        return carry

    lax.fori_loop(0, rows // step, second_norm, 0)
    rotate_rows(spin, rows - start, put(out_ref))

    def up_back(c, carry):
        at = pl.ds(pl.multiple_of(c * chunk, chunk), chunk)
        t = dot(hb[...], wd[at, :], 1, 1)
        act[:, at] = (t * gp[:, at].astype(f32)).astype(bf16)
        return carry

    lax.fori_loop(0, count, up_back, 0)

    def down_back(c, carry):
        at = pl.ds(pl.multiple_of(c * BIG, BIG), BIG)
        zs[:, at] = zs[:, at] + dot(act[...], wu[at, :], 1, 1)
        return carry

    lax.fori_loop(0, width // BIG, down_back, 0)

    def first_norm_back(i, carry):
        at = pl.ds(pl.multiple_of(i * step, step), step)
        d = norm_rows_back(zs[at, :] * line(g1[...]), n1[at, :], r1[at, :])
        dfirst_ref[at, :] = d
        hb[at, :] = d.astype(bf16)
        return carry

    lax.fori_loop(0, rows // step, first_norm_back, 0)
    cr[...] = dot(hb[...], wo[...], 1, 1).astype(bf16)

    def group_back(group, carry):
        ready = {}

        def slopes(unit):
            _, block, span, at, half = unit
            if half == 0:
                scaled = cr[span, at].astype(f32) * inv[span, at]
                minus = pltpu.roll(-scaled * att[span, at].astype(f32), HEAD_DIM, 1)
                scaled = scaled.astype(bf16)
                ready[id(at), block] = scaled, minus.astype(bf16), scaled.T, qs[span, at].T
            scaled, minus = ready[id(at), block][:2]
            mine = low if half == 0 else high
            left = jnp.where(mine, scaled, minus)
            return dot(left, jnp.where(mine, vs[span, at], ones_pair), 1, 1)

        def weigh(unit, d):
            pair, block, _, _, half = unit
            e = probs[2 * pair + half, block]
            return e * d.astype(bf16), e

        def grads_of(unit, held):
            _, block, span, at, half = unit
            ds, e = held
            _, _, scaled_t, query_t = ready[id(at), block]
            lines = slice(half * HEAD_DIM, (half + 1) * HEAD_DIM)
            return dot(ds, ks[span, at]), dot(query_t[lines], ds), dot(scaled_t[lines], e)

        def finish(unit, one, two):
            _, block, span, at, _ = unit
            ready.pop((id(at), block))
            dq_ref[span, at] = (jnp.where(low, one[0], two[0]) * HEAD_DIM**-0.5).astype(bf16)
            dk = jnp.concatenate([one[1], two[1]], axis=0) * (1.0 / LOG2E)
            dk_ref[span, at] = dk.astype(bf16).T
            dv_ref[span, at] = jnp.concatenate([one[2], two[2]], axis=0).astype(bf16).T

        pipeline(heads_of(group), slopes, weigh, grads_of, finish)
        return carry

    lax.fori_loop(0, pairs // GROUP, group_back, 0)

    dl = (dot(dq_ref[...], uq[...], 1, 1) + dot(dv_ref[...], uv[...], 1, 1)).astype(bf16)
    dl_ref[...] = jnp.where(narrow, dl, jnp.zeros((rows, LANES), bf16))
    gd = dot(dl, xr[...], 0, 0)
    gq = adapter_scale * dot(lora[...], dq_ref[...], 0, 0)[:RANK]
    gv = adapter_scale * dot(lora[...], dv_ref[...], 0, 0)[HEAD_DIM : HEAD_DIM + RANK]

    @pl.when(pid == 0)
    def _():
        gd_sum[...] = gd
        gu_sum[0] = gq
        gu_sum[1] = gv

    @pl.when(pid > 0)
    def _():
        gd_sum[...] += gd
        gu_sum[0] += gq
        gu_sum[1] += gv

    @pl.when(pid == pl.num_programs(0) - 1)
    def _():
        pack_grads(grad_ref, gd_sum[...], gu_sum[0], gu_sum[1])
        base, more = fac_ref.shape[0], first_ref.shape[0]
        grad_ref[base : base + more, :] = first_ref[...]
        grad_ref[base + more :, :] = second_ref[...]


def token_kernel(pack, start_ref, dfirst, dq, dk, dv, dl, wq, wk, wv, dcat, *rest):
    out_ref, spin = rest[-2:]
    total = dot(dq[...], wq[...], 1, 1) + dot(dk[...], wk[...], 1, 1)
    total = total + dot(dv[...], wv[...], 1, 1) + dot(dl[...], dcat[...], 1, 1)
    spin[...] = (dfirst[...] + total).reshape(spin.shape)

    def emit(at, block):
        out_ref[pl.ds(at, 16), :] = block.astype(bf16)

    rotate_rows(spin, dfirst.shape[0] - start_ref[pack], emit)


def optimizer_kernel(steps_ref, rate_ref, place_ref, total, params, moments, grad_out, new_params, first_out, second_out):
    shares = total.shape[0]
    norm_sq = jnp.sum(jnp.sum(total[...] * total[...], axis=0), keepdims=True)
    clip = jnp.minimum(1.0, lax.rsqrt(norm_sq + 1e-06))
    place = place_ref[0]

    def power(base):
        return lax.fori_loop(0, steps_ref[0], lambda _, value: value * base, jnp.float32(1.0))

    shape = total.shape[1:]
    fix_one = jnp.full(shape, 1.0 - power(beta_one), f32)
    fix_two = jnp.full(shape, 1.0 - power(beta_two), f32)
    grad_out[...] = total[place]
    for j in range(shares):
        share = place ^ j
        clipped = total[share] * clip
        first = beta_one * moments[j, 0] + (1.0 - beta_one) * clipped
        second = beta_two * moments[j, 1] + (1.0 - beta_two) * clipped * clipped
        if j == 0:
            first_out[...] = first
            second_out[...] = second
        held = params[share]
        update = first / fix_one / (jnp.sqrt(second / fix_two) + adam_eps) + decay_rate * held
        rate = rate_ref[0] * jnp.where(share < shares // 2, 1.0, rate_ratio)
        new_params[share] = held - rate * update


def swap(x, axis, bit):
    n = lax.axis_size(axis)
    return lax.ppermute(x, axis, [(i, i ^ bit) for i in range(n)])


def bits_of(axis):
    n = lax.axis_size(axis)
    return [1 << k for k in range(n.bit_length() - 1)]


def shards(
    tokens,
    segment_ids,
    cotangent,
    query_frozen_weight,
    query_bias_vector,
    w_key,
    value_frozen_weight,
    value_bias_vector,
    w_out,
    b_out,
    norm1_gain,
    norm1_bias,
    w_up,
    b_up,
    w_down,
    b_down,
    norm2_gain,
    norm2_bias,
    factors,
    moment_first,
    moment_second,
    step_count,
    learn_rate,
):
    width = tokens.shape[1]
    packs, rows = segment_ids.shape
    ff = w_up.shape[1]
    flat_rows = factors.shape[0] // LANES
    flat = factors.reshape(flat_rows, LANES)
    shares = lax.axis_size("wide")
    own_rows = flat_rows // shares

    per_pack = pl.BlockSpec((rows, width), lambda i: (i, 0))
    whole = lambda shape: pl.BlockSpec(shape, lambda i: (0,) * len(shape))
    anywhere = pl.BlockSpec(memory_space=pl.ANY)
    scalars = pl.BlockSpec(memory_space=pltpu.SMEM)
    total_rows = packs * rows
    result = lambda shape, dtype: jax.ShapeDtypeStruct(shape, dtype)
    weights = (query_frozen_weight, w_key, value_frozen_weight, w_out, w_up, w_down)
    vectors = (
        query_bias_vector,
        value_bias_vector,
        b_out,
        norm1_gain,
        norm1_bias,
        b_up,
        b_down,
        norm2_gain,
        norm2_bias,
    )
    start, dcat, output, dfirst, dq, dk, dv, dl, grads = pl.pallas_call(
        main_kernel,
        out_shape=(
            result((packs,), jnp.int32),
            result((width, LANES), bf16),
            result((total_rows, width), bf16),
            result((total_rows, width), f32),
            result((total_rows, width), bf16),
            result((total_rows, width), bf16),
            result((total_rows, width), bf16),
            result((total_rows, LANES), bf16),
            result((flat_rows + 2 * own_rows, LANES), f32),
        ),
        grid_spec=pltpu.PrefetchScalarGridSpec(
            num_scalar_prefetch=0,
            grid=(packs,),
            in_specs=[whole((packs, rows)), whole((flat_rows, LANES))]
            + [whole((own_rows, LANES))] * 2
            + [per_pack] * 2
            + [anywhere] * 6
            + [whole(v.shape) for v in vectors],
            out_specs=[scalars, whole((width, LANES))]
            + [per_pack] * 5
            + [pl.BlockSpec((rows, LANES), lambda i: (i, 0)), whole((flat_rows + 2 * own_rows, LANES))],
            scratch_shapes=[pltpu.VMEM(w.shape, bf16) for w in weights]
            + [
                pltpu.SemaphoreType.DMA((6,)),
                pltpu.VMEM((rows // 8, 8, width), f32),
                pltpu.VMEM((rows, width), bf16),
                pltpu.VMEM((rows, width), bf16),
                pltpu.VMEM((rows, width), bf16),
                pltpu.VMEM((rows, width), bf16),
                pltpu.VMEM((rows, width), bf16),
                pltpu.VMEM((rows, LANES), bf16),
                pltpu.VMEM((HEADS, 2, BIG, BIG), bf16),
                pltpu.VMEM((rows, width), bf16),
                pltpu.VMEM((rows, width), f32),
                pltpu.VMEM((rows, width), f32),
                pltpu.VMEM((rows, 1), f32),
                pltpu.VMEM((rows, width), bf16),
                pltpu.VMEM((rows, ff), bf16),
                pltpu.VMEM((rows, ff), bf16),
                pltpu.VMEM((LANES, width), bf16),
                pltpu.VMEM((LANES, width), bf16),
                pltpu.VMEM((LANES, width), f32),
                pltpu.VMEM((2, RANK, width), f32),
                pltpu.VMEM((rows, width), f32),
            ],
        ),
        compiler_params=pltpu.CompilerParams(
            dimension_semantics=("arbitrary",), vmem_limit_bytes=60 * 2**20
        ),
    )(
        segment_ids,
        flat,
        moment_first.reshape(own_rows, LANES),
        moment_second.reshape(own_rows, LANES),
        tokens,
        cotangent,
        *weights,
        *vectors,
    )

    parts = 2
    cut = width // parts
    grad_tokens = None

    def piece(number, before, tie):
        pack, part = divmod(number, parts)
        rows_of = lambda w: pl.BlockSpec((rows, w), lambda i: (pack, 0))
        cut_spec = pl.BlockSpec((rows, cut), lambda i: (pack, part))
        weight_of = lambda w: pl.BlockSpec((cut, w), lambda i: (part, 0))
        held = [] if before is None else [before]
        tied, _ = lax.optimization_barrier((start, tie))
        return pl.pallas_call(
            functools.partial(token_kernel, pack),
            out_shape=result((total_rows, width), bf16),
            grid=(1,),
            in_specs=[scalars, cut_spec]
            + [rows_of(width)] * 3
            + [rows_of(LANES)]
            + [weight_of(width)] * 3
            + [weight_of(LANES)]
            + [anywhere] * len(held),
            out_specs=cut_spec,
            scratch_shapes=[pltpu.VMEM((rows // 8, 8, cut), f32)],
            input_output_aliases={10: 0} if held else {},
            compiler_params=pltpu.CompilerParams(vmem_limit_bytes=60 * 2**20),
            cost_estimate=pl.CostEstimate(
                flops=2 * rows * cut * (3 * width + LANES),
                bytes_accessed=3 * rows * width * 2 + 3 * cut * width * 2 + rows * cut * 6,
                transcendentals=0,
            ),
        )(tied, dfirst, dq, dk, dv, dl, *weights[:3], dcat, *held)

    stages = [("wide", bit) for bit in bits_of("wide")] + [("dp", bit) for bit in bits_of("dp")]
    pieces = packs * parts
    after = max(len(stages) - pieces, 0)
    done = 0
    held = grads
    for number, (axis, bit) in enumerate(stages):
        got = swap(held, axis, bit)
        if number >= after and done < pieces:
            grad_tokens = piece(done, grad_tokens, held)
            done += 1
            got, grad_tokens = lax.optimization_barrier((got, grad_tokens))
        if axis == "wide":
            held = jnp.concatenate(
                [held[:flat_rows] + got[:flat_rows], held[flat_rows:], got[flat_rows:]]
            )
        else:
            held = held + got
        if number == len(bits_of("wide")) - 1:
            moments = held[flat_rows:]
            held = held[:flat_rows]
    if not stages:
        moments, held = held[flat_rows:], held[:flat_rows]
    while done < pieces:
        grad_tokens = piece(done, grad_tokens, held)
        done += 1
    total = held

    own = result((own_rows, LANES), f32)
    vmem = pl.BlockSpec(memory_space=pltpu.VMEM)
    shaped = (shares, own_rows, LANES)
    grad_own, new_factors, new_first, new_second = pl.pallas_call(
        optimizer_kernel,
        out_shape=(own, result(shaped, f32), own, own),
        in_specs=[scalars] * 3 + [vmem] * 3,
        out_specs=[vmem] * 4,
    )(
        step_count,
        learn_rate,
        lax.axis_index("wide").astype(jnp.int32).reshape(1),
        total.reshape(shaped),
        factors.reshape(shaped),
        moments.reshape(shares, 2, own_rows, LANES),
    )
    return (
        output,
        grad_tokens,
        grad_own.reshape(-1),
        new_factors.reshape(-1),
        new_first.reshape(-1),
        new_second.reshape(-1),
    )


def solution(mesh):
    rows = P(("dp", "wide"), None)
    in_specs = (rows,) * 3 + (P(),) * 16 + (P("wide"), P("wide"), P(), P())
    out_specs = (rows, rows, P("wide"), P(), P("wide"), P("wide"))
    return jax.shard_map(shards, mesh=mesh, in_specs=in_specs, out_specs=out_specs, check_vma=False)
```

time: 172 us -> 108 us (0.63)
  local copies, waits for them, and re-layouts: 28.1 us -> 0.75 us
  waiting for transfers between devices: 15.2 us -> 0.86 us
  other arithmetic: 15.5 us -> 2.36 us
  starting transfers between devices: 13.5 us -> 9.31 us
  Pallas kernels: 95.6 us -> 92.1 us
    ppermute x8 -> x5, waiting for transfers between devices: 15.2 us -> 0.86 us  [swap(): return lax.ppermute(x, axis, [(i, i ^ bit) for i in range(n)])]
    unnamed x42 -> x0, local copies, waits for them, and re-layouts: 10.8 us -> none
    reshape x12 -> x0, local copies, waits for them, and re-layouts: 10.1 us -> none  [the longest x9 5.33 us: vec(): return v.reshape(1, -1)]
    reduce_sum x3 -> x0, other arithmetic: 5.2 us -> none  [the longest x1 2.19 us: shards(): norm_sq = jnp.sum(total * total)]
    ppermute x8 -> x5, starting transfers between devices: 13.5 us -> 9.31 us  [swap(): return lax.ppermute(x, axis, [(i, i ^ bit) for i in range(n)])]
    scatter x4 -> x0, local copies, waits for them, and re-layouts: 3.79 us -> none  [the longest x1 2.37 us: shards(): dcat.at[:, RANK:2 * RANK]]
    pallas_call x2 -> x6, Pallas kernels: 95.6 us -> 92.1 us  [the longest x1 71 us: shards(): pl.pallas_call(main_kernel, out_shape=(result((packs,), jnp.int32), resul...]
    select_n x3 -> x0, other arithmetic: 2.9 us -> none  [the longest x2 2.9 us: gather_shares(): jnp.where(first, jnp.concatenate([held, other]), jnp.concatenate([other,...]
  transfers between devices with their start and end apart: 8 -> 5, of which waited for: 7 -> 2; matrix products, arithmetic and copies ran while one was open for 0% -> 1% of each run, Pallas kernels for 4% -> 18%
where the time goes in v2:
time: 108 us; the launch traced here: 107 us
  Pallas kernels  92.1 us (85%)
  starting transfers between devices  9.31 us (9%)
  other arithmetic  2.36 us (2%)
  between operations  1.99 us (2%)
    pallas_call x1, Pallas kernels, shards(): pl.pallas_call(main_kernel, out_shape=(result((packs,), jnp.int32), resul...  71 us
    pallas_call x4, Pallas kernels, piece(): pl.pallas_call(functools.partial(token_kernel, pack), out_shape=result((t...  19 us
    ppermute x5, starting transfers between devices, swap(): return lax.ppermute(x, axis, [(i, i ^ bit) for i in range(n)])  9.31 us
  transfers between devices with their start and end apart: 5, of which 2 were waited for; matrix products, arithmetic and copies ran while one was open for 1% of the time, Pallas kernels for 18%

profile of v2, /device:TPU:0, one launch (start us, length us, event | category | flops | bytes accessed | tf_op | source)
XLA Modules:
  0.0 107.3 jit_solution(5905161945398969546)
XLA Ops:
  0.6 71.0 %shard_map.262 = (s32[2]{0:T(128)}, bf16[768,128]{1,0:T(8,128)(2,1)}, bf16[1024,768]{1,0:T(8,128)(2,1)}, f32[1024,768]{1,0:T(8,128)}, bf16[1024,768]{1,0:T(8,128...) custom-call(s32[2,512]{1,0:T(2,128)} %seg_ref.1, ...), custom_call_target="tpu_custom_call" | custom-call | tf_op jit(solution)/shard_map/pallas_call | solution.py:549
  71.7 0.5 collective-permute-start
  72.2 0.7 slice.30
  73.0 0.4 collective-permute-done
  73.4 0.9 slice_add_fusion
  74.3 2.9 %collective-permute-start.1 = (f32[288,128]{1,0:T(8,128)S(1)}, f32[288,128]{1,0:T(8,128)S(1)}, u32[]{:S(2)}, u32[]{:S(2)}) collective-permute-start(f32[288,128]{1,0:T(8,128)S(1)} %pad_maximum_fusion.2), channel_id=1, source_target_pairs={{0,2},{1,3},{2,0},{3,1},{4,6},{5,7},{6,4},{7,5},{8,10},{9,11},{10,... | collective-permute-start | bytes 442376 | tf_op jit(solution)/shard_map/ppermute | solution.py:490
  77.2 4.8 %shard_map.263.rest_0_ = bf16[1024,768]{1,0:T(8,128)(2,1)} custom-call(s32[2]{0:T(128)} %get-tuple-element.48.start_ref, f32[1024,768]{1,0:T(8,128)} %get-tuple-element.35.dfirst, bf16[1024,768]{1,0:T(8,128)(2,1)} %get-tuple-element.36.dq, bf16[1024,768]{1,0:T(8,128)(2,1)} %get-tuple-element.37.dk, bf16[1024,768]{1,0:T(8,128)(2,1)} %get-tuple-element.38.dv, ...), custom_call_target="tpu_custom_call" | custom-call | flops 956301312 | bytes 5308416 | tf_op jit(solution)/shard_map/pallas_call | solution.py:623
  82.0 0.0 collective-permute-done.1
  82.1 1.6 %collective-permute-start.2 = (f32[384,128]{1,0:T(8,128)S(1)}, f32[384,128]{1,0:T(8,128)S(1)}, u32[]{:S(2)}, u32[]{:S(2)}) collective-permute-start(f32[384,128]{1,0:T(8,128)S(1)} %pad_maximum_fusion), channel_id=1, source_target_pairs={{0,4},{1,5},{2,6},{3,7},{4,0},{5,1},{6,2},{7,3},{8,12},{9,13},{10,... | collective-permute-start | bytes 589832 | tf_op jit(solution)/shard_map/ppermute | solution.py:490
  83.6 4.8 %shard_map.264.rest_0_ = bf16[1024,768]{1,0:T(8,128)(2,1)} custom-call(s32[2]{0:T(128)} %get-tuple-element.48.start_ref, f32[1024,768]{1,0:T(8,128)} %get-tuple-element.35.dfirst, bf16[1024,768]{1,0:T(8,128)(2,1)} %get-tuple-element.36.dq, bf16[1024,768]{1,0:T(8,128)(2,1)} %get-tuple-element.37.dk, ...), custom_call_target="tpu_custom_call", output_to_operand_aliasing={{}: (10, {})} | custom-call | flops 956301312 | bytes 5308416 | tf_op jit(solution)/shard_map/pallas_call | solution.py:623
  88.4 0.4 collective-permute-done.2
  88.8 1.6 %collective-permute-start.3 = (f32[192,128]{1,0:T(8,128)S(1)}, f32[192,128]{1,0:T(8,128)S(1)}, u32[]{:S(2)}, u32[]{:S(2)}) collective-permute-start(f32[192,128]{1,0:T(8,128)S(1)} %get-tuple-element.57), channel_id=1, source_target_pairs={{0,8},{8,0},{16,24},{24,16},{1,9},{9,1},{17,25},{25,17},{2,10},{10... | collective-permute-start | bytes 294920 | tf_op jit(solution)/shard_map/ppermute | solution.py:490
  91.7 4.8 %shard_map.265.rest_0_ = bf16[1024,768]{1,0:T(8,128)(2,1)} custom-call(s32[2]{0:T(128)} %get-tuple-element.48.start_ref, f32[1024,768]{1,0:T(8,128)} %get-tuple-element.35.dfirst, bf16[1024,768]{1,0:T(8,128)(2,1)} %get-tuple-element.36.dq, bf16[1024,768]{1,0:T(8,128)(2,1)} %get-tuple-element.37.dk, ...), custom_call_target="tpu_custom_call", output_to_operand_aliasing={{}: (10, {})} | custom-call | flops 956301312 | bytes 5308416 | tf_op jit(solution)/shard_map/pallas_call | solution.py:623
  96.5 0.0 collective-permute-done.3
  96.5 2.7 %collective-permute-start.4 = (f32[192,128]{1,0:T(8,128)S(1)}, f32[192,128]{1,0:T(8,128)S(1)}, u32[]{:S(2)}, u32[]{:S(2)}) collective-permute-start(f32[192,128]{1,0:T(8,128)S(1)} %add.18), channel_id=1, source_target_pairs={{0,16},{8,24},{16,0},{24,8},{1,17},{9,25},{17,1},{25,9},{2,18},{10... | collective-permute-start | bytes 294920 | tf_op jit(solution)/shard_map/ppermute | solution.py:490
  99.2 0.7 pad_maximum_fusion.1
  99.9 4.8 %shard_map.266 = bf16[1024,768]{1,0:T(8,128)(2,1)} custom-call(s32[2]{0:T(128)} %get-tuple-element.48.start_ref, f32[1024,768]{1,0:T(8,128)} %get-tuple-element.35.dfirst, bf16[1024,768]{1,0:T(8,128)(2,1)} %get-tuple-element.36.dq, bf16[1024,768]{1,0:T(8,128)(2,1)} %get-tuple-element.37.dk, ...), custom_call_target="tpu_custom_call", output_to_operand_aliasing={{}: (10, {})} | custom-call | flops 956301312 | bytes 5308416 | tf_op jit(solution)/shard_map/pallas_call | solution.py:623
  104.7 0.0 collective-permute-done.4
  104.7 0.6 add.19
  105.3 2.0 %shard_map.267 = (f32[24,128]{1,0:T(8,128)}, f32[8,24,128]{2,1,0:T(8,128)}, f32[24,128]{1,0:T(8,128)}, f32[24,128]{1,0:T(8,128)}) custom-call(s32[1]{0:T(128)S(6)} %copy.35.steps_ref, f32[1]{0:T(128)S(6)} %copy.36.rate_ref, s32[1]{0:T(128)} %bitcast.3.place_ref, f32[8,24,128]{2,1,0:T(8,128)} %bitcast.14, f32[8,24,128]{2,1,0:T(8,128)} %bitcast.13, ...), custom_call_target="tpu_custom_call" | custom-call | tf_op jit(solution)/shard_map/pallas_call | solution.py:674
  (7 shorter events, 0.1 us)
Async XLA Ops:
  71.7 1.7 %collective-permute-start = (f32[240,128]{1,0:T(8,128)}, f32[240,128]{1,0:T(8,128)S(1)}, u32[]{:S(2)}, u32[]{:S(2)}) collective-permute-start(f32[240,128]{1,0:T(8,128)} %get-tuple-element.32), channel_id=1, source_target_pairs={{0,1},{1,0},{2,3},{3,2},{4,5},{5,4},{6,7},{7,6},{8,9},{9,8},{10,11... | collective-permute-start | bytes 368648 | tf_op jit(solution)/shard_map/ppermute | solution.py:490
  74.3 7.7 %collective-permute-start.1 = (f32[288,128]{1,0:T(8,128)S(1)}, f32[288,128]{1,0:T(8,128)S(1)}, u32[]{:S(2)}, u32[]{:S(2)}) collective-permute-start(f32[288,128]{1,0:T(8,128)S(1)} %pad_maximum_fusion.2), channel_id=1, source_target_pairs={{0,2},{1,3},{2,0},{3,1},{4,6},{5,7},{6,4},{7,5},{8,10},{9,11},{10,... | collective-permute-start | bytes 442376 | tf_op jit(solution)/shard_map/ppermute | solution.py:490
  82.1 6.7 %collective-permute-start.2 = (f32[384,128]{1,0:T(8,128)S(1)}, f32[384,128]{1,0:T(8,128)S(1)}, u32[]{:S(2)}, u32[]{:S(2)}) collective-permute-start(f32[384,128]{1,0:T(8,128)S(1)} %pad_maximum_fusion), channel_id=1, source_target_pairs={{0,4},{1,5},{2,6},{3,7},{4,0},{5,1},{6,2},{7,3},{8,12},{9,13},{10,... | collective-permute-start | bytes 589832 | tf_op jit(solution)/shard_map/ppermute | solution.py:490
  88.8 7.7 %collective-permute-start.3 = (f32[192,128]{1,0:T(8,128)S(1)}, f32[192,128]{1,0:T(8,128)S(1)}, u32[]{:S(2)}, u32[]{:S(2)}) collective-permute-start(f32[192,128]{1,0:T(8,128)S(1)} %get-tuple-element.57), channel_id=1, source_target_pairs={{0,8},{8,0},{16,24},{24,16},{1,9},{9,1},{17,25},{25,17},{2,10},{10... | collective-permute-start | bytes 294920 | tf_op jit(solution)/shard_map/ppermute | solution.py:490
  96.5 8.2 %collective-permute-start.4 = (f32[192,128]{1,0:T(8,128)S(1)}, f32[192,128]{1,0:T(8,128)S(1)}, u32[]{:S(2)}, u32[]{:S(2)}) collective-permute-start(f32[192,128]{1,0:T(8,128)S(1)} %add.18), channel_id=1, source_target_pairs={{0,16},{8,24},{16,0},{24,8},{1,17},{9,25},{17,1},{25,9},{2,18},{10... | collective-permute-start | bytes 294920 | tf_op jit(solution)/shard_map/ppermute | solution.py:490

commit v3 on v2

v3 whole, which is shorter than its diff:
```python
import functools

import jax
import jax.numpy as jnp
from jax import lax
from jax.experimental import pallas as pl
from jax.experimental.pallas import tpu as pltpu
from jax.sharding import PartitionSpec as P

HEADS = 12
RANK = 8
BIG = 256
HEAD_DIM = 64
LANES = 128
GROUP = 3
STEP = 256
CHUNK = 512
VMEM_LIMIT = 63 * 2**20
LOG2E = 1.4426950408889634
LOG2_ROOT = 1.3257480647361592

norm_eps = 1e-05
adapter_scale = 2.0
beta_one = 0.9
beta_two = 0.999
adam_eps = 1e-08
decay_rate = 0.01
rate_ratio = 16.0

bf16 = jnp.bfloat16
f32 = jnp.float32


def dot(left, right, ca=1, cb=0):
    return lax.dot_general(left, right, (((ca,), (cb,)), ((), ())), preferred_element_type=f32)


def line(vector):
    return vector.astype(f32).reshape(1, -1)


def unpack_factors(fac_ref, dcat, uq, uv):
    width = dcat.shape[0]
    per = width * RANK // LANES
    group = LANES // RANK
    lane = lax.broadcasted_iota(jnp.int32, (width, LANES), 1)
    sub = lax.broadcasted_iota(jnp.int32, (width, LANES), 0)
    keep = (lane // RANK) == (sub % group)
    spread = []
    for which in range(2):
        flat = fac_ref[which * per : (which + 1) * per, :].astype(bf16).astype(f32)
        wide = jnp.broadcast_to(flat[:, None, :], (per, group, LANES)).reshape(width, LANES)
        wide = jnp.where(keep, wide, 0.0)
        for hop in (8, 16, 32, 64):
            wide = wide + pltpu.roll(wide, hop, 1)
        spread.append(wide)
    dcat[...] = jnp.where(lane < HEAD_DIM, *spread).astype(bf16)
    tiles = width // LANES
    none = jnp.zeros((HEAD_DIM, width), bf16)
    for which, ref in enumerate((uq, uv)):
        base = 2 * per + which * per
        block = jnp.concatenate(
            [fac_ref[pl.ds(base + j, RANK, stride=tiles), :] for j in range(tiles)], axis=1
        )
        block = (block * adapter_scale).astype(bf16)
        half = jnp.concatenate([block] * (HEAD_DIM // RANK), axis=0)
        ref[...] = jnp.concatenate([half, none] if which == 0 else [none, half], axis=0)


def pack_grads(grad_ref, gd, gq, gv):
    width = gd.shape[1]
    per = width * RANK // LANES
    group = LANES // RANK
    tiles = width // LANES
    lane = lax.broadcasted_iota(jnp.int32, (width, LANES), 1)
    sub = lax.broadcasted_iota(jnp.int32, (width, LANES), 0)
    keep = (lane // RANK) == (sub % group)
    turned = jnp.concatenate(
        [gd[:, j * LANES : (j + 1) * LANES].T for j in range(tiles)], axis=0
    )
    other = pltpu.roll(turned, HEAD_DIM, 1)
    for which, (first, second) in enumerate(((turned, other), (other, turned))):
        full = jnp.where(lane < HEAD_DIM, first, second)
        picked = jnp.where(keep, full, 0.0).reshape(per, group, LANES)
        grad_ref[which * per : (which + 1) * per, :] = jnp.sum(picked, axis=1)
    for which, block in enumerate((gq, gv)):
        base = 2 * per + which * per
        for j in range(tiles):
            grad_ref[pl.ds(base + j, RANK, stride=tiles), :] = block[:, j * LANES : (j + 1) * LANES]


def rotate_rows(src, base, count, shift, emit):
    width = src.shape[1]
    groups = count // 8
    coarse, fine = shift // 8, shift % 8
    back = lax.rem(8 - fine, 8)
    keep = lax.broadcasted_iota(jnp.int32, (8, width), 0) < 8 - fine

    def turned(i):
        at = pl.multiple_of(base + 8 * lax.rem(coarse + i, groups), 8)
        return pltpu.roll(src[pl.ds(at, 8), :], back, 0)

    spun = [turned(i) for i in range(groups + 1)]
    moved = [jnp.where(keep, spun[i], spun[i + 1]) for i in range(groups)]
    for i in range(0, groups, 2):
        emit(i * 8, jnp.concatenate([moved[i], moved[i + 1]], axis=0))


def norm_rows(z):
    mean = jnp.mean(z, axis=-1, keepdims=True)
    centered = z - mean
    spread = jnp.mean(centered * centered, axis=-1, keepdims=True)
    root = lax.rsqrt(spread + norm_eps)
    return centered * root, root


def norm_rows_back(c, n, root):
    return root * (
        c - jnp.mean(c, axis=-1, keepdims=True) - n * jnp.mean(c * n, axis=-1, keepdims=True)
    )


def main_kernel(
    side_ref,
    seg_ref,
    fac_ref,
    first_ref,
    second_ref,
    bq,
    bv,
    bo,
    g1,
    b1,
    bu,
    bd,
    g2,
    b2,
    tok_hbm,
    cot_hbm,
    wq_hbm,
    wk_hbm,
    wv_hbm,
    wo_hbm,
    wu_hbm,
    wd_hbm,
    keep_ref,
    send_ref,
    out_hbm,
    tgrad_hbm,
    wq,
    wk,
    wv,
    wo,
    wu,
    wd,
    sems,
    spin,
    xr,
    cr,
    qs,
    ks,
    vs,
    lora,
    probs,
    att,
    inv,
    zs,
    n1,
    r1,
    hb,
    act,
    gp,
    dcat,
    uq,
    uv,
    own_q,
    other_k,
    flat,
):
    packs, rows = seg_ref.shape
    total_rows, width = xr.shape
    pairs = width // LANES
    copies = []
    for src, dst in (
        (tok_hbm, xr),
        (wq_hbm, wq),
        (wk_hbm, wk),
        (wv_hbm, wv),
        (cot_hbm, cr),
        (wo_hbm, wo),
        (wu_hbm, wu),
        (wd_hbm, wd),
    ):
        copies.append(pltpu.make_async_copy(src, dst, sems.at[len(copies)]))
        copies[-1].start()

    def arrive(*which):
        for i in which:
            copies[i].wait()

    unpack_factors(fac_ref, dcat, uq, uv)

    lane = lax.broadcasted_iota(jnp.int32, (BIG, LANES), 1)
    low = lane < HEAD_DIM
    high = jnp.logical_not(low)
    used = (lane % HEAD_DIM) < 8
    none = jnp.zeros((BIG, LANES), bf16)
    ones_pair = jnp.ones((BIG, LANES), bf16)
    low_lane = lax.broadcasted_iota(jnp.int32, (1, LANES), 1) < HEAD_DIM
    slot = lax.broadcasted_iota(jnp.int32, (LANES, rows), 0) % HEAD_DIM
    ones = jnp.ones((8, rows), bf16)
    starts = []
    for pack in range(packs):
        seg = jnp.broadcast_to(seg_ref[pack : pack + 1, :], (LANES, rows))
        seg_lo = dot(ones, jnp.where(seg < slot, 1.0, 0.0).astype(bf16), 1, 1)[:1]
        seg_hi = dot(ones, jnp.where(seg <= slot, 1.0, 0.0).astype(bf16), 1, 1)[:1]
        large = low_lane & (seg_hi - seg_lo == BIG)
        start = jnp.sum(jnp.where(large, seg_lo, 0.0)).astype(jnp.int32)
        starts.append(start)
        row = lax.broadcasted_iota(jnp.int32, (BIG, LANES), 0) + (BIG + start)
        row = jnp.where(row >= rows, row - rows, row)
        inside = (row >= seg_lo.astype(jnp.int32)) & (row < seg_hi.astype(jnp.int32))
        own_q[pack] = jnp.where(inside, 1.0, 0.0).astype(bf16)
        other_k[pack] = jnp.where(used & jnp.logical_not(inside), -1e30, 0.0).astype(bf16)

    def put(dst, base):
        def emit(at, block):
            dst[pl.ds(base + at, 16), :] = block.astype(dst.dtype)

        return emit

    def turn(ref):
        for pack in range(packs):
            spin[...] = ref[pack * rows : (pack + 1) * rows, :].astype(f32)
            rotate_rows(spin, 0, rows, starts[pack], put(ref, pack * rows))

    arrive(0)
    turn(xr)

    lora[...] = dot(xr[...], dcat[...]).astype(bf16)
    narrow = lax.broadcasted_iota(jnp.int32, (total_rows, LANES), 1) % HEAD_DIM < RANK
    lora_once = jnp.where(narrow, lora[...], jnp.zeros((total_rows, LANES), bf16))
    arrive(1, 2, 3)
    for c in range(width // BIG):
        at = slice(c * BIG, (c + 1) * BIG)
        query = dot(xr[...], wq[:, at]) + dot(lora_once, uq[:, at]) + line(bq[at])
        qs[:, at] = (query * (HEAD_DIM**-0.5 * LOG2E)).astype(bf16)
        ks[:, at] = dot(xr[...], wk[:, at]).astype(bf16)
        value = dot(xr[...], wv[:, at]) + dot(lora_once, uv[:, at]) + line(bv[at])
        vs[:, at] = value.astype(bf16)

    def heads_of(turn_no):
        per = pairs // GROUP
        pack, group = turn_no // per, turn_no % per
        units = []
        for k in range(GROUP):
            pair = group * GROUP + k
            at = pl.ds(pl.multiple_of(pair * LANES, LANES), LANES)
            for block in range(2):
                span = pl.ds(pl.multiple_of(pack * rows + block * BIG, BIG), BIG)
                for half in range(2):
                    place = (pack * HEADS + 2 * pair + half) * 2 + block
                    units.append((pack, place, block, span, at, half))
        return units

    def pipeline(units, first, second, third, finish):
        count = len(units)
        begun, middle, ended = {}, {}, {}

        def close(k):
            ended[k] = third(units[k], middle.pop(k))
            if k % 2:
                finish(units[k], ended.pop(k - 1), ended.pop(k))

        for k in range(min(2, count)):
            begun[k] = first(units[k])
        for k in range(count):
            if k + 2 < count:
                begun[k + 2] = first(units[k + 2])
            middle[k] = second(units[k], begun.pop(k))
            if k:
                close(k - 1)
        close(count - 1)

    def group_forward(turn_no, carry):
        def scores(unit):
            pack, _, block, span, at, half = unit
            mine = low if half == 0 else high
            if block == 0:
                return dot(qs[span, at], jnp.where(mine, ks[span, at], none), 1, 1)
            query = jnp.where(mine, qs[span, at], own_q[pack])
            return dot(query, jnp.where(mine, ks[span, at], other_k[pack]), 1, 1)

        def soften(unit, s):
            e = jnp.exp2(s - jnp.max(s, axis=-1, keepdims=True))
            low_e = e.astype(bf16)
            probs[unit[1]] = low_e
            return low_e, jnp.sum(e, axis=-1, keepdims=True)

        def mix(unit, held):
            _, _, _, span, at, _ = unit
            return dot(held[0], vs[span, at]), held[1]

        def finish(unit, one, two):
            _, _, _, span, at, _ = unit
            scale = 1.0 / jnp.where(low, one[1], two[1])
            inv[span, at] = scale
            att[span, at] = (jnp.where(low, one[0], two[0]) * scale).astype(bf16)

        pipeline(heads_of(turn_no), scores, soften, mix, finish)
        return carry

    turns = packs * pairs // GROUP
    lax.fori_loop(0, turns, group_forward, 0)
    arrive(4)
    turn(cr)

    arrive(5)
    zs[...] = dot(att[...], wo[...])
    step = STEP

    def steps(body):
        def run(i, carry):
            body(pl.ds(pl.multiple_of(i * step, step), step))
            return carry

        lax.fori_loop(0, total_rows // step, run, 0)

    def first_norm(at):
        z = xr[at, :].astype(f32) + zs[at, :] + line(bo[...])
        n, root = norm_rows(z)
        n1[at, :] = n
        r1[at, :] = root
        hb[at, :] = (n * line(g1[...]) + line(b1[...])).astype(bf16)

    steps(first_norm)

    arrive(6)
    chunk = CHUNK
    count = act.shape[1] // chunk

    def up(c, carry):
        at = pl.ds(pl.multiple_of(c * chunk, chunk), chunk)
        u = dot(hb[...], wu[:, at]) + line(bu[at])
        z = u * (0.5**0.5)
        half_cdf = 0.5 + 0.5 * lax.erf(z)
        act[:, at] = (u * half_cdf).astype(bf16)
        bell = jnp.exp2(z * z * -LOG2E - LOG2_ROOT)
        gp[:, at] = (half_cdf + u * bell).astype(bf16)
        return carry

    lax.fori_loop(0, count, up, 0)
    arrive(7)

    def down(c, carry):
        at = pl.ds(pl.multiple_of(c * BIG, BIG), BIG)
        zs[:, at] = dot(act[...], wd[:, at])
        return carry

    lax.fori_loop(0, width // BIG, down, 0)
    results = []
    for pack in range(packs):
        for part in range(rows // step):
            at = slice(pack * rows + part * step, pack * rows + (part + 1) * step)
            hidden = n1[at, :] * line(g1[...]) + line(b1[...])
            z = hidden + zs[at, :] + line(bd[...])
            n, root = norm_rows(z)
            gain = line(g2[...])
            spin[part * step : (part + 1) * step, :] = n * gain + line(b2[...])
            d = norm_rows_back(cr[at, :].astype(f32) * gain, n, root)
            zs[at, :] = d
            hb[at, :] = d.astype(bf16)
        span = pl.ds(pack * rows, rows)
        rotate_rows(spin, 0, rows, rows - starts[pack], put(cr, pack * rows))
        results.append(
            pltpu.make_async_copy(cr.at[span, :], out_hbm.at[span, :], sems.at[8 + pack])
        )
        results[-1].start()

    def up_back(c, carry):
        at = pl.ds(pl.multiple_of(c * chunk, chunk), chunk)
        t = dot(hb[...], wd[at, :], 1, 1)
        act[:, at] = (t * gp[:, at].astype(f32)).astype(bf16)
        return carry

    lax.fori_loop(0, count, up_back, 0)

    def down_back(c, carry):
        at = pl.ds(pl.multiple_of(c * BIG, BIG), BIG)
        zs[:, at] = zs[:, at] + dot(act[...], wu[at, :], 1, 1)
        return carry

    lax.fori_loop(0, width // BIG, down_back, 0)

    def first_norm_back(at):
        d = norm_rows_back(zs[at, :] * line(g1[...]), n1[at, :], r1[at, :])
        zs[at, :] = d
        hb[at, :] = d.astype(bf16)

    steps(first_norm_back)
    for copy in results:
        copy.wait()
    cr[...] = dot(hb[...], wo[...], 1, 1).astype(bf16)

    def group_back(turn_no, carry):
        ready = {}

        def slopes(unit):
            _, _, block, span, at, half = unit
            if half == 0:
                scaled = cr[span, at].astype(f32) * inv[span, at]
                minus = pltpu.roll(-scaled * att[span, at].astype(f32), HEAD_DIM, 1)
                scaled = scaled.astype(bf16)
                ready[id(at), block] = scaled, minus.astype(bf16), scaled.T, qs[span, at].T
            scaled, minus = ready[id(at), block][:2]
            mine = low if half == 0 else high
            left = jnp.where(mine, scaled, minus)
            return dot(left, jnp.where(mine, vs[span, at], ones_pair), 1, 1)

        def weigh(unit, d):
            e = probs[unit[1]]
            return e * d.astype(bf16), e

        def grads_of(unit, held):
            _, _, block, span, at, half = unit
            ds, e = held
            _, _, scaled_t, query_t = ready[id(at), block]
            lines = slice(half * HEAD_DIM, (half + 1) * HEAD_DIM)
            return dot(ds, ks[span, at]), dot(query_t[lines], ds), dot(scaled_t[lines], e)

        def finish(unit, one, two):
            _, _, block, span, at, _ = unit
            ready.pop((id(at), block))
            qs[span, at] = (jnp.where(low, one[0], two[0]) * HEAD_DIM**-0.5).astype(bf16)
            dk = jnp.concatenate([one[1], two[1]], axis=0) * (1.0 / LOG2E)
            ks[span, at] = dk.astype(bf16).T
            vs[span, at] = jnp.concatenate([one[2], two[2]], axis=0).astype(bf16).T

        pipeline(heads_of(turn_no), slopes, weigh, grads_of, finish)
        return carry

    lax.fori_loop(0, turns, group_back, 0)

    dl = (dot(qs[...], uq[...], 1, 1) + dot(vs[...], uv[...], 1, 1)).astype(bf16)
    gd = dot(dl, xr[...], 0, 0)
    gq = adapter_scale * dot(lora[...], qs[...], 0, 0)[:RANK]
    gv = adapter_scale * dot(lora[...], vs[...], 0, 0)[HEAD_DIM : HEAD_DIM + RANK]
    pack_grads(flat, gd, gq, gv)
    half_rows = flat.shape[0] // 2
    side = side_ref[0]
    kept = flat[pl.ds(pl.multiple_of(side * half_rows, 8), half_rows), :]
    send_ref[...] = flat[pl.ds(pl.multiple_of((1 - side) * half_rows, 8), half_rows), :]
    more = first_ref.shape[0]
    keep_ref[:half_rows, :] = kept
    keep_ref[half_rows : half_rows + more, :] = first_ref[...]
    keep_ref[half_rows + more :, :] = second_ref[...]

    dl_once = jnp.where(narrow, dl, jnp.zeros((total_rows, LANES), bf16))
    for c in range(width // BIG):
        at = slice(c * BIG, (c + 1) * BIG)
        term = dot(qs[...], wq[at, :], 1, 1) + dot(ks[...], wk[at, :], 1, 1)
        term = term + dot(vs[...], wv[at, :], 1, 1) + dot(dl_once, dcat[at, :], 1, 1)
        zs[:, at] = zs[:, at] + term
    results = []
    for pack in range(packs):
        span = pl.ds(pack * rows, rows)
        rotate_rows(zs, pack * rows, rows, rows - starts[pack], put(hb, pack * rows))
        results.append(
            pltpu.make_async_copy(hb.at[span, :], tgrad_hbm.at[span, :], sems.at[8 + pack])
        )
        results[-1].start()
    for copy in results:
        copy.wait()


def optimizer_kernel(places, *refs):
    steps_ref, rate_ref, place_ref, held, other, params = refs[:6]
    grad_out, new_params, first_out, second_out, total = refs[6:]
    shares, own_rows = params.shape[:2]
    half = shares // 2
    place = place_ref[0]
    side = place & 1
    total[side] = held[:half]
    total[1 - side] = other[:half]
    norm_sq = jnp.sum(jnp.sum(total[...] * total[...], axis=(0, 1)), keepdims=True)
    clip = jnp.minimum(1.0, lax.rsqrt(norm_sq + 1e-06))

    def power(base):
        return lax.fori_loop(0, steps_ref[0], lambda _, value: value * base, jnp.float32(1.0))

    shape = (own_rows, LANES)
    fix_one = jnp.full(shape, 1.0 - power(beta_one), f32)
    fix_two = jnp.full(shape, 1.0 - power(beta_two), f32)
    grad_out[...] = total[place // half, place % half]
    for j, mask in enumerate(places + [mask ^ 1 for mask in places]):
        source, at = (held, half + 2 * j) if j < half else (other, half + 2 * (j - half))
        share = place ^ mask
        clipped = total[share // half, share % half] * clip
        first = beta_one * source[at] + (1.0 - beta_one) * clipped
        second = beta_two * source[at + 1] + (1.0 - beta_two) * clipped * clipped
        if j == 0:
            first_out[...] = first
            second_out[...] = second
        before = params[share]
        update = first / fix_one / (jnp.sqrt(second / fix_two) + adam_eps) + decay_rate * before
        rate = rate_ref[0] * jnp.where(share < half, 1.0, rate_ratio)
        new_params[share] = before - rate * update


def swap(x, axis, bit):
    n = lax.axis_size(axis)
    return lax.ppermute(x, axis, [(i, i ^ bit) for i in range(n)])


def bits_of(axis):
    n = lax.axis_size(axis)
    return [1 << k for k in range(n.bit_length() - 1)]


def shards(
    tokens,
    segment_ids,
    cotangent,
    query_frozen_weight,
    query_bias_vector,
    w_key,
    value_frozen_weight,
    value_bias_vector,
    w_out,
    b_out,
    norm1_gain,
    norm1_bias,
    w_up,
    b_up,
    w_down,
    b_down,
    norm2_gain,
    norm2_bias,
    factors,
    moment_first,
    moment_second,
    step_count,
    learn_rate,
):
    width = tokens.shape[1]
    packs, rows = segment_ids.shape
    ff = w_up.shape[1]
    total_rows = packs * rows
    flat_rows = factors.shape[0] // LANES
    shares = lax.axis_size("wide")
    own_rows = flat_rows // shares
    half_rows = flat_rows // 2
    place = lax.axis_index("wide").astype(jnp.int32)

    whole = pl.BlockSpec(memory_space=pltpu.VMEM)
    anywhere = pl.BlockSpec(memory_space=pl.ANY)
    scalars = pl.BlockSpec(memory_space=pltpu.SMEM)
    result = lambda shape, dtype: jax.ShapeDtypeStruct(shape, dtype)
    weights = (query_frozen_weight, w_key, value_frozen_weight, w_out, w_up, w_down)
    vectors = (
        query_bias_vector,
        value_bias_vector,
        b_out,
        norm1_gain,
        norm1_bias,
        b_up,
        b_down,
        norm2_gain,
        norm2_bias,
    )
    tall = lambda dtype: pltpu.VMEM((total_rows, width), dtype)
    kept, sent, output, grad_tokens = pl.pallas_call(
        main_kernel,
        out_shape=(
            result((half_rows + 2 * own_rows, LANES), f32),
            result((half_rows, LANES), f32),
            result((total_rows, width), bf16),
            result((total_rows, width), bf16),
        ),
        in_specs=[scalars] + [whole] * (4 + len(vectors)) + [anywhere] * 8,
        out_specs=[whole, whole, anywhere, anywhere],
        scratch_shapes=[pltpu.VMEM(w.shape, bf16) for w in weights]
        + [
            pltpu.SemaphoreType.DMA((8 + packs,)),
            pltpu.VMEM((rows, width), f32),
            tall(bf16),
            tall(bf16),
            tall(bf16),
            tall(bf16),
            tall(bf16),
            pltpu.VMEM((total_rows, LANES), bf16),
            pltpu.VMEM((packs * HEADS * 2, BIG, BIG), bf16),
            tall(bf16),
            tall(f32),
            tall(f32),
            tall(f32),
            pltpu.VMEM((total_rows, 1), f32),
            tall(bf16),
            pltpu.VMEM((total_rows, ff), bf16),
            pltpu.VMEM((total_rows, ff), bf16),
            pltpu.VMEM((width, LANES), bf16),
            pltpu.VMEM((LANES, width), bf16),
            pltpu.VMEM((LANES, width), bf16),
            pltpu.VMEM((packs, BIG, LANES), bf16),
            pltpu.VMEM((packs, BIG, LANES), bf16),
            pltpu.VMEM((flat_rows, LANES), f32),
        ],
        compiler_params=pltpu.CompilerParams(vmem_limit_bytes=VMEM_LIMIT),
    )(
        (place & 1).reshape(1),
        segment_ids,
        factors.reshape(flat_rows, LANES),
        moment_first.reshape(own_rows, LANES),
        moment_second.reshape(own_rows, LANES),
        *vectors,
        tokens,
        cotangent,
        *weights,
    )

    held = kept.at[:half_rows].add(swap(sent, "wide", 1))
    bits = bits_of("wide")[1:]
    places = [0]
    while bits:
        now, bits = bits[:2], bits[2:]
        masks = [now[0]] if len(now) == 1 else [now[0], now[1], now[0] | now[1]]
        got = [swap(held, "wide", mask) for mask in masks]
        if len(got) == 1:
            total = held[:half_rows] + got[0][:half_rows]
        else:
            total = (held[:half_rows] + got[0][:half_rows]) + (
                got[1][:half_rows] + got[2][:half_rows]
            )
        places = places + [old ^ mask for mask in masks for old in places]
        if bits:
            held = jnp.concatenate([total] + [part[half_rows:] for part in [held] + got])
        else:
            moments = [part[half_rows:] for part in [held] + got]
    for bit in bits_of("dp"):
        total = total + swap(total, "dp", bit)
    held = jnp.concatenate([total] + moments)
    other = swap(held, "wide", 1)

    own = result((own_rows, LANES), f32)
    shaped = (shares, own_rows, LANES)
    grad_own, new_factors, new_first, new_second = pl.pallas_call(
        functools.partial(optimizer_kernel, places),
        out_shape=(own, result(shaped, f32), own, own),
        in_specs=[scalars] * 3 + [whole] * 3,
        out_specs=[whole] * 4,
        scratch_shapes=[pltpu.VMEM((2, shares // 2, own_rows, LANES), f32)],
    )(
        step_count,
        learn_rate,
        place.reshape(1),
        held.reshape(-1, own_rows, LANES),
        other.reshape(-1, own_rows, LANES),
        factors.reshape(shaped),
    )
    return (
        output,
        grad_tokens,
        grad_own.reshape(-1),
        new_factors.reshape(-1),
        new_first.reshape(-1),
        new_second.reshape(-1),
    )


def solution(mesh):
    rows = P(("dp", "wide"), None)
    in_specs = (rows,) * 3 + (P(),) * 16 + (P("wide"), P("wide"), P(), P())
    out_specs = (rows, rows, P("wide"), P(), P("wide"), P("wide"))
    return jax.shard_map(shards, mesh=mesh, in_specs=in_specs, out_specs=out_specs, check_vma=False)
```

time: 108 us -> 95.7 us (0.89)
  Pallas kernels: 92.1 us -> 71.3 us
  waiting for transfers between devices: 0.86 us -> 10.2 us
  other arithmetic: 2.36 us -> 0.84 us
    pallas_call x6 -> x2, Pallas kernels: 92.1 us -> 71.3 us  [the longest x1 69.3 us: shards(): pl.pallas_call(main_kernel, out_shape=(result((half_rows + 2 * own_rows,...]
    ppermute x5 -> x7, waiting for transfers between devices: 0.86 us -> 10.2 us  [swap(): return lax.ppermute(x, axis, [(i, i ^ bit) for i in range(n)])]
    unnamed x0 -> x8, local copies, waits for them, and re-layouts: none -> 1.55 us
    ppermute x5 -> x7, starting transfers between devices: 9.31 us -> 9.57 us  [swap(): return lax.ppermute(x, axis, [(i, i ^ bit) for i in range(n)])]
  transfers between devices with their start and end apart: 5 -> 7, of which waited for: 2 -> 7; matrix products, arithmetic and copies ran while one was open for 1% -> 1% of each run, Pallas kernels for 18% -> 0%
where the time goes in v3:
time: 95.7 us; the launch traced here: 95.4 us
  Pallas kernels  71.3 us (75%)
  waiting for transfers between devices  10.2 us (11%)
  starting transfers between devices  9.57 us (10%)
  between operations  2.01 us (2%)
  local copies, waits for them, and re-layouts  1.56 us (2%)
    pallas_call x1, Pallas kernels, shards(): pl.pallas_call(main_kernel, out_shape=(result((half_rows + 2 * own_rows,...  69.3 us
    ppermute x7, waiting for transfers between devices, swap(): return lax.ppermute(x, axis, [(i, i ^ bit) for i in range(n)])  10.2 us
    ppermute x7, starting transfers between devices, swap(): return lax.ppermute(x, axis, [(i, i ^ bit) for i in range(n)])  9.57 us
    pallas_call x1, Pallas kernels, shards(): pl.pallas_call(functools.partial(optimizer_kernel, places), out_shape=(ow...  1.95 us
  transfers between devices with their start and end apart: 7, of which 7 were waited for; matrix products, arithmetic and copies ran while one was open for 1% of the time, Pallas kernels for 0%

profile of v3, /device:TPU:0, one launch (start us, length us, event | category | flops | bytes accessed | tf_op | source)
XLA Modules:
  0.0 95.4 jit_solution(12938847153027041556)
XLA Ops:
  0.6 69.3 %shard_map.262 = (f32[144,128]{1,0:T(8,128)}, f32[96,128]{1,0:T(8,128)}, bf16[1024,768]{1,0:T(8,128)(2,1)}, bf16[1024,768]{1,0:T(8,128)(2,1)}) custom-call(s32[1]{0:T(128)} %bitcast.side_ref, s32[2,512]{1,0:T(2,128)} %seg_ref.1, f32[192,128]{1,0:T(8,128)} %bitcast.12, f32[24,128]{1,0:T(8,128)} %bitcast.16, f32[24,128]{1,0:T(8,128)} %bitcast.17, ...), custom_call_target="tpu_custom_call" | custom-call | tf_op jit(solution)/shard_map/pallas_call | solution.py:572
  70.0 0.5 collective-permute-start
  70.5 0.9 copy.29
  71.4 0.2 collective-permute-done
  71.6 2.9 %collective-permute-start.1 = (f32[144,128]{1,0:T(8,128)S(1)}, f32[144,128]{1,0:T(8,128)S(1)}, u32[]{:S(2)}, u32[]{:S(2)}) collective-permute-start(f32[144,128]{1,0:T(8,128)S(1)} %fusion.1), channel_id=1, source_target_pairs={{0,2},{1,3},{2,0},{3,1},{4,6},{5,7},{6,4},{7,5},{8,10},{9,11},{10,... | collective-permute-start | bytes 221192 | tf_op jit(solution)/shard_map/ppermute | solution.py:512
  74.5 1.5 %collective-permute-start.2 = (f32[144,128]{1,0:T(8,128)S(1)}, f32[144,128]{1,0:T(8,128)S(1)}, u32[]{:S(2)}, u32[]{:S(2)}) collective-permute-start(f32[144,128]{1,0:T(8,128)S(1)} %fusion.1), channel_id=1, source_target_pairs={{0,4},{1,5},{2,6},{3,7},{4,0},{5,1},{6,2},{7,3},{8,12},{9,13},{10,... | collective-permute-start | bytes 221192 | tf_op jit(solution)/shard_map/ppermute | solution.py:512
  76.0 0.0 collective-permute-start.3
  76.1 1.1 %collective-permute-done.1 = f32[144,128]{1,0:T(8,128)S(1)} collective-permute-done((f32[144,128]{1,0:T(8,128)S(1)}, f32[144,128]{1,0:T(8,128)S(1)}, u32[]{:S(2)}, u32[]{:S(2)}) %collective-permute-start.1) | collective-permute-done | bytes 73760 | tf_op jit(solution)/shard_map/ppermute | solution.py:512
  77.1 1.8 %collective-permute-done.2 = f32[144,128]{1,0:T(8,128)S(1)} collective-permute-done((f32[144,128]{1,0:T(8,128)S(1)}, f32[144,128]{1,0:T(8,128)S(1)}, u32[]{:S(2)}, u32[]{:S(2)}) %collective-permute-start.2) | collective-permute-done | bytes 73760 | tf_op jit(solution)/shard_map/ppermute | solution.py:512
  78.9 2.4 %collective-permute-done.3 = f32[144,128]{1,0:T(8,128)S(1)} collective-permute-done((f32[144,128]{1,0:T(8,128)S(1)}, f32[144,128]{1,0:T(8,128)S(1)}, u32[]{:S(2)}, u32[]{:S(2)}) %collective-permute-start.3) | collective-permute-done | bytes 73760 | tf_op jit(solution)/shard_map/ppermute | solution.py:512
  81.3 0.8 fusion
  82.1 1.6 %collective-permute-start.4 = (f32[96,128]{1,0:T(8,128)S(1)}, f32[96,128]{1,0:T(8,128)S(1)}, u32[]{:S(2)}, u32[]{:S(2)}) collective-permute-start(f32[96,128]{1,0:T(8,128)S(1)} %fusion), channel_id=1, source_target_pairs={{0,8},{8,0},{16,24},{24,16},{1,9},{9,1},{17,25},{25,17},{2,10},{10... | collective-permute-start | bytes 147464 | tf_op jit(solution)/shard_map/ppermute | solution.py:512
  83.7 2.5 %collective-permute-done.4 = f32[96,128]{1,0:T(8,128)S(1)} collective-permute-done((f32[96,128]{1,0:T(8,128)S(1)}, f32[96,128]{1,0:T(8,128)S(1)}, u32[]{:S(2)}, u32[]{:S(2)}) %collective-permute-start.4) | collective-permute-done | bytes 49184 | tf_op jit(solution)/shard_map/ppermute | solution.py:512
  86.3 2.9 %collective-permute-start.5 = (f32[96,128]{1,0:T(8,128)S(1)}, f32[96,128]{1,0:T(8,128)S(1)}, u32[]{:S(2)}, u32[]{:S(2)}) collective-permute-start(f32[96,128]{1,0:T(8,128)S(1)} %add.26), channel_id=1, source_target_pairs={{0,16},{8,24},{16,0},{24,8},{1,17},{9,25},{17,1},{25,9},{2,18},{10... | collective-permute-start | bytes 147464 | tf_op jit(solution)/shard_map/ppermute | solution.py:512
  89.2 2.2 %collective-permute-done.5 = f32[96,128]{1,0:T(8,128)S(1)} collective-permute-done((f32[96,128]{1,0:T(8,128)S(1)}, f32[96,128]{1,0:T(8,128)S(1)}, u32[]{:S(2)}, u32[]{:S(2)}) %collective-permute-start.5) | collective-permute-done | bytes 49184 | tf_op jit(solution)/shard_map/ppermute | solution.py:512
  91.4 0.0 copy-start
  91.4 0.1 collective-permute-start.6
  92.8 0.1 collective-permute-done.6
  92.8 0.0 copy-start.1
  92.8 0.0 copy-done
  92.8 0.6 copy-done.1
  93.5 1.9 %shard_map.263 = (f32[24,128]{1,0:T(8,128)}, f32[8,24,128]{2,1,0:T(8,128)}, f32[24,128]{1,0:T(8,128)}, f32[24,128]{1,0:T(8,128)}) custom-call(s32[1]{0:T(128)S(6)} %copy.34.refs_0_, f32[1]{0:T(128)S(6)} %copy.35.refs_1_, s32[1]{0:T(128)} %bitcast.4.refs_2_, f32[12,24,128]{2,1,0:T(8,128)} %bitcast.14, f32[12,24,128]{2,1,0:T(8,128)} %bitcast.15, ...), custom_call_target="tpu_custom_call" | custom-call | tf_op jit(solution)/shard_map/pallas_call | solution.py:646
  (7 shorter events, 0.0 us)
Async XLA Ops:
  70.0 1.6 %collective-permute-start = (f32[96,128]{1,0:T(8,128)}, f32[96,128]{1,0:T(8,128)S(1)}, u32[]{:S(2)}, u32[]{:S(2)}) collective-permute-start(f32[96,128]{1,0:T(8,128)} %get-tuple-element.29), channel_id=1, source_target_pairs={{0,1},{1,0},{2,3},{3,2},{4,5},{5,4},{6,7},{7,6},{8,9},{9,8},{10,11... | collective-permute-start | bytes 147464 | tf_op jit(solution)/shard_map/ppermute | solution.py:512
  71.6 5.5 %collective-permute-start.1 = (f32[144,128]{1,0:T(8,128)S(1)}, f32[144,128]{1,0:T(8,128)S(1)}, u32[]{:S(2)}, u32[]{:S(2)}) collective-permute-start(f32[144,128]{1,0:T(8,128)S(1)} %fusion.1), channel_id=1, source_target_pairs={{0,2},{1,3},{2,0},{3,1},{4,6},{5,7},{6,4},{7,5},{8,10},{9,11},{10,... | collective-permute-start | bytes 221192 | tf_op jit(solution)/shard_map/ppermute | solution.py:512
  74.5 4.4 %collective-permute-start.2 = (f32[144,128]{1,0:T(8,128)S(1)}, f32[144,128]{1,0:T(8,128)S(1)}, u32[]{:S(2)}, u32[]{:S(2)}) collective-permute-start(f32[144,128]{1,0:T(8,128)S(1)} %fusion.1), channel_id=1, source_target_pairs={{0,4},{1,5},{2,6},{3,7},{4,0},{5,1},{6,2},{7,3},{8,12},{9,13},{10,... | collective-permute-start | bytes 221192 | tf_op jit(solution)/shard_map/ppermute | solution.py:512
  76.0 5.3 %collective-permute-start.3 = (f32[144,128]{1,0:T(8,128)S(1)}, f32[144,128]{1,0:T(8,128)S(1)}, u32[]{:S(2)}, u32[]{:S(2)}) collective-permute-start(f32[144,128]{1,0:T(8,128)S(1)} %fusion.1), channel_id=1, source_target_pairs={{0,6},{1,7},{2,4},{3,5},{4,2},{5,3},{6,0},{7,1},{8,14},{9,15},{10,... | collective-permute-start | bytes 221192 | tf_op jit(solution)/shard_map/ppermute | solution.py:512
  82.1 4.2 %collective-permute-start.4 = (f32[96,128]{1,0:T(8,128)S(1)}, f32[96,128]{1,0:T(8,128)S(1)}, u32[]{:S(2)}, u32[]{:S(2)}) collective-permute-start(f32[96,128]{1,0:T(8,128)S(1)} %fusion), channel_id=1, source_target_pairs={{0,8},{8,0},{16,24},{24,16},{1,9},{9,1},{17,25},{25,17},{2,10},{10... | collective-permute-start | bytes 147464 | tf_op jit(solution)/shard_map/ppermute | solution.py:512
  86.3 5.0 %collective-permute-start.5 = (f32[96,128]{1,0:T(8,128)S(1)}, f32[96,128]{1,0:T(8,128)S(1)}, u32[]{:S(2)}, u32[]{:S(2)}) collective-permute-start(f32[96,128]{1,0:T(8,128)S(1)} %add.26), channel_id=1, source_target_pairs={{0,16},{8,24},{16,0},{24,8},{1,17},{9,25},{17,1},{25,9},{2,18},{10... | collective-permute-start | bytes 147464 | tf_op jit(solution)/shard_map/ppermute | solution.py:512
  91.4 1.5 %copy-start = (f32[288,128]{1,0:T(8,128)}, f32[288,128]{1,0:T(8,128)S(1)}, u32[]{:S(2)}) copy-start(f32[288,128]{1,0:T(8,128)S(1)} %slice_dynamic-update-slice_fusion) | copy-start | bytes 442372
  91.4 1.4 %collective-permute-start.6 = (f32[288,128]{1,0:T(8,128)S(1)}, f32[288,128]{1,0:T(8,128)S(1)}, u32[]{:S(2)}, u32[]{:S(2)}) collective-permute-start(f32[288,128]{1,0:T(8,128)S(1)} %slice_dynamic-update-slice_fusion), channel_id=1, source_target_pairs={{0,1},{1,0},{2,3},{3,2},{4,5},{5,4},{6,7},{7,6},{8,9},{9,8},{10,11... | collective-permute-start | bytes 442376 | tf_op jit(solution)/shard_map/ppermute | solution.py:512
  92.8 0.7 copy-start.1

commit v4 on v3

--- a/solution.py
+++ b/solution.py
@@ -12,10 +12,10 @@
 BIG = 256
 HEAD_DIM = 64
 LANES = 128
-GROUP = 3
+GROUP = 6
 STEP = 256
-CHUNK = 512
-VMEM_LIMIT = 63 * 2**20
+CHUNK = 768
+VMEM_LIMIT = 50 * 2**20
 LOG2E = 1.4426950408889634
 LOG2_ROOT = 1.3257480647361592
 
@@ -146,10 +146,14 @@
     keep_ref,
     send_ref,
     out_hbm,
-    tgrad_hbm,
+    start_ref,
     wq,
     wk,
     wv,
+    dcat,
+    act,
+    zs,
+    dl_once,
     wo,
     wu,
     wd,
@@ -164,13 +168,10 @@
     probs,
     att,
     inv,
-    zs,
     n1,
     r1,
     hb,
-    act,
     gp,
-    dcat,
     uq,
     uv,
     own_q,
@@ -217,6 +218,7 @@
         large = low_lane & (seg_hi - seg_lo == BIG)
         start = jnp.sum(jnp.where(large, seg_lo, 0.0)).astype(jnp.int32)
         starts.append(start)
+        start_ref[pack] = start
         row = lax.broadcasted_iota(jnp.int32, (BIG, LANES), 0) + (BIG + start)
         row = jnp.where(row >= rows, row - rows, row)
         inside = (row >= seg_lo.astype(jnp.int32)) & (row < seg_hi.astype(jnp.int32))
@@ -402,6 +404,8 @@
         copy.wait()
     cr[...] = dot(hb[...], wo[...], 1, 1).astype(bf16)
 
+    dq, dk, dv = (act.at[:, k * width : (k + 1) * width] for k in range(3))
+
     def group_back(turn_no, carry):
         ready = {}
 
@@ -431,20 +435,20 @@
         def finish(unit, one, two):
             _, _, block, span, at, _ = unit
             ready.pop((id(at), block))
-            qs[span, at] = (jnp.where(low, one[0], two[0]) * HEAD_DIM**-0.5).astype(bf16)
-            dk = jnp.concatenate([one[1], two[1]], axis=0) * (1.0 / LOG2E)
-            ks[span, at] = dk.astype(bf16).T
-            vs[span, at] = jnp.concatenate([one[2], two[2]], axis=0).astype(bf16).T
+            dq[span, at] = (jnp.where(low, one[0], two[0]) * HEAD_DIM**-0.5).astype(bf16)
+            turned = jnp.concatenate([one[1], two[1]], axis=0) * (1.0 / LOG2E)
+            dk[span, at] = turned.astype(bf16).T
+            dv[span, at] = jnp.concatenate([one[2], two[2]], axis=0).astype(bf16).T
 
         pipeline(heads_of(turn_no), slopes, weigh, grads_of, finish)
         return carry
 
     lax.fori_loop(0, turns, group_back, 0)
 
-    dl = (dot(qs[...], uq[...], 1, 1) + dot(vs[...], uv[...], 1, 1)).astype(bf16)
+    dl = (dot(dq[...], uq[...], 1, 1) + dot(dv[...], uv[...], 1, 1)).astype(bf16)
     gd = dot(dl, xr[...], 0, 0)
-    gq = adapter_scale * dot(lora[...], qs[...], 0, 0)[:RANK]
-    gv = adapter_scale * dot(lora[...], vs[...], 0, 0)[HEAD_DIM : HEAD_DIM + RANK]
+    gq = adapter_scale * dot(lora[...], dq[...], 0, 0)[:RANK]
+    gv = adapter_scale * dot(lora[...], dv[...], 0, 0)[HEAD_DIM : HEAD_DIM + RANK]
     pack_grads(flat, gd, gq, gv)
     half_rows = flat.shape[0] // 2
     side = side_ref[0]
@@ -455,21 +459,34 @@
     keep_ref[half_rows : half_rows + more, :] = first_ref[...]
     keep_ref[half_rows + more :, :] = second_ref[...]
 
-    dl_once = jnp.where(narrow, dl, jnp.zeros((total_rows, LANES), bf16))
-    for c in range(width // BIG):
-        at = slice(c * BIG, (c + 1) * BIG)
-        term = dot(qs[...], wq[at, :], 1, 1) + dot(ks[...], wk[at, :], 1, 1)
-        term = term + dot(vs[...], wv[at, :], 1, 1) + dot(dl_once, dcat[at, :], 1, 1)
-        zs[:, at] = zs[:, at] + term
-    results = []
+    dl_once[...] = jnp.where(narrow, dl, jnp.zeros((total_rows, LANES), bf16))
+
+
+def token_kernel(begin, start_ref, wq, wk, wv, dcat, grads, first, dl_once, *rest):
+    out_hbm, total, stage, sems = rest[-4:]
+    total_rows, cut = total.shape
+    packs = start_ref.shape[0]
+    rows = total_rows // packs
+    width = first.shape[1]
+    for c in range(cut // BIG):
+        here = slice(c * BIG, (c + 1) * BIG)
+        at = slice(begin + c * BIG, begin + (c + 1) * BIG)
+        term = first[:, at] + dot(dl_once[...], dcat[at, :], 1, 1)
+        for k, weight in enumerate((wq, wk, wv)):
+            term = term + dot(grads[:, k * width : (k + 1) * width], weight[at, :], 1, 1)
+        total[:, here] = term
+    copies = []
     for pack in range(packs):
         span = pl.ds(pack * rows, rows)
-        rotate_rows(zs, pack * rows, rows, rows - starts[pack], put(hb, pack * rows))
-        results.append(
-            pltpu.make_async_copy(hb.at[span, :], tgrad_hbm.at[span, :], sems.at[8 + pack])
-        )
-        results[-1].start()
-    for copy in results:
+
+        def emit(at, block, base=pack * rows):
+            stage[pl.ds(base + at, 16), :] = block.astype(bf16)
+
+        rotate_rows(total, pack * rows, rows, rows - start_ref[pack], emit)
+        to = out_hbm.at[span, begin : begin + cut]
+        copies.append(pltpu.make_async_copy(stage.at[span, :], to, sems.at[pack]))
+        copies[-1].start()
+    for copy in copies:
         copy.wait()
 
 
@@ -569,17 +586,22 @@
         norm2_bias,
     )
     tall = lambda dtype: pltpu.VMEM((total_rows, width), dtype)
-    kept, sent, output, grad_tokens = pl.pallas_call(
+    kept, sent, output, *for_tokens = pl.pallas_call(
         main_kernel,
         out_shape=(
             result((half_rows + 2 * own_rows, LANES), f32),
             result((half_rows, LANES), f32),
             result((total_rows, width), bf16),
-            result((total_rows, width), bf16),
+            result((packs,), jnp.int32),
+            *[pltpu.VMEM((width, width), bf16)] * 3,
+            pltpu.VMEM((width, LANES), bf16),
+            pltpu.VMEM((total_rows, ff), bf16),
+            tall(f32),
+            pltpu.VMEM((total_rows, LANES), bf16),
         ),
         in_specs=[scalars] + [whole] * (4 + len(vectors)) + [anywhere] * 8,
-        out_specs=[whole, whole, anywhere, anywhere],
-        scratch_shapes=[pltpu.VMEM(w.shape, bf16) for w in weights]
+        out_specs=[whole, whole, anywhere, scalars] + [whole] * 7,
+        scratch_shapes=[pltpu.VMEM(w.shape, bf16) for w in weights[3:]]
         + [
             pltpu.SemaphoreType.DMA((8 + packs,)),
             pltpu.VMEM((rows, width), f32),
@@ -593,12 +615,9 @@
             tall(bf16),
             tall(f32),
             tall(f32),
-            tall(f32),
             pltpu.VMEM((total_rows, 1), f32),
             tall(bf16),
             pltpu.VMEM((total_rows, ff), bf16),
-            pltpu.VMEM((total_rows, ff), bf16),
-            pltpu.VMEM((width, LANES), bf16),
             pltpu.VMEM((LANES, width), bf16),
             pltpu.VMEM((LANES, width), bf16),
             pltpu.VMEM((packs, BIG, LANES), bf16),
@@ -618,13 +637,39 @@
         *weights,
     )
 
+    def token_piece(begin, cut, before, tie):
+        held = [] if before is None else [before]
+        start, _ = lax.optimization_barrier((for_tokens[0], tie))
+        return pl.pallas_call(
+            functools.partial(token_kernel, begin),
+            out_shape=result((total_rows, width), bf16),
+            in_specs=[scalars] + [whole] * 7 + [anywhere] * len(held),
+            out_specs=anywhere,
+            scratch_shapes=[
+                pltpu.VMEM((total_rows, cut), f32),
+                pltpu.VMEM((total_rows, cut), bf16),
+                pltpu.SemaphoreType.DMA((packs,)),
+            ],
+            input_output_aliases={8: 0} if held else {},
+            compiler_params=pltpu.CompilerParams(vmem_limit_bytes=16 * 2**20),
+            cost_estimate=pl.CostEstimate(
+                flops=2 * total_rows * cut * (3 * width + LANES),
+                bytes_accessed=total_rows * cut * 2,
+                transcendentals=0,
+            ),
+        )(start, *for_tokens[1:], *held)
+
     held = kept.at[:half_rows].add(swap(sent, "wide", 1))
     bits = bits_of("wide")[1:]
     places = [0]
+    grad_tokens = None
     while bits:
         now, bits = bits[:2], bits[2:]
         masks = [now[0]] if len(now) == 1 else [now[0], now[1], now[0] | now[1]]
         got = [swap(held, "wide", mask) for mask in masks]
+        if grad_tokens is None:
+            grad_tokens = token_piece(0, width - BIG, None, held)
+            grad_tokens, *got = lax.optimization_barrier((grad_tokens, *got))
         if len(got) == 1:
             total = held[:half_rows] + got[0][:half_rows]
         else:
@@ -636,8 +681,12 @@
             held = jnp.concatenate([total] + [part[half_rows:] for part in [held] + got])
         else:
             moments = [part[half_rows:] for part in [held] + got]
-    for bit in bits_of("dp"):
-        total = total + swap(total, "dp", bit)
+    for k, bit in enumerate(bits_of("dp")):
+        got = swap(total, "dp", bit)
+        if k == 0:
+            grad_tokens = token_piece(width - BIG, BIG, grad_tokens, total)
+            grad_tokens, got = lax.optimization_barrier((grad_tokens, got))
+        total = total + got
     held = jnp.concatenate([total] + moments)
     other = swap(held, "wide", 1)
 

time: 95.7 us -> 85.1 us (0.89)
  waiting for transfers between devices: 10.2 us -> 3.21 us
  Pallas kernels: 71.3 us -> 67.5 us
    pallas_call x1, Pallas kernels: 69.3 us -> 57.8 us  [shards(): pl.pallas_call(main_kernel, out_shape=(result((half_rows + 2 * own_rows,...]
    pallas_call x0 -> x2, Pallas kernels: none -> 7.73 us  [token_piece(): pl.pallas_call(functools.partial(token_kernel, begin), out_shape=result((...]
    ppermute x7, waiting for transfers between devices: 10.2 us -> 3.21 us  [swap(): return lax.ppermute(x, axis, [(i, i ^ bit) for i in range(n)])]
    unnamed x8 -> x12, local copies, waits for them, and re-layouts: 1.55 us -> 2.22 us
  transfers between devices with their start and end apart: 7 -> 7, of which waited for: 7 -> 3; matrix products, arithmetic and copies ran while one was open for 1% -> 1% of each run, Pallas kernels for 0% -> 9%
where the time goes in v4:
time: 85.1 us; the launch traced here: 84.8 us
  Pallas kernels  67.5 us (79%)
  starting transfers between devices  9.79 us (12%)
  waiting for transfers between devices  3.21 us (4%)
  local copies, waits for them, and re-layouts  2.22 us (3%)
  between operations  2.07 us (2%)
    pallas_call x1, Pallas kernels, shards(): pl.pallas_call(main_kernel, out_shape=(result((half_rows + 2 * own_rows,...  57.8 us
    ppermute x7, starting transfers between devices, swap(): return lax.ppermute(x, axis, [(i, i ^ bit) for i in range(n)])  9.79 us
    pallas_call x2, Pallas kernels, token_piece(): pl.pallas_call(functools.partial(token_kernel, begin), out_shape=result((...  7.73 us
    ppermute x7, waiting for transfers between devices, swap(): return lax.ppermute(x, axis, [(i, i ^ bit) for i in range(n)])  3.21 us
    unnamed x12, local copies, waits for them, and re-layouts  2.22 us
    pallas_call x1, Pallas kernels, shards(): pl.pallas_call(functools.partial(optimizer_kernel, places), out_shape=(ow...  2 us
  transfers between devices with their start and end apart: 7, of which 3 were waited for; matrix products, arithmetic and copies ran while one was open for 1% of the time, Pallas kernels for 9%

profile of v4, /device:TPU:0, one launch (start us, length us, event | category | flops | bytes accessed | tf_op | source)
XLA Modules:
  0.0 84.8 jit_solution(14320347776472413609)
XLA Ops:
  0.6 57.8 %shard_map.262 = (f32[144,128]{1,0:T(8,128)}, f32[96,128]{1,0:T(8,128)}, bf16[1024,768]{1,0:T(8,128)(2,1)}, s32[2]{0:T(128)}, bf16[768,768]{1,0:T(8,128)(2,1)S(1...) custom-call(s32[1]{0:T(128)} %bitcast.side_ref, ...), custom_call_target="tpu_custom_call" | custom-call | tf_op jit(solution)/shard_map/pallas_call | solution.py:589
  58.4 0.5 collective-permute-start
  58.9 0.9 %copy.30 = f32[144,128]{1,0:T(8,128)S(1)} copy(f32[144,128]{1,0:T(8,128)} %get-tuple-element.43) | data formatting | bytes 147456
  59.8 0.2 collective-permute-done
  60.0 2.9 %collective-permute-start.1 = (f32[144,128]{1,0:T(8,128)S(1)}, f32[144,128]{1,0:T(8,128)S(1)}, u32[]{:S(2)}, u32[]{:S(2)}) collective-permute-start(f32[144,128]{1,0:T(8,128)S(1)} %fusion), channel_id=1, source_target_pairs={{0,2},{1,3},{2,0},{3,1},{4,6},{5,7},{6,4},{7,5},{8,10},{9,11},{10,... | collective-permute-start | bytes 221192 | tf_op jit(solution)/shard_map/ppermute | solution.py:529
  63.0 1.5 %collective-permute-start.2 = (f32[144,128]{1,0:T(8,128)S(1)}, f32[144,128]{1,0:T(8,128)S(1)}, u32[]{:S(2)}, u32[]{:S(2)}) collective-permute-start(f32[144,128]{1,0:T(8,128)S(1)} %fusion), channel_id=1, source_target_pairs={{0,4},{1,5},{2,6},{3,7},{4,0},{5,1},{6,2},{7,3},{8,12},{9,13},{10,... | collective-permute-start | bytes 221192 | tf_op jit(solution)/shard_map/ppermute | solution.py:529
  64.5 0.0 collective-permute-start.3
  64.5 0.0 copy-start
  64.5 0.7 copy-done
  65.2 0.0 copy-start.2
  65.2 4.6 %shard_map.263.rest_0_ = bf16[1024,768]{1,0:T(8,128)(2,1)} custom-call(s32[2]{0:T(128)S(1)} %copy-done, bf16[768,768]{1,0:T(8,128)(2,1)S(1)} %get-tuple-element.46.wq, bf16[768,768]{1,0:T(8,128)(2,1)S(1)} %get-tuple-element.47.wk, bf16[768,768]{1,0:T(8,128)(2,1)S(1)} %get-tuple-element.48.wv, bf16[768,128]{1,0:T(8,128)(2,1)S(1)} %get-tuple-element.49.dcat, ...), custom_call_target="tpu_custom_call" | custom-call | flops 2550136832 | bytes 1048576 | tf_op jit(solution)/shard_map/pallas_call | solution.py:643
  69.8 0.0 collective-permute-done.1
  69.8 0.0 collective-permute-done.2
  69.8 0.0 collective-permute-done.3
  69.8 0.0 copy-done.2
  69.9 2.1 %collective-permute-start.4 = (f32[96,128]{1,0:T(8,128)S(1)}, f32[96,128]{1,0:T(8,128)S(1)}, u32[]{:S(2)}, u32[]{:S(2)}) collective-permute-start(f32[96,128]{1,0:T(8,128)S(1)} %add_add_fusion), channel_id=1, source_target_pairs={{0,8},{8,0},{16,24},{24,16},{1,9},{9,1},{17,25},{25,17},{2,10},{10... | collective-permute-start | bytes 147464 | tf_op jit(solution)/shard_map/ppermute | solution.py:529
  72.0 3.1 %shard_map.264 = bf16[1024,768]{1,0:T(8,128)(2,1)} custom-call(s32[2]{0:T(128)S(1)} %copy-done, bf16[768,768]{1,0:T(8,128)(2,1)S(1)} %get-tuple-element.46.wq, bf16[768,768]{1,0:T(8,128)(2,1)S(1)} %get-tuple-element.47.wk, bf16[768,768]{1,0:T(8,128)(2,1)S(1)} %get-tuple-element.48.wv, ...), custom_call_target="tpu_custom_call", output_to_operand_aliasing={{}: (8, {})} | custom-call | flops 1275068416 | bytes 524288 | tf_op jit(solution)/shard_map/pallas_call | solution.py:643
  75.1 0.0 collective-permute-done.4
  75.1 2.6 %collective-permute-start.5 = (f32[96,128]{1,0:T(8,128)S(1)}, f32[96,128]{1,0:T(8,128)S(1)}, u32[]{:S(2)}, u32[]{:S(2)}) collective-permute-start(f32[96,128]{1,0:T(8,128)S(1)} %add.26), channel_id=1, source_target_pairs={{0,16},{8,24},{16,0},{24,8},{1,17},{9,25},{17,1},{25,9},{2,18},{10... | collective-permute-start | bytes 147464 | tf_op jit(solution)/shard_map/ppermute | solution.py:529
  77.7 2.9 %collective-permute-done.5 = f32[96,128]{1,0:T(8,128)S(1)} collective-permute-done((f32[96,128]{1,0:T(8,128)S(1)}, f32[96,128]{1,0:T(8,128)S(1)}, u32[]{:S(2)}, u32[]{:S(2)}) %collective-permute-start.5) | collective-permute-done | bytes 49184 | tf_op jit(solution)/shard_map/ppermute | solution.py:529
  80.7 0.0 copy-start.1
  80.7 0.1 collective-permute-start.6
  82.1 0.1 collective-permute-done.6
  82.2 0.0 copy-start.3
  82.2 0.0 copy-done.1
  82.2 0.7 copy-done.3
  82.8 2.0 %shard_map.265 = (f32[24,128]{1,0:T(8,128)}, f32[8,24,128]{2,1,0:T(8,128)}, f32[24,128]{1,0:T(8,128)}, f32[24,128]{1,0:T(8,128)}) custom-call(s32[1]{0:T(128)S(6)} %copy.36.refs_0_, f32[1]{0:T(128)S(6)} %copy.37.refs_1_, s32[1]{0:T(128)} %bitcast.4.refs_2_, f32[12,24,128]{2,1,0:T(8,128)} %bitcast.14, f32[12,24,128]{2,1,0:T(8,128)} %bitcast.15, ...), custom_call_target="tpu_custom_call" | custom-call | tf_op jit(solution)/shard_map/pallas_call | solution.py:695
  (8 shorter events, 0.1 us)
Async XLA Ops:
  58.4 1.6 %collective-permute-start = (f32[96,128]{1,0:T(8,128)}, f32[96,128]{1,0:T(8,128)S(1)}, u32[]{:S(2)}, u32[]{:S(2)}) collective-permute-start(f32[96,128]{1,0:T(8,128)} %get-tuple-element.44), channel_id=1, source_target_pairs={{0,1},{1,0},{2,3},{3,2},{4,5},{5,4},{6,7},{7,6},{8,9},{9,8},{10,11... | collective-permute-start | bytes 147464 | tf_op jit(solution)/shard_map/ppermute | solution.py:529
  60.0 9.8 %collective-permute-start.1 = (f32[144,128]{1,0:T(8,128)S(1)}, f32[144,128]{1,0:T(8,128)S(1)}, u32[]{:S(2)}, u32[]{:S(2)}) collective-permute-start(f32[144,128]{1,0:T(8,128)S(1)} %fusion), channel_id=1, source_target_pairs={{0,2},{1,3},{2,0},{3,1},{4,6},{5,7},{6,4},{7,5},{8,10},{9,11},{10,... | collective-permute-start | bytes 221192 | tf_op jit(solution)/shard_map/ppermute | solution.py:529
  63.0 6.8 %collective-permute-start.2 = (f32[144,128]{1,0:T(8,128)S(1)}, f32[144,128]{1,0:T(8,128)S(1)}, u32[]{:S(2)}, u32[]{:S(2)}) collective-permute-start(f32[144,128]{1,0:T(8,128)S(1)} %fusion), channel_id=1, source_target_pairs={{0,4},{1,5},{2,6},{3,7},{4,0},{5,1},{6,2},{7,3},{8,12},{9,13},{10,... | collective-permute-start | bytes 221192 | tf_op jit(solution)/shard_map/ppermute | solution.py:529
  64.5 5.3 %collective-permute-start.3 = (f32[144,128]{1,0:T(8,128)S(1)}, f32[144,128]{1,0:T(8,128)S(1)}, u32[]{:S(2)}, u32[]{:S(2)}) collective-permute-start(f32[144,128]{1,0:T(8,128)S(1)} %fusion), channel_id=1, source_target_pairs={{0,6},{1,7},{2,4},{3,5},{4,2},{5,3},{6,0},{7,1},{8,14},{9,15},{10,... | collective-permute-start | bytes 221192 | tf_op jit(solution)/shard_map/ppermute | solution.py:529
  64.5 0.7 copy-start
  65.2 4.7 %copy-start.2 = (f32[144,128]{1,0:T(8,128)S(1)}, f32[144,128]{1,0:T(8,128)}, u32[]{:S(2)}) copy-start(f32[144,128]{1,0:T(8,128)} %get-tuple-element.43) | copy-start | bytes 221188
  69.9 5.2 %collective-permute-start.4 = (f32[96,128]{1,0:T(8,128)S(1)}, f32[96,128]{1,0:T(8,128)S(1)}, u32[]{:S(2)}, u32[]{:S(2)}) collective-permute-start(f32[96,128]{1,0:T(8,128)S(1)} %add_add_fusion), channel_id=1, source_target_pairs={{0,8},{8,0},{16,24},{24,16},{1,9},{9,1},{17,25},{25,17},{2,10},{10... | collective-permute-start | bytes 147464 | tf_op jit(solution)/shard_map/ppermute | solution.py:529
  75.1 5.6 %collective-permute-start.5 = (f32[96,128]{1,0:T(8,128)S(1)}, f32[96,128]{1,0:T(8,128)S(1)}, u32[]{:S(2)}, u32[]{:S(2)}) collective-permute-start(f32[96,128]{1,0:T(8,128)S(1)} %add.26), channel_id=1, source_target_pairs={{0,16},{8,24},{16,0},{24,8},{1,17},{9,25},{17,1},{25,9},{2,18},{10... | collective-permute-start | bytes 147464 | tf_op jit(solution)/shard_map/ppermute | solution.py:529
  80.7 1.5 %copy-start.1 = (f32[288,128]{1,0:T(8,128)}, f32[288,128]{1,0:T(8,128)S(1)}, u32[]{:S(2)}) copy-start(f32[288,128]{1,0:T(8,128)S(1)} %slice_dynamic-update-slice_fusion.1) | copy-start | bytes 442372
  80.7 1.4 %collective-permute-start.6 = (f32[288,128]{1,0:T(8,128)S(1)}, f32[288,128]{1,0:T(8,128)S(1)}, u32[]{:S(2)}, u32[]{:S(2)}) collective-permute-start(f32[288,128]{1,0:T(8,128)S(1)} %slice_dynamic-update-slice_fusion.1), channel_id=1, source_target_pairs={{0,1},{1,0},{2,3},{3,2},{4,5},{5,4},{6,7},{7,6},{8,9},{9,8},{10,11... | collective-permute-start | bytes 442376 | tf_op jit(solution)/shard_map/ppermute | solution.py:529
  82.2 0.7 copy-start.3

commit v5 on v4

--- a/solution.py
+++ b/solution.py
@@ -15,7 +15,7 @@
 GROUP = 6
 STEP = 256
 CHUNK = 768
-VMEM_LIMIT = 50 * 2**20
+VMEM_LIMIT = 199 * 2**18
 LOG2E = 1.4426950408889634
 LOG2_ROOT = 1.3257480647361592
 
@@ -98,7 +98,7 @@
 
     def turned(i):
         at = pl.multiple_of(base + 8 * lax.rem(coarse + i, groups), 8)
-        return pltpu.roll(src[pl.ds(at, 8), :], back, 0)
+        return pltpu.roll(src[pl.ds(at, 8), :].astype(f32), back, 0)
 
     spun = [turned(i) for i in range(groups + 1)]
     moved = [jnp.where(keep, spun[i], spun[i + 1]) for i in range(groups)]
@@ -147,18 +147,13 @@
     send_ref,
     out_hbm,
     start_ref,
-    wq,
-    wk,
-    wv,
-    dcat,
+    wcat,
     act,
     zs,
-    dl_once,
     wo,
     wu,
     wd,
     sems,
-    spin,
     xr,
     cr,
     qs,
@@ -181,13 +176,17 @@
     packs, rows = seg_ref.shape
     total_rows, width = xr.shape
     pairs = width // LANES
+    wq, wk, wv = (wcat.at[:, k * width : (k + 1) * width] for k in range(3))
+    dcat = wcat.at[:, 3 * width :]
+    raw_tokens = act.at[:, :width]
+    raw_cotangent = act.at[:, width : 2 * width]
     copies = []
     for src, dst in (
-        (tok_hbm, xr),
+        (tok_hbm, raw_tokens),
         (wq_hbm, wq),
         (wk_hbm, wk),
         (wv_hbm, wv),
-        (cot_hbm, cr),
+        (cot_hbm, raw_cotangent),
         (wo_hbm, wo),
         (wu_hbm, wu),
         (wd_hbm, wd),
@@ -218,7 +217,7 @@
         large = low_lane & (seg_hi - seg_lo == BIG)
         start = jnp.sum(jnp.where(large, seg_lo, 0.0)).astype(jnp.int32)
         starts.append(start)
-        start_ref[pack] = start
+        start_ref[pack : pack + 1, :] = jnp.full((1, LANES), start.astype(f32))
         row = lax.broadcasted_iota(jnp.int32, (BIG, LANES), 0) + (BIG + start)
         row = jnp.where(row >= rows, row - rows, row)
         inside = (row >= seg_lo.astype(jnp.int32)) & (row < seg_hi.astype(jnp.int32))
@@ -231,13 +230,12 @@
 
         return emit
 
-    def turn(ref):
+    def turn(src, dst):
         for pack in range(packs):
-            spin[...] = ref[pack * rows : (pack + 1) * rows, :].astype(f32)
-            rotate_rows(spin, 0, rows, starts[pack], put(ref, pack * rows))
+            rotate_rows(src, pack * rows, rows, starts[pack], put(dst, pack * rows))
 
     arrive(0)
-    turn(xr)
+    turn(raw_tokens, xr)
 
     lora[...] = dot(xr[...], dcat[...]).astype(bf16)
     narrow = lax.broadcasted_iota(jnp.int32, (total_rows, LANES), 1) % HEAD_DIM < RANK
@@ -314,28 +312,24 @@
 
     turns = packs * pairs // GROUP
     lax.fori_loop(0, turns, group_forward, 0)
-    arrive(4)
-    turn(cr)
-
-    arrive(5)
-    zs[...] = dot(att[...], wo[...])
+
+    arrive(4, 5)
+    halves = [slice(pack * rows, (pack + 1) * rows) for pack in range(packs)]
+    for at in halves:
+        zs[at, :] = dot(att[at, :], wo[...])
     step = STEP
 
-    def steps(body):
-        def run(i, carry):
-            body(pl.ds(pl.multiple_of(i * step, step), step))
-            return carry
-
-        lax.fori_loop(0, total_rows // step, run, 0)
-
-    def first_norm(at):
-        z = xr[at, :].astype(f32) + zs[at, :] + line(bo[...])
-        n, root = norm_rows(z)
-        n1[at, :] = n
-        r1[at, :] = root
-        hb[at, :] = (n * line(g1[...]) + line(b1[...])).astype(bf16)
-
-    steps(first_norm)
+    def pieces_of(at):
+        return [slice(k, k + step) for k in range(at.start, at.stop, step)]
+
+    for half in halves:
+        for at in pieces_of(half):
+            z = xr[at, :].astype(f32) + zs[at, :] + line(bo[...])
+            n, root = norm_rows(z)
+            n1[at, :] = n
+            r1[at, :] = root
+            hb[at, :] = (n * line(g1[...]) + line(b1[...])).astype(bf16)
+    turn(raw_cotangent, cr)
 
     arrive(6)
     chunk = CHUNK
@@ -354,26 +348,23 @@
     lax.fori_loop(0, count, up, 0)
     arrive(7)
 
-    def down(c, carry):
-        at = pl.ds(pl.multiple_of(c * BIG, BIG), BIG)
-        zs[:, at] = dot(act[...], wd[:, at])
-        return carry
-
-    lax.fori_loop(0, width // BIG, down, 0)
+    for half in halves:
+        for c in range(width // BIG):
+            at = slice(c * BIG, (c + 1) * BIG)
+            zs[half, at] = dot(act[half, :], wd[:, at])
     results = []
     for pack in range(packs):
-        for part in range(rows // step):
-            at = slice(pack * rows + part * step, pack * rows + (part + 1) * step)
+        for at in pieces_of(halves[pack]):
             hidden = n1[at, :] * line(g1[...]) + line(b1[...])
             z = hidden + zs[at, :] + line(bd[...])
             n, root = norm_rows(z)
             gain = line(g2[...])
-            spin[part * step : (part + 1) * step, :] = n * gain + line(b2[...])
+            raw_tokens[at, :] = (n * gain + line(b2[...])).astype(bf16)
             d = norm_rows_back(cr[at, :].astype(f32) * gain, n, root)
             zs[at, :] = d
             hb[at, :] = d.astype(bf16)
         span = pl.ds(pack * rows, rows)
-        rotate_rows(spin, 0, rows, rows - starts[pack], put(cr, pack * rows))
+        rotate_rows(raw_tokens, pack * rows, rows, rows - starts[pack], put(cr, pack * rows))
         results.append(
             pltpu.make_async_copy(cr.at[span, :], out_hbm.at[span, :], sems.at[8 + pack])
         )
@@ -394,15 +385,14 @@
 
     lax.fori_loop(0, width // BIG, down_back, 0)
 
-    def first_norm_back(at):
-        d = norm_rows_back(zs[at, :] * line(g1[...]), n1[at, :], r1[at, :])
-        zs[at, :] = d
-        hb[at, :] = d.astype(bf16)
-
-    steps(first_norm_back)
     for copy in results:
         copy.wait()
-    cr[...] = dot(hb[...], wo[...], 1, 1).astype(bf16)
+    for half in halves:
+        for at in pieces_of(half):
+            d = norm_rows_back(zs[at, :] * line(g1[...]), n1[at, :], r1[at, :])
+            zs[at, :] = d
+            hb[at, :] = d.astype(bf16)
+        cr[half, :] = dot(hb[half, :], wo[...], 1, 1).astype(bf16)
 
     dq, dk, dv = (act.at[:, k * width : (k + 1) * width] for k in range(3))
 
@@ -453,28 +443,28 @@
     half_rows = flat.shape[0] // 2
     side = side_ref[0]
     kept = flat[pl.ds(pl.multiple_of(side * half_rows, 8), half_rows), :]
-    send_ref[...] = flat[pl.ds(pl.multiple_of((1 - side) * half_rows, 8), half_rows), :]
     more = first_ref.shape[0]
+    send_ref[:half_rows, :] = flat[pl.ds(pl.multiple_of((1 - side) * half_rows, 8), half_rows), :]
+    send_ref[half_rows:, :] = jnp.zeros((2 * more, LANES), f32)
     keep_ref[:half_rows, :] = kept
     keep_ref[half_rows : half_rows + more, :] = first_ref[...]
     keep_ref[half_rows + more :, :] = second_ref[...]
 
-    dl_once[...] = jnp.where(narrow, dl, jnp.zeros((total_rows, LANES), bf16))
-
-
-def token_kernel(begin, start_ref, wq, wk, wv, dcat, grads, first, dl_once, *rest):
+    act[:, 3 * width : 3 * width + LANES] = jnp.where(
+        narrow, dl, jnp.zeros((total_rows, LANES), bf16)
+    )
+
+
+def token_kernel(begin, start_ref, wcat, grads, first, *rest):
     out_hbm, total, stage, sems = rest[-4:]
     total_rows, cut = total.shape
     packs = start_ref.shape[0]
     rows = total_rows // packs
-    width = first.shape[1]
+    depth = wcat.shape[1]
     for c in range(cut // BIG):
-        here = slice(c * BIG, (c + 1) * BIG)
         at = slice(begin + c * BIG, begin + (c + 1) * BIG)
-        term = first[:, at] + dot(dl_once[...], dcat[at, :], 1, 1)
-        for k, weight in enumerate((wq, wk, wv)):
-            term = term + dot(grads[:, k * width : (k + 1) * width], weight[at, :], 1, 1)
-        total[:, here] = term
+        term = dot(grads[:, :depth], wcat[at, :], 1, 1)
+        total[:, c * BIG : (c + 1) * BIG] = first[:, at] + term
     copies = []
     for pack in range(packs):
         span = pl.ds(pack * rows, rows)
@@ -482,7 +472,8 @@
         def emit(at, block, base=pack * rows):
             stage[pl.ds(base + at, 16), :] = block.astype(bf16)
 
-        rotate_rows(total, pack * rows, rows, rows - start_ref[pack], emit)
+        start = jnp.max(start_ref[pack : pack + 1, :]).astype(jnp.int32)
+        rotate_rows(total, pack * rows, rows, rows - start, emit)
         to = out_hbm.at[span, begin : begin + cut]
         copies.append(pltpu.make_async_copy(stage.at[span, :], to, sems.at[pack]))
         copies[-1].start()
@@ -497,8 +488,10 @@
     half = shares // 2
     place = place_ref[0]
     side = place & 1
-    total[side] = held[:half]
-    total[1 - side] = other[:half]
+    for k in range(half):
+        at = slice(k * own_rows, (k + 1) * own_rows)
+        total[side, k] = held[at, :]
+        total[1 - side, k] = other[at, :]
     norm_sq = jnp.sum(jnp.sum(total[...] * total[...], axis=(0, 1)), keepdims=True)
     clip = jnp.minimum(1.0, lax.rsqrt(norm_sq + 1e-06))
 
@@ -511,10 +504,12 @@
     grad_out[...] = total[place // half, place % half]
     for j, mask in enumerate(places + [mask ^ 1 for mask in places]):
         source, at = (held, half + 2 * j) if j < half else (other, half + 2 * (j - half))
+        moment = source[at * own_rows : (at + 1) * own_rows, :]
+        square = source[(at + 1) * own_rows : (at + 2) * own_rows, :]
         share = place ^ mask
         clipped = total[share // half, share % half] * clip
-        first = beta_one * source[at] + (1.0 - beta_one) * clipped
-        second = beta_two * source[at + 1] + (1.0 - beta_two) * clipped * clipped
+        first = beta_one * moment + (1.0 - beta_one) * clipped
+        second = beta_two * square + (1.0 - beta_two) * clipped * clipped
         if j == 0:
             first_out[...] = first
             second_out[...] = second
@@ -589,22 +584,19 @@
     kept, sent, output, *for_tokens = pl.pallas_call(
         main_kernel,
         out_shape=(
-            result((half_rows + 2 * own_rows, LANES), f32),
-            result((half_rows, LANES), f32),
+            pltpu.VMEM((half_rows + 2 * own_rows, LANES), f32),
+            pltpu.VMEM((half_rows + 2 * own_rows, LANES), f32),
             result((total_rows, width), bf16),
-            result((packs,), jnp.int32),
-            *[pltpu.VMEM((width, width), bf16)] * 3,
-            pltpu.VMEM((width, LANES), bf16),
+            pltpu.VMEM((packs, LANES), f32),
+            pltpu.VMEM((width, 3 * width + LANES), bf16),
             pltpu.VMEM((total_rows, ff), bf16),
             tall(f32),
-            pltpu.VMEM((total_rows, LANES), bf16),
         ),
         in_specs=[scalars] + [whole] * (4 + len(vectors)) + [anywhere] * 8,
-        out_specs=[whole, whole, anywhere, scalars] + [whole] * 7,
+        out_specs=[whole, whole, anywhere] + [whole] * 4,
         scratch_shapes=[pltpu.VMEM(w.shape, bf16) for w in weights[3:]]
         + [
             pltpu.SemaphoreType.DMA((8 + packs,)),
-            pltpu.VMEM((rows, width), f32),
             tall(bf16),
             tall(bf16),
             tall(bf16),
@@ -643,14 +635,14 @@
         return pl.pallas_call(
             functools.partial(token_kernel, begin),
             out_shape=result((total_rows, width), bf16),
-            in_specs=[scalars] + [whole] * 7 + [anywhere] * len(held),
+            in_specs=[whole] * 4 + [anywhere] * len(held),
             out_specs=anywhere,
             scratch_shapes=[
                 pltpu.VMEM((total_rows, cut), f32),
                 pltpu.VMEM((total_rows, cut), bf16),
                 pltpu.SemaphoreType.DMA((packs,)),
             ],
-            input_output_aliases={8: 0} if held else {},
+            input_output_aliases={4: 0} if held else {},
             compiler_params=pltpu.CompilerParams(vmem_limit_bytes=16 * 2**20),
             cost_estimate=pl.CostEstimate(
                 flops=2 * total_rows * cut * (3 * width + LANES),
@@ -659,7 +651,7 @@
             ),
         )(start, *for_tokens[1:], *held)
 
-    held = kept.at[:half_rows].add(swap(sent, "wide", 1))
+    held = kept + swap(sent, "wide", 1)
     bits = bits_of("wide")[1:]
     places = [0]
     grad_tokens = None
@@ -681,9 +673,9 @@
             held = jnp.concatenate([total] + [part[half_rows:] for part in [held] + got])
         else:
             moments = [part[half_rows:] for part in [held] + got]
-    for k, bit in enumerate(bits_of("dp")):
+    for bit in bits_of("dp"):
         got = swap(total, "dp", bit)
-        if k == 0:
+        if bit == bits_of("dp")[-1]:
             grad_tokens = token_piece(width - BIG, BIG, grad_tokens, total)
             grad_tokens, got = lax.optimization_barrier((grad_tokens, got))
         total = total + got
@@ -702,8 +694,8 @@
         step_count,
         learn_rate,
         place.reshape(1),
-        held.reshape(-1, own_rows, LANES),
-        other.reshape(-1, own_rows, LANES),
+        held,
+        other,
         factors.reshape(shaped),
     )
     return (

time: 85.1 us -> 79.7 us (0.937)
  Pallas kernels: 67.5 us -> 62.8 us
  local copies, waits for them, and re-layouts: 2.22 us -> 0.67 us
  waiting for transfers between devices: 3.21 us -> 4.63 us
    pallas_call x1, Pallas kernels: 57.8 us -> 54.1 us  [shards(): pl.pallas_call(main_kernel, out_shape=(pltpu.VMEM((half_rows + 2 * own_ro...]
    unnamed x12 -> x7, local copies, waits for them, and re-layouts: 2.22 us -> 0.67 us
    ppermute x7, waiting for transfers between devices: 3.21 us -> 4.63 us  [swap(): return lax.ppermute(x, axis, [(i, i ^ bit) for i in range(n)])]
    pallas_call x2, Pallas kernels: 7.73 us -> 6.74 us  [token_piece(): pl.pallas_call(functools.partial(token_kernel, begin), out_shape=result((...]
  transfers between devices with their start and end apart: 7 -> 7, of which waited for: 3 -> 4; matrix products, arithmetic and copies ran while one was open for 1% -> 0% of each run, Pallas kernels for 9% -> 8%
where the time goes in v5:
time: 79.7 us; the launch traced here: 79.5 us
  Pallas kernels  62.8 us (79%)
  starting transfers between devices  9.27 us (12%)
  waiting for transfers between devices  4.63 us (6%)
  between operations  2.05 us (3%)
    pallas_call x1, Pallas kernels, shards(): pl.pallas_call(main_kernel, out_shape=(pltpu.VMEM((half_rows + 2 * own_ro...  54.1 us
    ppermute x7, starting transfers between devices, swap(): return lax.ppermute(x, axis, [(i, i ^ bit) for i in range(n)])  9.27 us
    pallas_call x2, Pallas kernels, token_piece(): pl.pallas_call(functools.partial(token_kernel, begin), out_shape=result((...  6.74 us
    ppermute x7, waiting for transfers between devices, swap(): return lax.ppermute(x, axis, [(i, i ^ bit) for i in range(n)])  4.63 us
    pallas_call x1, Pallas kernels, shards(): pl.pallas_call(functools.partial(optimizer_kernel, places), out_shape=(ow...  1.96 us
  transfers between devices with their start and end apart: 7, of which 4 were waited for; matrix products, arithmetic and copies ran while one was open for 0% of the time, Pallas kernels for 8%

profile of v5, /device:TPU:0, one launch (start us, length us, event | category | flops | bytes accessed | tf_op | source)
XLA Modules:
  0.0 79.5 jit_solution(12925392083224722551)
XLA Ops:
  0.6 54.1 %shard_map.262 = (f32[144,128]{1,0:T(8,128)S(1)}, f32[144,128]{1,0:T(8,128)S(1)}, bf16[1024,768]{1,0:T(8,128)(2,1)}, f32[2,128]{1,0:T(2,128)S(1)}, bf16[768,2432...) custom-call(s32[1]{0:T(128)} %bitcast.side_ref, s32[2,512]{1,0:T(2,128)} %seg_ref.1, ...), custom_call_target="tpu_custom_call" | custom-call | tf_op jit(solution)/shard_map/pallas_call | solution.py:584
  54.8 0.5 collective-permute-start
  55.3 0.9 %collective-permute-done = f32[144,128]{1,0:T(8,128)S(1)} collective-permute-done((f32[144,128]{1,0:T(8,128)S(1)}, f32[144,128]{1,0:T(8,128)S(1)}, u32[]{:S(2)}, u32[]{:S(2)}) %collective-permute-start) | collective-permute-done | bytes 73760 | tf_op jit(solution)/shard_map/ppermute | solution.py:524
  56.2 2.9 %collective-permute-start.1 = (f32[144,128]{1,0:T(8,128)S(1)}, f32[144,128]{1,0:T(8,128)S(1)}, u32[]{:S(2)}, u32[]{:S(2)}) collective-permute-start(f32[144,128]{1,0:T(8,128)S(1)} %add.18), channel_id=1, source_target_pairs={{0,2},{1,3},{2,0},{3,1},{4,6},{5,7},{6,4},{7,5},{8,10},{9,11},{10,... | collective-permute-start | bytes 221192 | tf_op jit(solution)/shard_map/ppermute | solution.py:524
  59.1 1.5 %collective-permute-start.2 = (f32[144,128]{1,0:T(8,128)S(1)}, f32[144,128]{1,0:T(8,128)S(1)}, u32[]{:S(2)}, u32[]{:S(2)}) collective-permute-start(f32[144,128]{1,0:T(8,128)S(1)} %add.18), channel_id=1, source_target_pairs={{0,4},{1,5},{2,6},{3,7},{4,0},{5,1},{6,2},{7,3},{8,12},{9,13},{10,... | collective-permute-start | bytes 221192 | tf_op jit(solution)/shard_map/ppermute | solution.py:524
  60.7 0.0 collective-permute-start.3
  60.7 4.1 %shard_map.263.rest_0_ = bf16[1024,768]{1,0:T(8,128)(2,1)} custom-call(f32[2,128]{1,0:T(2,128)S(1)} %get-tuple-element.36.start_ref, bf16[768,2432]{1,0:T(8,128)(2,1)S(1)} %get-tuple-element.30.wcat, bf16[1024,3072]{1,0:T(8,128)(2,1)S(1)} %get-tuple-element.31.grads, f32[1024,768]{1,0:T(8,128)S(1)} %get-tuple-element.32.first), custom_call_target="tpu_custom_call" | custom-call | flops 2550136832 | bytes 1048576 | tf_op jit(solution)/shard_map/pallas_call | solution.py:635
  64.8 0.0 collective-permute-done.1
  64.8 0.0 collective-permute-done.2
  64.8 1.1 %collective-permute-done.3 = f32[144,128]{1,0:T(8,128)S(1)} collective-permute-done((f32[144,128]{1,0:T(8,128)S(1)}, f32[144,128]{1,0:T(8,128)S(1)}, u32[]{:S(2)}, u32[]{:S(2)}) %collective-permute-start.3) | collective-permute-done | bytes 73760 | tf_op jit(solution)/shard_map/ppermute | solution.py:524
  65.9 1.6 %collective-permute-start.4 = (f32[96,128]{1,0:T(8,128)S(1)}, f32[96,128]{1,0:T(8,128)S(1)}, u32[]{:S(2)}, u32[]{:S(2)}) collective-permute-start(f32[96,128]{1,0:T(8,128)S(1)} %fusion), channel_id=1, source_target_pairs={{0,8},{8,0},{16,24},{24,16},{1,9},{9,1},{17,25},{25,17},{2,10},{10... | collective-permute-start | bytes 147464 | tf_op jit(solution)/shard_map/ppermute | solution.py:524
  67.5 2.5 %collective-permute-done.4 = f32[96,128]{1,0:T(8,128)S(1)} collective-permute-done((f32[96,128]{1,0:T(8,128)S(1)}, f32[96,128]{1,0:T(8,128)S(1)}, u32[]{:S(2)}, u32[]{:S(2)}) %collective-permute-start.4) | collective-permute-done | bytes 49184 | tf_op jit(solution)/shard_map/ppermute | solution.py:524
  70.1 2.6 %collective-permute-start.5 = (f32[96,128]{1,0:T(8,128)S(1)}, f32[96,128]{1,0:T(8,128)S(1)}, u32[]{:S(2)}, u32[]{:S(2)}) collective-permute-start(f32[96,128]{1,0:T(8,128)S(1)} %add.22), channel_id=1, source_target_pairs={{0,16},{8,24},{16,0},{24,8},{1,17},{9,25},{17,1},{25,9},{2,18},{10... | collective-permute-start | bytes 147464 | tf_op jit(solution)/shard_map/ppermute | solution.py:524
  72.7 2.6 %shard_map.264 = bf16[1024,768]{1,0:T(8,128)(2,1)} custom-call(f32[2,128]{1,0:T(2,128)S(1)} %get-tuple-element.36.start_ref, bf16[768,2432]{1,0:T(8,128)(2,1)S(1)} %get-tuple-element.30.wcat, bf16[1024,3072]{1,0:T(8,128)(2,1)S(1)} %get-tuple-element.31.grads, f32[1024,768]{1,0:T(8,128)S(1)} %get-tuple-element.32.first, ...), custom_call_target="tpu_custom_call", output_to_operand_aliasing={{}: (4, {})} | custom-call | flops 1275068416 | bytes 524288 | tf_op jit(solution)/shard_map/pallas_call | solution.py:635
  75.4 0.0 collective-permute-done.5
  75.4 0.0 copy-start
  75.4 0.1 collective-permute-start.6
  76.8 0.1 collective-permute-done.6.refs_4_
  76.9 0.0 copy-start.1
  76.9 0.0 copy-done
  76.9 0.6 copy-done.1
  77.5 2.0 %shard_map.265 = (f32[24,128]{1,0:T(8,128)}, f32[8,24,128]{2,1,0:T(8,128)}, f32[24,128]{1,0:T(8,128)}, f32[24,128]{1,0:T(8,128)}) custom-call(s32[1]{0:T(128)S(6)} %copy.35.refs_0_, f32[1]{0:T(128)S(6)} %copy.36.refs_1_, s32[1]{0:T(128)} %bitcast.4.refs_2_, f32[288,128]{1,0:T(8,128)} %copy-done, f32[288,128]{1,0:T(8,128)} %copy-done.1, f32[8,24,128]{2,1,0:T(8,128)} %bitcast.11), custom_call_target="tpu_custom_call" | custom-call | tf_op jit(solution)/shard_map/pallas_call | solution.py:687
  (8 shorter events, 0.1 us)
Async XLA Ops:
  54.8 1.4 %collective-permute-start = (f32[144,128]{1,0:T(8,128)S(1)}, f32[144,128]{1,0:T(8,128)S(1)}, u32[]{:S(2)}, u32[]{:S(2)}) collective-permute-start(f32[144,128]{1,0:T(8,128)S(1)} %get-tuple-element.28), channel_id=1, source_target_pairs={{0,1},{1,0},{2,3},{3,2},{4,5},{5,4},{6,7},{7,6},{8,9},{9,8},{10,11... | collective-permute-start | bytes 221192 | tf_op jit(solution)/shard_map/ppermute | solution.py:524
  56.2 8.6 %collective-permute-start.1 = (f32[144,128]{1,0:T(8,128)S(1)}, f32[144,128]{1,0:T(8,128)S(1)}, u32[]{:S(2)}, u32[]{:S(2)}) collective-permute-start(f32[144,128]{1,0:T(8,128)S(1)} %add.18), channel_id=1, source_target_pairs={{0,2},{1,3},{2,0},{3,1},{4,6},{5,7},{6,4},{7,5},{8,10},{9,11},{10,... | collective-permute-start | bytes 221192 | tf_op jit(solution)/shard_map/ppermute | solution.py:524
  59.1 5.7 %collective-permute-start.2 = (f32[144,128]{1,0:T(8,128)S(1)}, f32[144,128]{1,0:T(8,128)S(1)}, u32[]{:S(2)}, u32[]{:S(2)}) collective-permute-start(f32[144,128]{1,0:T(8,128)S(1)} %add.18), channel_id=1, source_target_pairs={{0,4},{1,5},{2,6},{3,7},{4,0},{5,1},{6,2},{7,3},{8,12},{9,13},{10,... | collective-permute-start | bytes 221192 | tf_op jit(solution)/shard_map/ppermute | solution.py:524
  60.7 5.3 %collective-permute-start.3 = (f32[144,128]{1,0:T(8,128)S(1)}, f32[144,128]{1,0:T(8,128)S(1)}, u32[]{:S(2)}, u32[]{:S(2)}) collective-permute-start(f32[144,128]{1,0:T(8,128)S(1)} %add.18), channel_id=1, source_target_pairs={{0,6},{1,7},{2,4},{3,5},{4,2},{5,3},{6,0},{7,1},{8,14},{9,15},{10,... | collective-permute-start | bytes 221192 | tf_op jit(solution)/shard_map/ppermute | solution.py:524
  65.9 4.2 %collective-permute-start.4 = (f32[96,128]{1,0:T(8,128)S(1)}, f32[96,128]{1,0:T(8,128)S(1)}, u32[]{:S(2)}, u32[]{:S(2)}) collective-permute-start(f32[96,128]{1,0:T(8,128)S(1)} %fusion), channel_id=1, source_target_pairs={{0,8},{8,0},{16,24},{24,16},{1,9},{9,1},{17,25},{25,17},{2,10},{10... | collective-permute-start | bytes 147464 | tf_op jit(solution)/shard_map/ppermute | solution.py:524
  70.1 5.3 %collective-permute-start.5 = (f32[96,128]{1,0:T(8,128)S(1)}, f32[96,128]{1,0:T(8,128)S(1)}, u32[]{:S(2)}, u32[]{:S(2)}) collective-permute-start(f32[96,128]{1,0:T(8,128)S(1)} %add.22), channel_id=1, source_target_pairs={{0,16},{8,24},{16,0},{24,8},{1,17},{9,25},{17,1},{25,9},{2,18},{10... | collective-permute-start | bytes 147464 | tf_op jit(solution)/shard_map/ppermute | solution.py:524
  75.4 1.5 %copy-start = (f32[288,128]{1,0:T(8,128)}, f32[288,128]{1,0:T(8,128)S(1)}, u32[]{:S(2)}) copy-start(f32[288,128]{1,0:T(8,128)S(1)} %slice_dynamic-update-slice_fusion.1.refs_3_) | copy-start | bytes 442372
  75.4 1.4 %collective-permute-start.6 = (f32[288,128]{1,0:T(8,128)S(1)}, f32[288,128]{1,0:T(8,128)S(1)}, u32[]{:S(2)}, u32[]{:S(2)}) collective-permute-start(f32[288,128]{1,0:T(8,128)S(1)} %slice_dynamic-update-slice_fusion.1.refs_3_), channel_id=1, source_target_pairs={{0,1},{1,0},{2,3},{3,2},{4,5},{5,4},{6,7},{7,6},{8,9},{9,8},{10,11... | collective-permute-start | bytes 442376 | tf_op jit(solution)/shard_map/ppermute | solution.py:524
  76.9 0.7 copy-start.1

commit v6 on v5

--- a/solution.py
+++ b/solution.py
@@ -192,11 +192,16 @@
         (wd_hbm, wd),
     ):
         copies.append(pltpu.make_async_copy(src, dst, sems.at[len(copies)]))
-        copies[-1].start()
+
+    def depart(*which):
+        for i in which:
+            copies[i].start()
 
     def arrive(*which):
         for i in which:
             copies[i].wait()
+
+    depart(0, 1)
 
     unpack_factors(fac_ref, dcat, uq, uv)
 
@@ -235,19 +240,35 @@
             rotate_rows(src, pack * rows, rows, starts[pack], put(dst, pack * rows))
 
     arrive(0)
+    depart(2, 3)
     turn(raw_tokens, xr)
 
     lora[...] = dot(xr[...], dcat[...]).astype(bf16)
     narrow = lax.broadcasted_iota(jnp.int32, (total_rows, LANES), 1) % HEAD_DIM < RANK
-    lora_once = jnp.where(narrow, lora[...], jnp.zeros((total_rows, LANES), bf16))
-    arrive(1, 2, 3)
-    for c in range(width // BIG):
-        at = slice(c * BIG, (c + 1) * BIG)
-        query = dot(xr[...], wq[:, at]) + dot(lora_once, uq[:, at]) + line(bq[at])
+    once = att.at[:, :LANES]
+    once[...] = jnp.where(narrow, lora[...], jnp.zeros((total_rows, LANES), bf16))
+    columns = [slice(c * BIG, (c + 1) * BIG) for c in range(width // BIG)]
+    arrive(1)
+    def by_columns(body):
+        def run(c, carry):
+            body(pl.ds(pl.multiple_of(c * BIG, BIG), BIG))
+            return carry
+
+        lax.fori_loop(0, width // BIG, run, 0)
+
+    def project_query(at):
+        query = dot(xr[...], wq[:, at]) + dot(once[...], uq[:, at]) + line(bq[at])
         qs[:, at] = (query * (HEAD_DIM**-0.5 * LOG2E)).astype(bf16)
+
+    by_columns(project_query)
+    arrive(2, 3)
+    depart(4, 5, 6, 7)
+    def project_rest(at):
         ks[:, at] = dot(xr[...], wk[:, at]).astype(bf16)
-        value = dot(xr[...], wv[:, at]) + dot(lora_once, uv[:, at]) + line(bv[at])
+        value = dot(xr[...], wv[:, at]) + dot(once[...], uv[:, at]) + line(bv[at])
         vs[:, at] = value.astype(bf16)
+
+    by_columns(project_rest)
 
     def heads_of(turn_no):
         per = pairs // GROUP
@@ -437,8 +458,9 @@
 
     dl = (dot(dq[...], uq[...], 1, 1) + dot(dv[...], uv[...], 1, 1)).astype(bf16)
     gd = dot(dl, xr[...], 0, 0)
-    gq = adapter_scale * dot(lora[...], dq[...], 0, 0)[:RANK]
-    gv = adapter_scale * dot(lora[...], dv[...], 0, 0)[HEAD_DIM : HEAD_DIM + RANK]
+    lora_t = lora[...].T
+    gq = adapter_scale * dot(lora_t[: 2 * RANK], dq[...])[:RANK]
+    gv = adapter_scale * dot(lora_t[HEAD_DIM : HEAD_DIM + 2 * RANK], dv[...])[:RANK]
     pack_grads(flat, gd, gq, gv)
     half_rows = flat.shape[0] // 2
     side = side_ref[0]
@@ -675,7 +697,7 @@
             moments = [part[half_rows:] for part in [held] + got]
     for bit in bits_of("dp"):
         got = swap(total, "dp", bit)
-        if bit == bits_of("dp")[-1]:
+        if bit == 1:
             grad_tokens = token_piece(width - BIG, BIG, grad_tokens, total)
             grad_tokens, got = lax.optimization_barrier((grad_tokens, got))
         total = total + got
@@ -694,8 +716,8 @@
         step_count,
         learn_rate,
         place.reshape(1),
-        held,
-        other,
+        pltpu.with_memory_space_constraint(held, pltpu.VMEM),
+        pltpu.with_memory_space_constraint(other, pltpu.VMEM),
         factors.reshape(shaped),
     )
     return (

time: 79.7 us -> 78.6 us (0.986)
  transfers between devices with their start and end apart: 7 -> 7, of which waited for: 4 -> 4; matrix products, arithmetic and copies ran while one was open for 0% -> 0% of each run, Pallas kernels for 8% -> 9%
where the time goes in v6:
time: 78.6 us; the launch traced here: 78.4 us
  Pallas kernels  62.5 us (80%)
  starting transfers between devices  9.37 us (12%)
  waiting for transfers between devices  4.44 us (6%)
  between operations  2.04 us (3%)
    pallas_call x1, Pallas kernels, shards(): pl.pallas_call(main_kernel, out_shape=(pltpu.VMEM((half_rows + 2 * own_ro...  53.9 us
    ppermute x7, starting transfers between devices, swap(): return lax.ppermute(x, axis, [(i, i ^ bit) for i in range(n)])  9.37 us
    pallas_call x2, Pallas kernels, token_piece(): pl.pallas_call(functools.partial(token_kernel, begin), out_shape=result((...  6.74 us
    ppermute x7, waiting for transfers between devices, swap(): return lax.ppermute(x, axis, [(i, i ^ bit) for i in range(n)])  4.44 us
    pallas_call x1, Pallas kernels, shards(): pl.pallas_call(functools.partial(optimizer_kernel, places), out_shape=(ow...  1.88 us
  transfers between devices with their start and end apart: 7, of which 4 were waited for; matrix products, arithmetic and copies ran while one was open for 0% of the time, Pallas kernels for 9%

profile of v6, /device:TPU:0, one launch (start us, length us, event | category | flops | bytes accessed | tf_op | source)
XLA Modules:
  0.0 78.4 jit_solution(257966489902658709)
XLA Ops:
  0.6 53.9 %shard_map.262 = (f32[144,128]{1,0:T(8,128)S(1)}, f32[144,128]{1,0:T(8,128)S(1)}, bf16[1024,768]{1,0:T(8,128)(2,1)}, f32[2,128]{1,0:T(2,128)S(1)}, bf16[768,2432...) custom-call(s32[1]{0:T(128)} %bitcast.side_ref, s32[2,512]{1,0:T(2,128)} %seg_ref.1, ...), custom_call_target="tpu_custom_call" | custom-call | tf_op jit(solution)/shard_map/pallas_call | solution.py:606
  54.5 0.5 collective-permute-start
  55.0 0.9 %collective-permute-done = f32[144,128]{1,0:T(8,128)S(1)} collective-permute-done((f32[144,128]{1,0:T(8,128)S(1)}, f32[144,128]{1,0:T(8,128)S(1)}, u32[]{:S(2)}, u32[]{:S(2)}) %collective-permute-start) | collective-permute-done | bytes 73760 | tf_op jit(solution)/shard_map/ppermute | solution.py:546
  56.0 2.9 %collective-permute-start.1 = (f32[144,128]{1,0:T(8,128)S(1)}, f32[144,128]{1,0:T(8,128)S(1)}, u32[]{:S(2)}, u32[]{:S(2)}) collective-permute-start(f32[144,128]{1,0:T(8,128)S(1)} %add.18), channel_id=1, source_target_pairs={{0,2},{1,3},{2,0},{3,1},{4,6},{5,7},{6,4},{7,5},{8,10},{9,11},{10,... | collective-permute-start | bytes 221192 | tf_op jit(solution)/shard_map/ppermute | solution.py:546
  58.9 1.5 %collective-permute-start.2 = (f32[144,128]{1,0:T(8,128)S(1)}, f32[144,128]{1,0:T(8,128)S(1)}, u32[]{:S(2)}, u32[]{:S(2)}) collective-permute-start(f32[144,128]{1,0:T(8,128)S(1)} %add.18), channel_id=1, source_target_pairs={{0,4},{1,5},{2,6},{3,7},{4,0},{5,1},{6,2},{7,3},{8,12},{9,13},{10,... | collective-permute-start | bytes 221192 | tf_op jit(solution)/shard_map/ppermute | solution.py:546
  60.3 0.1 collective-permute-start.3
  60.4 4.1 %shard_map.263.rest_0_ = bf16[1024,768]{1,0:T(8,128)(2,1)} custom-call(f32[2,128]{1,0:T(2,128)S(1)} %get-tuple-element.36.start_ref, bf16[768,2432]{1,0:T(8,128)(2,1)S(1)} %get-tuple-element.30.wcat, bf16[1024,3072]{1,0:T(8,128)(2,1)S(1)} %get-tuple-element.31.grads, f32[1024,768]{1,0:T(8,128)S(1)} %get-tuple-element.32.first), custom_call_target="tpu_custom_call" | custom-call | flops 2550136832 | bytes 1048576 | tf_op jit(solution)/shard_map/pallas_call | solution.py:657
  64.5 0.0 collective-permute-done.1
  64.5 0.0 collective-permute-done.2
  64.5 1.1 %collective-permute-done.3 = f32[144,128]{1,0:T(8,128)S(1)} collective-permute-done((f32[144,128]{1,0:T(8,128)S(1)}, f32[144,128]{1,0:T(8,128)S(1)}, u32[]{:S(2)}, u32[]{:S(2)}) %collective-permute-start.3) | collective-permute-done | bytes 73760 | tf_op jit(solution)/shard_map/ppermute | solution.py:546
  65.6 1.7 %collective-permute-start.4 = (f32[96,128]{1,0:T(8,128)S(1)}, f32[96,128]{1,0:T(8,128)S(1)}, u32[]{:S(2)}, u32[]{:S(2)}) collective-permute-start(f32[96,128]{1,0:T(8,128)S(1)} %fusion), channel_id=1, source_target_pairs={{0,8},{8,0},{16,24},{24,16},{1,9},{9,1},{17,25},{25,17},{2,10},{10... | collective-permute-start | bytes 147464 | tf_op jit(solution)/shard_map/ppermute | solution.py:546
  67.3 2.6 %shard_map.264 = bf16[1024,768]{1,0:T(8,128)(2,1)} custom-call(f32[2,128]{1,0:T(2,128)S(1)} %get-tuple-element.36.start_ref, bf16[768,2432]{1,0:T(8,128)(2,1)S(1)} %get-tuple-element.30.wcat, bf16[1024,3072]{1,0:T(8,128)(2,1)S(1)} %get-tuple-element.31.grads, f32[1024,768]{1,0:T(8,128)S(1)} %get-tuple-element.32.first, ...), custom_call_target="tpu_custom_call", output_to_operand_aliasing={{}: (4, {})} | custom-call | flops 1275068416 | bytes 524288 | tf_op jit(solution)/shard_map/pallas_call | solution.py:657
  69.9 0.0 collective-permute-done.4
  70.0 2.6 %collective-permute-start.5 = (f32[96,128]{1,0:T(8,128)S(1)}, f32[96,128]{1,0:T(8,128)S(1)}, u32[]{:S(2)}, u32[]{:S(2)}) collective-permute-start(f32[96,128]{1,0:T(8,128)S(1)} %add.22), channel_id=1, source_target_pairs={{0,16},{8,24},{16,0},{24,8},{1,17},{9,25},{17,1},{25,9},{2,18},{10... | collective-permute-start | bytes 147464 | tf_op jit(solution)/shard_map/ppermute | solution.py:546
  72.6 2.4 %collective-permute-done.5 = f32[96,128]{1,0:T(8,128)S(1)} collective-permute-done((f32[96,128]{1,0:T(8,128)S(1)}, f32[96,128]{1,0:T(8,128)S(1)}, u32[]{:S(2)}, u32[]{:S(2)}) %collective-permute-start.5) | collective-permute-done | bytes 49184 | tf_op jit(solution)/shard_map/ppermute | solution.py:546
  75.1 0.1 collective-permute-start.6
  76.4 0.1 collective-permute-done.6.refs_4_
  76.5 1.9 %shard_map.265 = (f32[24,128]{1,0:T(8,128)}, f32[8,24,128]{2,1,0:T(8,128)}, f32[24,128]{1,0:T(8,128)}, f32[24,128]{1,0:T(8,128)}) custom-call(s32[1]{0:T(128)S(6)} %copy.35.refs_0_, f32[1]{0:T(128)S(6)} %copy.36.refs_1_, s32[1]{0:T(128)} %bitcast.4.refs_2_, f32[288,128]{1,0:T(8,128)S(1)} %slice_dynamic-update-slice_fusion.1.refs_3_, ...), custom_call_target="tpu_custom_call" | custom-call | tf_op jit(solution)/shard_map/pallas_call | solution.py:709
  (8 shorter events, 0.1 us)
Async XLA Ops:
  54.5 1.4 %collective-permute-start = (f32[144,128]{1,0:T(8,128)S(1)}, f32[144,128]{1,0:T(8,128)S(1)}, u32[]{:S(2)}, u32[]{:S(2)}) collective-permute-start(f32[144,128]{1,0:T(8,128)S(1)} %get-tuple-element.28), channel_id=1, source_target_pairs={{0,1},{1,0},{2,3},{3,2},{4,5},{5,4},{6,7},{7,6},{8,9},{9,8},{10,11... | collective-permute-start | bytes 221192 | tf_op jit(solution)/shard_map/ppermute | solution.py:546
  56.0 8.6 %collective-permute-start.1 = (f32[144,128]{1,0:T(8,128)S(1)}, f32[144,128]{1,0:T(8,128)S(1)}, u32[]{:S(2)}, u32[]{:S(2)}) collective-permute-start(f32[144,128]{1,0:T(8,128)S(1)} %add.18), channel_id=1, source_target_pairs={{0,2},{1,3},{2,0},{3,1},{4,6},{5,7},{6,4},{7,5},{8,10},{9,11},{10,... | collective-permute-start | bytes 221192 | tf_op jit(solution)/shard_map/ppermute | solution.py:546
  58.9 5.7 %collective-permute-start.2 = (f32[144,128]{1,0:T(8,128)S(1)}, f32[144,128]{1,0:T(8,128)S(1)}, u32[]{:S(2)}, u32[]{:S(2)}) collective-permute-start(f32[144,128]{1,0:T(8,128)S(1)} %add.18), channel_id=1, source_target_pairs={{0,4},{1,5},{2,6},{3,7},{4,0},{5,1},{6,2},{7,3},{8,12},{9,13},{10,... | collective-permute-start | bytes 221192 | tf_op jit(solution)/shard_map/ppermute | solution.py:546
  60.3 5.3 %collective-permute-start.3 = (f32[144,128]{1,0:T(8,128)S(1)}, f32[144,128]{1,0:T(8,128)S(1)}, u32[]{:S(2)}, u32[]{:S(2)}) collective-permute-start(f32[144,128]{1,0:T(8,128)S(1)} %add.18), channel_id=1, source_target_pairs={{0,6},{1,7},{2,4},{3,5},{4,2},{5,3},{6,0},{7,1},{8,14},{9,15},{10,... | collective-permute-start | bytes 221192 | tf_op jit(solution)/shard_map/ppermute | solution.py:546
  65.6 4.3 %collective-permute-start.4 = (f32[96,128]{1,0:T(8,128)S(1)}, f32[96,128]{1,0:T(8,128)S(1)}, u32[]{:S(2)}, u32[]{:S(2)}) collective-permute-start(f32[96,128]{1,0:T(8,128)S(1)} %fusion), channel_id=1, source_target_pairs={{0,8},{8,0},{16,24},{24,16},{1,9},{9,1},{17,25},{25,17},{2,10},{10... | collective-permute-start | bytes 147464 | tf_op jit(solution)/shard_map/ppermute | solution.py:546
  70.0 5.1 %collective-permute-start.5 = (f32[96,128]{1,0:T(8,128)S(1)}, f32[96,128]{1,0:T(8,128)S(1)}, u32[]{:S(2)}, u32[]{:S(2)}) collective-permute-start(f32[96,128]{1,0:T(8,128)S(1)} %add.22), channel_id=1, source_target_pairs={{0,16},{8,24},{16,0},{24,8},{1,17},{9,25},{17,1},{25,9},{2,18},{10... | collective-permute-start | bytes 147464 | tf_op jit(solution)/shard_map/ppermute | solution.py:546
  75.1 1.4 %collective-permute-start.6 = (f32[288,128]{1,0:T(8,128)S(1)}, f32[288,128]{1,0:T(8,128)S(1)}, u32[]{:S(2)}, u32[]{:S(2)}) collective-permute-start(f32[288,128]{1,0:T(8,128)S(1)} %slice_dynamic-update-slice_fusion.1.refs_3_), channel_id=1, source_target_pairs={{0,1},{1,0},{2,3},{3,2},{4,5},{5,4},{6,7},{7,6},{8,9},{9,8},{10,11... | collective-permute-start | bytes 442376 | tf_op jit(solution)/shard_map/ppermute | solution.py:546

commit v7 on v6

--- a/solution.py
+++ b/solution.py
@@ -718,7 +718,7 @@
         place.reshape(1),
         pltpu.with_memory_space_constraint(held, pltpu.VMEM),
         pltpu.with_memory_space_constraint(other, pltpu.VMEM),
-        factors.reshape(shaped),
+        pltpu.with_memory_space_constraint(factors.reshape(shaped), pltpu.VMEM),
     )
     return (
         output,

time: 78.6 us -> 77.7 us (0.989)
  Pallas kernels: 62.5 us -> 61.5 us
    pallas_call x1, Pallas kernels: 1.88 us -> 0.94 us  [shards(): pl.pallas_call(functools.partial(optimizer_kernel, places), out_shape=(ow...]
where the time goes in v7:
time: 77.7 us; the launch traced here: 77.4 us
  Pallas kernels  61.5 us (79%)
  starting transfers between devices  9.34 us (12%)
  waiting for transfers between devices  4.46 us (6%)
  between operations  2.05 us (3%)
    pallas_call x1, Pallas kernels, shards(): pl.pallas_call(main_kernel, out_shape=(pltpu.VMEM((half_rows + 2 * own_ro...  53.8 us
    ppermute x7, starting transfers between devices, swap(): return lax.ppermute(x, axis, [(i, i ^ bit) for i in range(n)])  9.34 us
    pallas_call x2, Pallas kernels, token_piece(): pl.pallas_call(functools.partial(token_kernel, begin), out_shape=result((...  6.76 us
    ppermute x7, waiting for transfers between devices, swap(): return lax.ppermute(x, axis, [(i, i ^ bit) for i in range(n)])  4.46 us
  transfers between devices with their start and end apart: 7, of which 4 were waited for; matrix products, arithmetic and copies ran while one was open for 0% of the time, Pallas kernels for 9%

profile of v7, /device:TPU:0, one launch (start us, length us, event | category | flops | bytes accessed | tf_op | source)
XLA Modules:
  0.0 77.4 jit_solution(3638080744307570368)
XLA Ops:
  0.6 53.8 %shard_map.262 = (f32[144,128]{1,0:T(8,128)S(1)}, f32[144,128]{1,0:T(8,128)S(1)}, bf16[1024,768]{1,0:T(8,128)(2,1)}, f32[2,128]{1,0:T(2,128)S(1)}, bf16[768,2432...) custom-call(s32[1]{0:T(128)} %bitcast.side_ref, s32[2,512]{1,0:T(2,128)} %seg_ref.1, ...), custom_call_target="tpu_custom_call" | custom-call | tf_op jit(solution)/shard_map/pallas_call | solution.py:606
  54.5 0.5 collective-permute-start
  55.0 0.9 %collective-permute-done = f32[144,128]{1,0:T(8,128)S(1)} collective-permute-done((f32[144,128]{1,0:T(8,128)S(1)}, f32[144,128]{1,0:T(8,128)S(1)}, u32[]{:S(2)}, u32[]{:S(2)}) %collective-permute-start) | collective-permute-done | bytes 73760 | tf_op jit(solution)/shard_map/ppermute | solution.py:546
  56.0 2.9 %collective-permute-start.1 = (f32[144,128]{1,0:T(8,128)S(1)}, f32[144,128]{1,0:T(8,128)S(1)}, u32[]{:S(2)}, u32[]{:S(2)}) collective-permute-start(f32[144,128]{1,0:T(8,128)S(1)} %add.18), channel_id=1, source_target_pairs={{0,2},{1,3},{2,0},{3,1},{4,6},{5,7},{6,4},{7,5},{8,10},{9,11},{10,... | collective-permute-start | bytes 221192 | tf_op jit(solution)/shard_map/ppermute | solution.py:546
  58.8 1.5 %collective-permute-start.2 = (f32[144,128]{1,0:T(8,128)S(1)}, f32[144,128]{1,0:T(8,128)S(1)}, u32[]{:S(2)}, u32[]{:S(2)}) collective-permute-start(f32[144,128]{1,0:T(8,128)S(1)} %add.18), channel_id=1, source_target_pairs={{0,4},{1,5},{2,6},{3,7},{4,0},{5,1},{6,2},{7,3},{8,12},{9,13},{10,... | collective-permute-start | bytes 221192 | tf_op jit(solution)/shard_map/ppermute | solution.py:546
  60.4 0.0 collective-permute-start.3
  60.4 4.1 %shard_map.263.rest_0_ = bf16[1024,768]{1,0:T(8,128)(2,1)} custom-call(f32[2,128]{1,0:T(2,128)S(1)} %get-tuple-element.36.start_ref, bf16[768,2432]{1,0:T(8,128)(2,1)S(1)} %get-tuple-element.30.wcat, bf16[1024,3072]{1,0:T(8,128)(2,1)S(1)} %get-tuple-element.31.grads, f32[1024,768]{1,0:T(8,128)S(1)} %get-tuple-element.32.first), custom_call_target="tpu_custom_call" | custom-call | flops 2550136832 | bytes 1048576 | tf_op jit(solution)/shard_map/pallas_call | solution.py:657
  64.5 0.0 collective-permute-done.1
  64.5 0.0 collective-permute-done.2
  64.5 1.1 %collective-permute-done.3 = f32[144,128]{1,0:T(8,128)S(1)} collective-permute-done((f32[144,128]{1,0:T(8,128)S(1)}, f32[144,128]{1,0:T(8,128)S(1)}, u32[]{:S(2)}, u32[]{:S(2)}) %collective-permute-start.3) | collective-permute-done | bytes 73760 | tf_op jit(solution)/shard_map/ppermute | solution.py:546
  65.6 0.0 copy-start
  65.7 1.6 %collective-permute-start.4 = (f32[96,128]{1,0:T(8,128)S(1)}, f32[96,128]{1,0:T(8,128)S(1)}, u32[]{:S(2)}, u32[]{:S(2)}) collective-permute-start(f32[96,128]{1,0:T(8,128)S(1)} %fusion), channel_id=1, source_target_pairs={{0,8},{8,0},{16,24},{24,16},{1,9},{9,1},{17,25},{25,17},{2,10},{10... | collective-permute-start | bytes 147464 | tf_op jit(solution)/shard_map/ppermute | solution.py:546
  67.3 2.6 %shard_map.264 = bf16[1024,768]{1,0:T(8,128)(2,1)} custom-call(f32[2,128]{1,0:T(2,128)S(1)} %get-tuple-element.36.start_ref, bf16[768,2432]{1,0:T(8,128)(2,1)S(1)} %get-tuple-element.30.wcat, bf16[1024,3072]{1,0:T(8,128)(2,1)S(1)} %get-tuple-element.31.grads, f32[1024,768]{1,0:T(8,128)S(1)} %get-tuple-element.32.first, ...), custom_call_target="tpu_custom_call", output_to_operand_aliasing={{}: (4, {})} | custom-call | flops 1275068416 | bytes 524288 | tf_op jit(solution)/shard_map/pallas_call | solution.py:657
  69.9 0.0 collective-permute-done.4
  70.0 2.7 %collective-permute-start.5 = (f32[96,128]{1,0:T(8,128)S(1)}, f32[96,128]{1,0:T(8,128)S(1)}, u32[]{:S(2)}, u32[]{:S(2)}) collective-permute-start(f32[96,128]{1,0:T(8,128)S(1)} %add.22), channel_id=1, source_target_pairs={{0,16},{8,24},{16,0},{24,8},{1,17},{9,25},{17,1},{25,9},{2,18},{10... | collective-permute-start | bytes 147464 | tf_op jit(solution)/shard_map/ppermute | solution.py:546
  72.6 2.4 %collective-permute-done.5 = f32[96,128]{1,0:T(8,128)S(1)} collective-permute-done((f32[96,128]{1,0:T(8,128)S(1)}, f32[96,128]{1,0:T(8,128)S(1)}, u32[]{:S(2)}, u32[]{:S(2)}) %collective-permute-start.5) | collective-permute-done | bytes 49184 | tf_op jit(solution)/shard_map/ppermute | solution.py:546
  75.1 0.1 collective-permute-start.6
  76.4 0.1 collective-permute-done.6.refs_4_
  76.5 0.0 copy-done
  76.5 0.9 %shard_map.265 = (f32[24,128]{1,0:T(8,128)}, f32[8,24,128]{2,1,0:T(8,128)}, f32[24,128]{1,0:T(8,128)}, f32[24,128]{1,0:T(8,128)}) custom-call(s32[1]{0:T(128)S(6)} %copy.35.refs_0_, f32[1]{0:T(128)S(6)} %copy.36.refs_1_, s32[1]{0:T(128)} %bitcast.4.refs_2_, f32[288,128]{1,0:T(8,128)S(1)} %slice_dynamic-update-slice_fusion.1.refs_3_, ...), custom_call_target="tpu_custom_call" | custom-call | tf_op jit(solution)/shard_map/pallas_call | solution.py:709
  (8 shorter events, 0.1 us)
Async XLA Ops:
  54.5 1.5 %collective-permute-start = (f32[144,128]{1,0:T(8,128)S(1)}, f32[144,128]{1,0:T(8,128)S(1)}, u32[]{:S(2)}, u32[]{:S(2)}) collective-permute-start(f32[144,128]{1,0:T(8,128)S(1)} %get-tuple-element.28), channel_id=1, source_target_pairs={{0,1},{1,0},{2,3},{3,2},{4,5},{5,4},{6,7},{7,6},{8,9},{9,8},{10,11... | collective-permute-start | bytes 221192 | tf_op jit(solution)/shard_map/ppermute | solution.py:546
  56.0 8.5 %collective-permute-start.1 = (f32[144,128]{1,0:T(8,128)S(1)}, f32[144,128]{1,0:T(8,128)S(1)}, u32[]{:S(2)}, u32[]{:S(2)}) collective-permute-start(f32[144,128]{1,0:T(8,128)S(1)} %add.18), channel_id=1, source_target_pairs={{0,2},{1,3},{2,0},{3,1},{4,6},{5,7},{6,4},{7,5},{8,10},{9,11},{10,... | collective-permute-start | bytes 221192 | tf_op jit(solution)/shard_map/ppermute | solution.py:546
  58.8 5.7 %collective-permute-start.2 = (f32[144,128]{1,0:T(8,128)S(1)}, f32[144,128]{1,0:T(8,128)S(1)}, u32[]{:S(2)}, u32[]{:S(2)}) collective-permute-start(f32[144,128]{1,0:T(8,128)S(1)} %add.18), channel_id=1, source_target_pairs={{0,4},{1,5},{2,6},{3,7},{4,0},{5,1},{6,2},{7,3},{8,12},{9,13},{10,... | collective-permute-start | bytes 221192 | tf_op jit(solution)/shard_map/ppermute | solution.py:546
  60.4 5.3 %collective-permute-start.3 = (f32[144,128]{1,0:T(8,128)S(1)}, f32[144,128]{1,0:T(8,128)S(1)}, u32[]{:S(2)}, u32[]{:S(2)}) collective-permute-start(f32[144,128]{1,0:T(8,128)S(1)} %add.18), channel_id=1, source_target_pairs={{0,6},{1,7},{2,4},{3,5},{4,2},{5,3},{6,0},{7,1},{8,14},{9,15},{10,... | collective-permute-start | bytes 221192 | tf_op jit(solution)/shard_map/ppermute | solution.py:546
  65.6 10.9 %copy-start = (f32[24576]{0:T(1024)S(1)}, f32[24576]{0:T(1024)}, u32[]{:S(2)}) copy-start(f32[24576]{0:T(1024)} %param.41) | copy-start | bytes 294916
  65.7 4.3 %collective-permute-start.4 = (f32[96,128]{1,0:T(8,128)S(1)}, f32[96,128]{1,0:T(8,128)S(1)}, u32[]{:S(2)}, u32[]{:S(2)}) collective-permute-start(f32[96,128]{1,0:T(8,128)S(1)} %fusion), channel_id=1, source_target_pairs={{0,8},{8,0},{16,24},{24,16},{1,9},{9,1},{17,25},{25,17},{2,10},{10... | collective-permute-start | bytes 147464 | tf_op jit(solution)/shard_map/ppermute | solution.py:546
  70.0 5.1 %collective-permute-start.5 = (f32[96,128]{1,0:T(8,128)S(1)}, f32[96,128]{1,0:T(8,128)S(1)}, u32[]{:S(2)}, u32[]{:S(2)}) collective-permute-start(f32[96,128]{1,0:T(8,128)S(1)} %add.22), channel_id=1, source_target_pairs={{0,16},{8,24},{16,0},{24,8},{1,17},{9,25},{17,1},{25,9},{2,18},{10... | collective-permute-start | bytes 147464 | tf_op jit(solution)/shard_map/ppermute | solution.py:546
  75.1 1.4 %collective-permute-start.6 = (f32[288,128]{1,0:T(8,128)S(1)}, f32[288,128]{1,0:T(8,128)S(1)}, u32[]{:S(2)}, u32[]{:S(2)}) collective-permute-start(f32[288,128]{1,0:T(8,128)S(1)} %slice_dynamic-update-slice_fusion.1.refs_3_), channel_id=1, source_target_pairs={{0,1},{1,0},{2,3},{3,2},{4,5},{5,4},{6,7},{7,6},{8,9},{9,8},{10,11... | collective-permute-start | bytes 442376 | tf_op jit(solution)/shard_map/ppermute | solution.py:546

commit v8 on v7

--- a/solution.py
+++ b/solution.py
@@ -504,8 +504,8 @@
 
 
 def optimizer_kernel(places, *refs):
-    steps_ref, rate_ref, place_ref, held, other, params = refs[:6]
-    grad_out, new_params, first_out, second_out, total = refs[6:]
+    steps_ref, rate_ref, place_ref, held, other, mine, theirs, params = refs[:8]
+    grad_out, new_params, first_out, second_out, total = refs[8:]
     shares, own_rows = params.shape[:2]
     half = shares // 2
     place = place_ref[0]
@@ -525,7 +525,7 @@
     fix_two = jnp.full(shape, 1.0 - power(beta_two), f32)
     grad_out[...] = total[place // half, place % half]
     for j, mask in enumerate(places + [mask ^ 1 for mask in places]):
-        source, at = (held, half + 2 * j) if j < half else (other, half + 2 * (j - half))
+        source, at = (mine, 2 * j) if j < half else (theirs, 2 * (j - half))
         moment = source[at * own_rows : (at + 1) * own_rows, :]
         square = source[(at + 1) * own_rows : (at + 2) * own_rows, :]
         share = place ^ mask
@@ -695,30 +695,34 @@
             held = jnp.concatenate([total] + [part[half_rows:] for part in [held] + got])
         else:
             moments = [part[half_rows:] for part in [held] + got]
+    mine = jnp.concatenate(moments)
+    theirs = swap(mine, "wide", 1)
     for bit in bits_of("dp"):
         got = swap(total, "dp", bit)
         if bit == 1:
             grad_tokens = token_piece(width - BIG, BIG, grad_tokens, total)
             grad_tokens, got = lax.optimization_barrier((grad_tokens, got))
         total = total + got
-    held = jnp.concatenate([total] + moments)
-    other = swap(held, "wide", 1)
+    other = swap(total, "wide", 1)
+    placed = functools.partial(pltpu.with_memory_space_constraint, memory_space=pltpu.VMEM)
 
     own = result((own_rows, LANES), f32)
     shaped = (shares, own_rows, LANES)
     grad_own, new_factors, new_first, new_second = pl.pallas_call(
         functools.partial(optimizer_kernel, places),
         out_shape=(own, result(shaped, f32), own, own),
-        in_specs=[scalars] * 3 + [whole] * 3,
+        in_specs=[scalars] * 3 + [whole] * 5,
         out_specs=[whole] * 4,
         scratch_shapes=[pltpu.VMEM((2, shares // 2, own_rows, LANES), f32)],
     )(
         step_count,
         learn_rate,
         place.reshape(1),
-        pltpu.with_memory_space_constraint(held, pltpu.VMEM),
-        pltpu.with_memory_space_constraint(other, pltpu.VMEM),
-        pltpu.with_memory_space_constraint(factors.reshape(shaped), pltpu.VMEM),
+        placed(total),
+        placed(other),
+        placed(mine),
+        placed(theirs),
+        placed(factors.reshape(shaped)),
     )
     return (
         output,

time: 77.7 us -> 77.7 us (level)
    ppermute x7 -> x8, waiting for transfers between devices: 4.46 us -> 4.4 us  [swap(): return lax.ppermute(x, axis, [(i, i ^ bit) for i in range(n)])]
    ppermute x7 -> x8, starting transfers between devices: 9.34 us -> 9.36 us  [swap(): return lax.ppermute(x, axis, [(i, i ^ bit) for i in range(n)])]
  transfers between devices with their start and end apart: 7 -> 8, of which waited for: 4 -> 3; matrix products, arithmetic and copies ran while one was open for 0% -> 0% of each run, Pallas kernels for 9% -> 9%
where the time goes in v8:
time: 77.7 us; the launch traced here: 77.4 us
  Pallas kernels  61.5 us (79%)
  starting transfers between devices  9.36 us (12%)
  waiting for transfers between devices  4.4 us (6%)
  between operations  2.07 us (3%)
    pallas_call x1, Pallas kernels, shards(): pl.pallas_call(main_kernel, out_shape=(pltpu.VMEM((half_rows + 2 * own_ro...  53.8 us
    ppermute x8, starting transfers between devices, swap(): return lax.ppermute(x, axis, [(i, i ^ bit) for i in range(n)])  9.36 us
    pallas_call x2, Pallas kernels, token_piece(): pl.pallas_call(functools.partial(token_kernel, begin), out_shape=result((...  6.74 us
    ppermute x8, waiting for transfers between devices, swap(): return lax.ppermute(x, axis, [(i, i ^ bit) for i in range(n)])  4.4 us
  transfers between devices with their start and end apart: 8, of which 3 were waited for; matrix products, arithmetic and copies ran while one was open for 0% of the time, Pallas kernels for 9%

profile of v8, /device:TPU:0, one launch (start us, length us, event | category | flops | bytes accessed | tf_op | source)
XLA Modules:
  0.0 77.4 jit_solution(18395456749260622596)
XLA Ops:
  0.6 53.8 %shard_map.262 = (f32[144,128]{1,0:T(8,128)S(1)}, f32[144,128]{1,0:T(8,128)S(1)}, bf16[1024,768]{1,0:T(8,128)(2,1)}, f32[2,128]{1,0:T(2,128)S(1)}, bf16[768,2432...) custom-call(s32[1]{0:T(128)} %bitcast.side_ref, s32[2,512]{1,0:T(2,128)} %seg_ref.1, ...), custom_call_target="tpu_custom_call" | custom-call | tf_op jit(solution)/shard_map/pallas_call | solution.py:606
  54.5 0.5 collective-permute-start
  55.0 0.9 %collective-permute-done = f32[144,128]{1,0:T(8,128)S(1)} collective-permute-done((f32[144,128]{1,0:T(8,128)S(1)}, f32[144,128]{1,0:T(8,128)S(1)}, u32[]{:S(2)}, u32[]{:S(2)}) %collective-permute-start) | collective-permute-done | bytes 73760 | tf_op jit(solution)/shard_map/ppermute | solution.py:546
  56.0 2.9 %collective-permute-start.1 = (f32[144,128]{1,0:T(8,128)S(1)}, f32[144,128]{1,0:T(8,128)S(1)}, u32[]{:S(2)}, u32[]{:S(2)}) collective-permute-start(f32[144,128]{1,0:T(8,128)S(1)} %add.18), channel_id=1, source_target_pairs={{0,2},{1,3},{2,0},{3,1},{4,6},{5,7},{6,4},{7,5},{8,10},{9,11},{10,... | collective-permute-start | bytes 221192 | tf_op jit(solution)/shard_map/ppermute | solution.py:546
  58.9 1.5 %collective-permute-start.2 = (f32[144,128]{1,0:T(8,128)S(1)}, f32[144,128]{1,0:T(8,128)S(1)}, u32[]{:S(2)}, u32[]{:S(2)}) collective-permute-start(f32[144,128]{1,0:T(8,128)S(1)} %add.18), channel_id=1, source_target_pairs={{0,4},{1,5},{2,6},{3,7},{4,0},{5,1},{6,2},{7,3},{8,12},{9,13},{10,... | collective-permute-start | bytes 221192 | tf_op jit(solution)/shard_map/ppermute | solution.py:546
  60.4 0.0 collective-permute-start.3
  60.4 4.1 %shard_map.263.rest_0_ = bf16[1024,768]{1,0:T(8,128)(2,1)} custom-call(f32[2,128]{1,0:T(2,128)S(1)} %get-tuple-element.36.start_ref, bf16[768,2432]{1,0:T(8,128)(2,1)S(1)} %get-tuple-element.30.wcat, bf16[1024,3072]{1,0:T(8,128)(2,1)S(1)} %get-tuple-element.31.grads, f32[1024,768]{1,0:T(8,128)S(1)} %get-tuple-element.32.first), custom_call_target="tpu_custom_call" | custom-call | flops 2550136832 | bytes 1048576 | tf_op jit(solution)/shard_map/pallas_call | solution.py:657
  64.5 0.0 collective-permute-done.1
  64.5 0.0 collective-permute-done.2
  64.6 1.1 %collective-permute-done.3 = f32[144,128]{1,0:T(8,128)S(1)} collective-permute-done((f32[144,128]{1,0:T(8,128)S(1)}, f32[144,128]{1,0:T(8,128)S(1)}, u32[]{:S(2)}, u32[]{:S(2)}) %collective-permute-start.3) | collective-permute-done | bytes 73760 | tf_op jit(solution)/shard_map/ppermute | solution.py:546
  65.7 0.0 copy-start
  65.7 1.7 %collective-permute-start.4 = (f32[96,128]{1,0:T(8,128)S(1)}, f32[96,128]{1,0:T(8,128)S(1)}, u32[]{:S(2)}, u32[]{:S(2)}) collective-permute-start(f32[96,128]{1,0:T(8,128)S(1)} %fusion), channel_id=1, source_target_pairs={{0,8},{8,0},{16,24},{24,16},{1,9},{9,1},{17,25},{25,17},{2,10},{10... | collective-permute-start | bytes 147464 | tf_op jit(solution)/shard_map/ppermute | solution.py:546
  67.3 2.6 %shard_map.264 = bf16[1024,768]{1,0:T(8,128)(2,1)} custom-call(f32[2,128]{1,0:T(2,128)S(1)} %get-tuple-element.36.start_ref, bf16[768,2432]{1,0:T(8,128)(2,1)S(1)} %get-tuple-element.30.wcat, bf16[1024,3072]{1,0:T(8,128)(2,1)S(1)} %get-tuple-element.31.grads, f32[1024,768]{1,0:T(8,128)S(1)} %get-tuple-element.32.first, ...), custom_call_target="tpu_custom_call", output_to_operand_aliasing={{}: (4, {})} | custom-call | flops 1275068416 | bytes 524288 | tf_op jit(solution)/shard_map/pallas_call | solution.py:657
  70.0 0.0 collective-permute-done.4
  70.0 2.6 %collective-permute-start.5 = (f32[96,128]{1,0:T(8,128)S(1)}, f32[96,128]{1,0:T(8,128)S(1)}, u32[]{:S(2)}, u32[]{:S(2)}) collective-permute-start(f32[96,128]{1,0:T(8,128)S(1)} %add.22), channel_id=1, source_target_pairs={{0,16},{8,24},{16,0},{24,8},{1,17},{9,25},{17,1},{25,9},{2,18},{10... | collective-permute-start | bytes 147464 | tf_op jit(solution)/shard_map/ppermute | solution.py:546
  72.7 0.0 collective-permute-start.7
  72.7 2.4 %collective-permute-done.5 = f32[96,128]{1,0:T(8,128)S(1)} collective-permute-done((f32[96,128]{1,0:T(8,128)S(1)}, f32[96,128]{1,0:T(8,128)S(1)}, u32[]{:S(2)}, u32[]{:S(2)}) %collective-permute-start.5) | collective-permute-done | bytes 49184 | tf_op jit(solution)/shard_map/ppermute | solution.py:546
  75.1 0.1 collective-permute-start.6
  76.4 0.0 collective-permute-done.7.refs_6_
  76.4 0.0 collective-permute-done.6.refs_4_
  76.5 0.0 copy-done
  76.5 1.0 %shard_map.265 = (f32[24,128]{1,0:T(8,128)}, f32[8,24,128]{2,1,0:T(8,128)}, f32[24,128]{1,0:T(8,128)}, f32[24,128]{1,0:T(8,128)}) custom-call(s32[1]{0:T(128)S(6)} %copy.31.refs_0_, f32[1]{0:T(128)S(6)} %copy.32.refs_1_, s32[1]{0:T(128)} %bitcast.4.refs_2_, f32[96,128]{1,0:T(8,128)S(1)} %add.23.refs_3_, f32[96,128]{1,0:T(8,128)S(1)} %collective-permute-done.6.refs_4_, ...), custom_call_target="tpu_custom_call" | custom-call | tf_op jit(solution)/shard_map/pallas_call | solution.py:711
  (9 shorter events, 0.1 us)
Async XLA Ops:
  54.5 1.5 %collective-permute-start = (f32[144,128]{1,0:T(8,128)S(1)}, f32[144,128]{1,0:T(8,128)S(1)}, u32[]{:S(2)}, u32[]{:S(2)}) collective-permute-start(f32[144,128]{1,0:T(8,128)S(1)} %get-tuple-element.28), channel_id=1, source_target_pairs={{0,1},{1,0},{2,3},{3,2},{4,5},{5,4},{6,7},{7,6},{8,9},{9,8},{10,11... | collective-permute-start | bytes 221192 | tf_op jit(solution)/shard_map/ppermute | solution.py:546
  56.0 8.6 %collective-permute-start.1 = (f32[144,128]{1,0:T(8,128)S(1)}, f32[144,128]{1,0:T(8,128)S(1)}, u32[]{:S(2)}, u32[]{:S(2)}) collective-permute-start(f32[144,128]{1,0:T(8,128)S(1)} %add.18), channel_id=1, source_target_pairs={{0,2},{1,3},{2,0},{3,1},{4,6},{5,7},{6,4},{7,5},{8,10},{9,11},{10,... | collective-permute-start | bytes 221192 | tf_op jit(solution)/shard_map/ppermute | solution.py:546
  58.9 5.7 %collective-permute-start.2 = (f32[144,128]{1,0:T(8,128)S(1)}, f32[144,128]{1,0:T(8,128)S(1)}, u32[]{:S(2)}, u32[]{:S(2)}) collective-permute-start(f32[144,128]{1,0:T(8,128)S(1)} %add.18), channel_id=1, source_target_pairs={{0,4},{1,5},{2,6},{3,7},{4,0},{5,1},{6,2},{7,3},{8,12},{9,13},{10,... | collective-permute-start | bytes 221192 | tf_op jit(solution)/shard_map/ppermute | solution.py:546
  60.4 5.3 %collective-permute-start.3 = (f32[144,128]{1,0:T(8,128)S(1)}, f32[144,128]{1,0:T(8,128)S(1)}, u32[]{:S(2)}, u32[]{:S(2)}) collective-permute-start(f32[144,128]{1,0:T(8,128)S(1)} %add.18), channel_id=1, source_target_pairs={{0,6},{1,7},{2,4},{3,5},{4,2},{5,3},{6,0},{7,1},{8,14},{9,15},{10,... | collective-permute-start | bytes 221192 | tf_op jit(solution)/shard_map/ppermute | solution.py:546
  65.7 10.8 %copy-start = (f32[24576]{0:T(1024)S(1)}, f32[24576]{0:T(1024)}, u32[]{:S(2)}) copy-start(f32[24576]{0:T(1024)} %param.41) | copy-start | bytes 294916
  65.7 4.3 %collective-permute-start.4 = (f32[96,128]{1,0:T(8,128)S(1)}, f32[96,128]{1,0:T(8,128)S(1)}, u32[]{:S(2)}, u32[]{:S(2)}) collective-permute-start(f32[96,128]{1,0:T(8,128)S(1)} %fusion), channel_id=1, source_target_pairs={{0,8},{8,0},{16,24},{24,16},{1,9},{9,1},{17,25},{25,17},{2,10},{10... | collective-permute-start | bytes 147464 | tf_op jit(solution)/shard_map/ppermute | solution.py:546
  70.0 5.1 %collective-permute-start.5 = (f32[96,128]{1,0:T(8,128)S(1)}, f32[96,128]{1,0:T(8,128)S(1)}, u32[]{:S(2)}, u32[]{:S(2)}) collective-permute-start(f32[96,128]{1,0:T(8,128)S(1)} %add.22), channel_id=1, source_target_pairs={{0,16},{8,24},{16,0},{24,8},{1,17},{9,25},{17,1},{25,9},{2,18},{10... | collective-permute-start | bytes 147464 | tf_op jit(solution)/shard_map/ppermute | solution.py:546
  72.7 3.8 %collective-permute-start.7 = (f32[192,128]{1,0:T(8,128)S(1)}, f32[192,128]{1,0:T(8,128)S(1)}, u32[]{:S(2)}, u32[]{:S(2)}) collective-permute-start(f32[192,128]{1,0:T(8,128)S(1)} %pad_maximum_fusion.refs_5_), channel_id=1, source_target_pairs={{0,1},{1,0},{2,3},{3,2},{4,5},{5,4},{6,7},{7,6},{8,9},{9,8},{10,11... | collective-permute-start | bytes 294920 | tf_op jit(solution)/shard_map/ppermute | solution.py:546
  75.1 1.4 %collective-permute-start.6 = (f32[96,128]{1,0:T(8,128)S(1)}, f32[96,128]{1,0:T(8,128)S(1)}, u32[]{:S(2)}, u32[]{:S(2)}) collective-permute-start(f32[96,128]{1,0:T(8,128)S(1)} %add.23.refs_3_), channel_id=1, source_target_pairs={{0,1},{1,0},{2,3},{3,2},{4,5},{5,4},{6,7},{7,6},{8,9},{9,8},{10,11... | collective-permute-start | bytes 147464 | tf_op jit(solution)/shard_map/ppermute | solution.py:546
